TPU v7x, 256 devices: a whole 4x4x8 slice. The times are simulated.
256 devices in a mesh: dp: 4 (over x), expert: 64 (over y, z, core).
Axes of the slice: x: 4, y: 4, z: 8, core: 2. Of those that a mesh axis runs over, the one named last changes fastest.
Arguments:
- tokens: bfloat16 [32768, 2048], P(('dp', 'expert')), may hold values from -6 to 6
- cotangent: bfloat16 [32768, 2048], P(('dp', 'expert')), may hold values from -6 to 6
- gate_probs: bfloat16 [32768, 2], P(('dp', 'expert')), may hold values from 0.099609375 to 0.8984375
- expert_ids: int32 [32768, 2], P(('dp', 'expert')), may hold values from 0 to 127, all different within a row; in each aligned block of 128 rows (0 to 127, 128 to 255, ...) at most 3 rows name the same one
- gate_weight: bfloat16 [64, 2048, 768], P('expert'), may hold values from -0.125 to 0.125
- up_weight: bfloat16 [64, 2048, 768], P('expert'), may hold values from -0.125 to 0.125
- down_weight: bfloat16 [64, 768, 2048], P('expert'), may hold values from -0.21875 to 0.21875
Outputs:
- grad_tokens: bfloat16 [32768, 2048], P(('dp', 'expert'))
- grad_probs: bfloat16 [32768, 2], P(('dp', 'expert'))
- grad_gate: bfloat16 [64, 2048, 768], P('expert', 'dp')
- grad_up: bfloat16 [64, 2048, 768], P('expert', 'dp')
- grad_down: bfloat16 [64, 768, 2048], P('expert', None, 'dp')
Inputs may be any that keep to these rules, and one draw needn't show every extreme that they name: `expert_ids`: each row names 2 different slots; among the 128 tokens of one device no slot is named more than 3 times, a bound that some block reaches.
All inputs are finite; a program needn't handle non-finite values.
Results may differ from a plain program's by a relative error of at most 0.009.
Values may be sent and summed in bfloat16 or wider, within the bound.
No kernel may reach another device: no remote copies, remote signals or barrier semaphores. Data moves between devices by JAX's collectives and lax.ppermute only.
A program may use at most 128 MiB of HBM per device.

v0:
```python
import jax
import jax.numpy as jnp
import numpy as np
from jax import lax
from jax.experimental import pallas as pl
from jax.experimental.pallas import tpu as pltpu
from jax.sharding import PartitionSpec as P

F32 = jnp.float32
BF16 = jnp.bfloat16
N = 64
CAP = 3
PER = 2 * CAP
ROWS = N * PER
D = 2048
FF = 768
TOK = 128
DP = 4
SEG = 512
NSEG = D // SEG
SPAN = NSEG * PER
BSEG = 256
NBSEG = D // BSEG
BSPAN = NBSEG * PER + 8
GROUP = 8
GROWS = GROUP * PER
NGROUP = N // GROUP
FB = 256
NFB = FF // FB


def permutations():
    unmix = np.zeros((NSEG * GROWS, GROUP * SPAN), np.float32)
    back = np.zeros((NBSEG * GROWS + 16, GROUP * BSPAN), np.float32)
    mark = np.zeros((GROWS, BSEG), np.float32)
    spread = np.zeros((GROUP * BSPAN, GROWS), np.float32)
    for d in range(GROUP):
        for j in range(PER):
            row = d * PER + j
            mark[row, j] = 1
            spread[d * BSPAN + NBSEG * PER, row] = 1
            for s in range(NSEG):
                unmix[s * GROWS + row, d * SPAN + s * PER + j] = 1
            for s in range(NBSEG):
                back[s * GROWS + row, d * BSPAN + s * PER + j] = 1
        back[NBSEG * GROWS + d, d * BSPAN + NBSEG * PER] = 1
    mix = np.concatenate([back[: NBSEG * GROWS].T, spread], axis=1)
    return unmix, back, mix, mark


UNMIX, BACK, MIX, MARK = permutations()


def mm(a, b):
    return jnp.dot(a, b, preferred_element_type=F32)


def mm_t(a, b):
    return lax.dot_general(a, b, (((1,), (1,)), ((), ())), preferred_element_type=F32)


def iota(shape, dim):
    return lax.broadcasted_iota(jnp.int32, shape, dim)


def split_slot(ids):
    is_copy = (ids >= N).astype(jnp.int32)
    base = ids - N * is_copy
    target = jnp.where(ids >= N, jnp.bitwise_xor(base, N // 2), base)
    return target, is_copy * CAP


def places_in_lanes(ids_ref):
    ids = [ids_ref[k : k + 1, :] for k in range(2)]
    hot = [(iota((2 * N, TOK), 0) == v).astype(F32) for v in ids]
    before = (iota((TOK, TOK), 0) < iota((TOK, TOK), 1)).astype(F32).astype(BF16)
    count = mm((hot[0] + hot[1]).astype(BF16), before)
    out = []
    for k in range(2):
        rank = jnp.sum(count * hot[k], axis=0, keepdims=True).astype(jnp.int32)
        target, first = split_slot(ids[k])
        out.append((target, first + rank))
    return out


def places_in_rows(ids_ref):
    ids = [ids_ref[:, k : k + 1] for k in range(2)]
    hot = [(iota((TOK, 2 * N), 1) == v).astype(F32) for v in ids]
    before = (iota((TOK, TOK), 1) < iota((TOK, TOK), 0)).astype(F32).astype(BF16)
    count = mm(before, (hot[0] + hot[1]).astype(BF16))
    out = []
    for k in range(2):
        rank = jnp.sum(count * hot[k], axis=1, keepdims=True).astype(jnp.int32)
        target, first = split_slot(ids[k])
        out.append((target, first + rank))
    return out


def send_rows(ids_ref, weights, x_ref, out_ref):
    lanes = []
    for target, slot in places_in_lanes(ids_ref):
        at = target * SPAN + slot
        lanes.append(jnp.concatenate([at + s * PER for s in range(NSEG)], axis=1))
    stacked = jnp.concatenate([x_ref[:, s * SEG : (s + 1) * SEG] for s in range(NSEG)], axis=0)
    block = 384
    for c in range(N * SPAN // block):
        rows = iota((block, NSEG * TOK), 0) + c * block
        pick = jnp.where(
            rows == lanes[0], weights[0], jnp.where(rows == lanes[1], weights[1], 0.0)
        ).astype(BF16)
        out_ref[c * block : (c + 1) * block, :] = mm(pick, stacked).astype(BF16)


def send_tokens_kernel(ids_ref, x_ref, out_ref):
    send_rows(ids_ref, (1.0, 1.0), x_ref, out_ref)


def send_scaled_kernel(ids_ref, prob_ref, x_ref, out_ref):
    probs = [prob_ref[k : k + 1, :].astype(F32) for k in range(2)]
    weights = [jnp.concatenate([v] * NSEG, axis=1) for v in probs]
    send_rows(ids_ref, weights, x_ref, out_ref)


def unmix_rows(perm_ref, got_ref, rows_ref):
    perm = perm_ref[...]
    for g in range(NGROUP):
        part = mm(perm, got_ref[g * GROUP * SPAN : (g + 1) * GROUP * SPAN, :]).astype(BF16)
        for s in range(NSEG):
            rows_ref[s, g * GROWS : (g + 1) * GROWS, :] = part[s * GROWS : (s + 1) * GROWS]


def forward_kernel(
    dp_ref, perm_ref, got_ref, gate_w, up_w, gate_ref, up_ref, hidden_t, x0, x1, x2, x3, rows
):
    @pl.when(pl.program_id(0) == 0)
    def _():
        unmix_rows(perm_ref, got_ref, rows)
        for k, ref in enumerate((x0, x1, x2, x3)):
            which = lax.rem(dp_ref[0] + k, DP)
            ref[...] = rows[which].astype(F32).T.astype(BF16)

    gate = sum(mm(rows[s], gate_w[s * SEG : (s + 1) * SEG, :]) for s in range(NSEG))
    up = sum(mm(rows[s], up_w[s * SEG : (s + 1) * SEG, :]) for s in range(NSEG))
    gate_ref[...] = gate
    up_ref[...] = up
    hidden_t[...] = (gate * jax.nn.sigmoid(gate) * up).T.astype(BF16)


def backward_kernel(
    dp_ref, perm_ref, got_ref, down_w, gate_ref, up_ref, back_ref, q_ref, s0, s1, s2, s3, rows
):
    step = pl.program_id(0)

    @pl.when(step == 0)
    def _():
        unmix_rows(perm_ref, got_ref, rows)
        for k, ref in enumerate((s0, s1, s2, s3)):
            which = lax.rem(dp_ref[0] + k, DP)
            ref[...] = rows[which]
        q_ref[...] = jnp.zeros_like(q_ref)

    back_hidden = sum(mm_t(rows[s], down_w[:, s * SEG : (s + 1) * SEG]) for s in range(NSEG))
    gate = gate_ref[...]
    up = up_ref[...]
    sig = jax.nn.sigmoid(gate)
    activated = gate * sig
    hidden = (activated * up).astype(BF16).astype(F32)
    back_ref[0] = (back_hidden * up * sig * (1.0 + gate * (1.0 - sig))).astype(BF16)
    back_ref[1] = (back_hidden * activated).astype(BF16)
    q_ref[...] += jnp.broadcast_to(jnp.sum(hidden * back_hidden, axis=1, keepdims=True), q_ref.shape)


def return_kernel(mix_ref, mark_ref, back_ref, q_ref, gate_w, up_w, out_ref, rows):
    step = pl.program_id(0)
    part = (mm_t(back_ref[0], gate_w[...]) + mm_t(back_ref[1], up_w[...])).astype(BF16)
    for h in range(SEG // BSEG):
        rows[step * (SEG // BSEG) + h] = part[:, h * BSEG : (h + 1) * BSEG]

    @pl.when(step == pl.num_programs(0) - 1)
    def _():
        mix = mix_ref[...]
        for g in range(NGROUP):
            lo, hi = g * GROWS, (g + 1) * GROWS
            probs = (q_ref[lo:hi, 0:1] * mark_ref[...].astype(F32)).astype(BF16)
            stacked = jnp.concatenate([rows[s, lo:hi, :] for s in range(NBSEG)] + [probs], axis=0)
            out_ref[g * GROUP * BSPAN : (g + 1) * GROUP * BSPAN, :] = mm(mix, stacked).astype(BF16)


def combine_kernel(ids_ref, prob_ref, perm_ref, got_ref, tok_ref, gprob_ref, rows, probs):
    perm = perm_ref[...]
    for g in range(NGROUP):
        part = mm(perm, got_ref[g * GROUP * BSPAN : (g + 1) * GROUP * BSPAN, :])
        for s in range(NBSEG):
            rows[g * GROWS : (g + 1) * GROWS, s * BSEG : (s + 1) * BSEG] = part[
                s * GROWS : (s + 1) * GROWS
            ].astype(BF16)
        probs[g * GROUP : (g + 1) * GROUP, :] = part[NBSEG * GROWS : NBSEG * GROWS + GROUP]
    places = places_in_rows(ids_ref)
    at = [target * PER + slot for target, slot in places]
    columns = iota((TOK, ROWS), 1)
    pick = jnp.where((columns == at[0]) | (columns == at[1]), 1.0, 0.0).astype(BF16)
    tok_ref[...] = mm(pick, rows[...]).astype(BF16)
    home = probs[...].astype(BF16)
    result = []
    for k, (target, slot) in enumerate(places):
        owner = (iota((TOK, N), 1) == target).astype(F32).astype(BF16)
        line = mm(owner, home)
        value = jnp.sum(jnp.where(iota((TOK, BSEG), 1) == slot, line, 0.0), axis=1, keepdims=True)
        result.append(value / prob_ref[:, k : k + 1].astype(F32))
    gprob_ref[...] = jnp.where(iota((TOK, 2), 1) == 0, result[0], result[1]).astype(BF16)


def down_grad_kernel(dp_ref, hidden_t, s0, s1, s2, s3, out_ref, acc):
    step = pl.program_id(0)
    for k, ref in enumerate((s0, s1, s2, s3)):

        @pl.when(step == k)
        def _():
            term = mm(hidden_t[0], ref[...])
            acc[...] = term if k == 0 else acc[...] + term

    @pl.when(step == DP - 1)
    def _():
        out_ref[...] = acc[...].astype(BF16)


def gate_up_grad_kernel(dp_ref, back_ref, x0, x1, x2, x3, gate_out, up_out, acc):
    step = pl.program_id(0)
    for k, ref in enumerate((x0, x1, x2, x3)):

        @pl.when(step == k)
        def _():
            for m in range(2):
                term = mm(ref[...], back_ref[0, m])
                acc[m] = term if k == 0 else acc[m] + term

    @pl.when(step == DP - 1)
    def _():
        gate_out[...] = acc[0].astype(BF16)
        up_out[...] = acc[1].astype(BF16)


def shape(dims, kind=BF16):
    return jax.ShapeDtypeStruct(dims, kind)


def whole(dims):
    return pl.BlockSpec(dims, lambda *_: (0,) * len(dims))


def call(kernel, name, grid, in_specs, out_specs, out_shape, scratch=(), scalars=0, flops=0):
    return pl.pallas_call(
        kernel,
        name=name,
        grid_spec=pltpu.PrefetchScalarGridSpec(
            num_scalar_prefetch=scalars,
            grid=grid,
            in_specs=in_specs,
            out_specs=out_specs,
            scratch_shapes=list(scratch),
        ),
        out_shape=out_shape,
        compiler_params=pltpu.CompilerParams(vmem_limit_bytes=48 * 1024 * 1024),
        cost_estimate=pl.CostEstimate(flops=flops, bytes_accessed=8 << 20, transcendentals=0),
    )


def exchange(values):
    return lax.all_to_all(values, "expert", split_axis=0, concat_axis=0, tiled=True)


def spread(pieces):
    moved = [pieces[0]]
    for k in range(1, DP):
        moved.append(lax.ppermute(pieces[k], "dp", [(i, (i + k) % DP) for i in range(DP)]))
    return moved


def body(tokens, cotangent, gate_probs, expert_ids, gate_weight, up_weight, down_weight):
    gate_w, up_w, down_w = gate_weight[0], up_weight[0], down_weight[0]
    unmix = jnp.asarray(UNMIX, BF16)
    back_perm = jnp.asarray(BACK, BF16)
    mix = jnp.asarray(MIX, BF16)
    mark = jnp.asarray(MARK, BF16)
    dp = lax.axis_index("dp").astype(jnp.int32).reshape(1)
    ids_t = expert_ids.T
    probs_t = gate_probs.T

    send_x = call(
        send_tokens_kernel, "send_tokens", (1,), [whole((2, TOK)), whole((TOK, D))],
        whole((N * SPAN, SEG)), shape((N * SPAN, SEG)), flops=800 << 20,
    )(ids_t, tokens)
    got_x = exchange(send_x.reshape(N, SPAN, SEG)).reshape(N * SPAN, SEG)
    send_c = call(
        send_scaled_kernel, "send_scaled", (1,),
        [whole((2, TOK)), whole((2, TOK)), whole((TOK, D))],
        whole((N * SPAN, SEG)), shape((N * SPAN, SEG)), flops=800 << 20,
    )(ids_t, probs_t, cotangent)
    got_c = exchange(send_c.reshape(N, SPAN, SEG)).reshape(N * SPAN, SEG)

    gate, up, hidden_t, *x_pieces = call(
        forward_kernel, "forward", (NFB,),
        [
            whole(UNMIX.shape),
            whole((N * SPAN, SEG)),
            pl.BlockSpec((D, FB), lambda i, *_: (0, i)),
            pl.BlockSpec((D, FB), lambda i, *_: (0, i)),
        ],
        [
            pl.BlockSpec((ROWS, FB), lambda i, *_: (0, i)),
            pl.BlockSpec((ROWS, FB), lambda i, *_: (0, i)),
            pl.BlockSpec((FB, ROWS), lambda i, *_: (i, 0)),
        ]
        + [whole((SEG, ROWS))] * DP,
        [shape((ROWS, FF), F32), shape((ROWS, FF), F32), shape((FF, ROWS))]
        + [shape((SEG, ROWS))] * DP,
        scratch=[pltpu.VMEM((NSEG, ROWS, SEG), BF16)], scalars=1, flops=3000 << 20,
    )(dp, unmix, got_x, gate_w, up_w)
    x_pieces = spread(x_pieces)
    hidden_all = lax.all_gather(hidden_t, "dp", axis=0, tiled=True).reshape(DP, FF, ROWS)

    back, q, *s_pieces = call(
        backward_kernel, "backward", (NFB,),
        [
            whole(UNMIX.shape),
            whole((N * SPAN, SEG)),
            pl.BlockSpec((FB, D), lambda i, *_: (i, 0)),
            pl.BlockSpec((ROWS, FB), lambda i, *_: (0, i)),
            pl.BlockSpec((ROWS, FB), lambda i, *_: (0, i)),
        ],
        [pl.BlockSpec((2, ROWS, FB), lambda i, *_: (0, 0, i)), whole((ROWS, 128))]
        + [whole((ROWS, SEG))] * DP,
        [shape((2, ROWS, FF)), shape((ROWS, 128), F32)] + [shape((ROWS, SEG))] * DP,
        scratch=[pltpu.VMEM((NSEG, ROWS, SEG), BF16)], scalars=1, flops=2000 << 20,
    )(dp, unmix, got_c, down_w, gate, up)
    back_all = lax.all_gather(back.reshape(2 * ROWS, FF), "dp", axis=0, tiled=True)
    back_all = back_all.reshape(DP, 2, ROWS, FF)
    s_pieces = spread(s_pieces)

    send_b = call(
        return_kernel, "send_back", (NSEG,),
        [
            whole(MIX.shape),
            whole(MARK.shape),
            whole((2, ROWS, FF)),
            whole((ROWS, 128)),
            pl.BlockSpec((SEG, FF), lambda i, *_: (i, 0)),
            pl.BlockSpec((SEG, FF), lambda i, *_: (i, 0)),
        ],
        whole((N * BSPAN, BSEG)), shape((N * BSPAN, BSEG)),
        scratch=[pltpu.VMEM((NBSEG, ROWS, BSEG), BF16)], flops=3000 << 20,
    )(mix, mark, back, q, gate_w, up_w)
    got_b = exchange(send_b.reshape(N, BSPAN, BSEG)).reshape(N * BSPAN, BSEG)

    def other(i, dp_ref):
        return lax.rem(dp_ref[0] - i + DP, DP)

    grad_down = call(
        down_grad_kernel, "down_grad", (DP,),
        [pl.BlockSpec((1, FF, ROWS), lambda i, r: (other(i, r), 0, 0))] + [whole((ROWS, SEG))] * DP,
        whole((FF, SEG)), shape((FF, SEG)),
        scratch=[pltpu.VMEM((FF, SEG), F32)], scalars=1, flops=1200 << 20,
    )(dp, hidden_all, *s_pieces)
    grad_gate, grad_up = call(
        gate_up_grad_kernel, "gate_up_grad", (DP,),
        [pl.BlockSpec((1, 2, ROWS, FF), lambda i, r: (other(i, r), 0, 0, 0))]
        + [whole((SEG, ROWS))] * DP,
        [whole((SEG, FF))] * 2, [shape((SEG, FF))] * 2,
        scratch=[pltpu.VMEM((2, SEG, FF), F32)], scalars=1, flops=2400 << 20,
    )(dp, back_all, *x_pieces)
    grad_tokens, grad_probs = call(
        combine_kernel, "combine", (1,),
        [whole((TOK, 2)), whole((TOK, 2)), whole(BACK.shape), whole((N * BSPAN, BSEG))],
        [whole((TOK, D)), whole((TOK, 2))], [shape((TOK, D)), shape((TOK, 2))],
        scratch=[pltpu.VMEM((ROWS, D), BF16), pltpu.VMEM((N, BSEG), F32)], flops=1000 << 20,
    )(expert_ids, gate_probs, back_perm, got_b)
    return grad_tokens, grad_probs, grad_gate[None], grad_up[None], grad_down[None]


def solution(mesh):
    in_specs = (
        P(("dp", "expert"), None),
        P(("dp", "expert"), None),
        P(("dp", "expert"), None),
        P(("dp", "expert"), None),
        P("expert", None, None),
        P("expert", None, None),
        P("expert", None, None),
    )
    out_specs = (
        P(("dp", "expert"), None),
        P(("dp", "expert"), None),
        P("expert", "dp", None),
        P("expert", "dp", None),
        P("expert", None, "dp"),
    )
    return jax.shard_map(body, mesh=mesh, in_specs=in_specs, out_specs=out_specs, check_vma=False)
```

profile of v0, /device:TPU:1, one launch (start us, length us, event | category | flops | bytes accessed | tf_op | source)
XLA Modules:
  0.0 229.9 jit_solution(14228376140107184609)
XLA Ops:
  7.2 0.0 copy-start.2
  7.2 0.7 copy-done.2
  7.8 0.0 copy-start.5
  7.8 1.0 copy-done.5
  8.9 2.3 %send_tokens.1 = bf16[1536,512]{1,0:T(8,128)(2,1)} custom-call(s32[2,128]{1,0:T(2,128)S(1)} %bitcast.23, bf16[128,2048]{1,0:T(8,128)(2,1)S(1)} %copy-done.5), custom_call_target="tpu_custom_call" | custom-call | flops 838860800 | bytes 8388608 | tf_op jit(solution)/shard_map/send_tokens/pallas_call | solution.py:289
  11.2 0.0 copy-start.13
  11.2 13.3 %all-to-all-start.1 = ((bf16[64,24,512]{2,1,0:T(8,128)(2,1)}), bf16[64,24,512]{2,1,0:T(8,128)(2,1)S(1)}, u32[]{:S(2)}, u32[]{:S(2)}) async-start(bf16[64,24,512]{2,1,0:T(8,128)(2,1)} %bitcast.6), calls=%async_computation.1 | async-start | bytes 3145728 | tf_op jit(solution)/shard_map/all_to_all | solution.py:269
  24.5 0.0 all-gather.5.cloned.1.call-start
  24.6 39.7 %all-to-all-done.1 = bf16[64,24,512]{2,1,0:T(8,128)(2,1)S(1)} async-done(((bf16[64,24,512]{2,1,0:T(8,128)(2,1)}), bf16[64,24,512]{2,1,0:T(8,128)(2,1)S(1)}, u32[]{:S(2)}, u32[]{:S(2)}) %all-to-all-start.1) | async-done | bytes 1572896 | tf_op jit(solution)/shard_map/all_to_all | solution.py:269
  64.3 0.0 copy-done.13
  64.3 0.0 copy-start.3
  64.3 0.0 copy-start.4
  64.3 0.0 copy-start.6
  64.3 7.2 %forward.1 = (f32[384,768]{1,0:T(8,128)S(1)}, f32[384,768]{1,0:T(8,128)S(1)}, bf16[768,384]{1,0:T(8,128)(2,1)}, bf16[512,384]{1,0:T(8,128)(2,1)S(1)}, bf16[512,3...) custom-call(s32[1]{0:T(128)} %bitcast.dp_ref, bf16[192,192]{1,0:T(8,128)(2,1)S(1)} %copy-done.13, ...), custom_call_target="tpu_custom_call" | custom-call | flops 3145728000 | bytes 8388608 | tf_op jit(solution)/shard_map/forward/pallas_call | solution.py:301
  71.5 0.0 copy-start.7
  71.5 0.8 copy-done.7
  72.2 0.0 copy-start.8
  72.2 0.8 copy-done.8
  73.0 0.8 copy-done.9
  73.8 1.0 copy-done.15
  74.8 0.7 copy-done.19
  75.5 0.0 all-gather.5.cloned.1.call-update
  75.6 0.0 all-gather.3.cloned.1.call-start
  75.6 0.0 copy-done.3
  75.6 0.0 copy-done.4
  75.6 0.0 copy-done.6
  75.6 1.1 send_scaled.1
  76.8 0.0 copy-start.16
  76.8 45.9 %all_to_all.15 = bf16[64,24,512]{2,1,0:T(8,128)(2,1)} all-to-all(bf16[64,24,512]{2,1,0:T(8,128)(2,1)S(1)} %bitcast.22), channel_id=1, replica_groups=mesh['dp'=4,'expert'=64] {'expert'}, dimensions={0} | all-to-all | bytes 3145728 | tf_op jit(solution)/shard_map/all_to_all | solution.py:269
  122.7 0.0 copy-done.16
  122.7 6.1 %backward.1 = (bf16[2,384,768]{2,1,0:T(8,128)(2,1)}, f32[384,128]{1,0:T(8,128)S(1)}, bf16[384,512]{1,0:T(8,128)(2,1)S(1)}, bf16[384,512]{1,0:T(8,128)(2,1)}, bf1...) custom-call(s32[1]{0:T(128)} %bitcast.dp_ref, bf16[192,192]{1,0:T(8,128)(2,1)S(1)} %copy-done.13, ...), custom_call_target="tpu_custom_call" | custom-call | flops 2097152000 | bytes 8388608 | tf_op jit(solution)/shard_map/backward/pallas_call | solution.py:322
  128.8 0.8 copy-done.10
  129.5 0.7 copy-done.17
  130.2 0.0 all-gather.3.cloned.1.call-update
  130.2 0.0 copy-done.11
  130.2 0.0 copy-done.14
  130.2 0.0 copy-start.18
  130.3 0.9 copy-done.18
  131.2 6.8 %send_back.1 = bf16[3584,256]{1,0:T(8,128)(2,1)S(1)} custom-call(bf16[448,432]{1,0:T(8,128)(2,1)S(1)} %copy-done.11, bf16[48,256]{1,0:T(8,128)(2,1)S(1)} %copy-done.14, bf16[2,384,768]{2,1,0:T(8,128)(2,1)} %get-tuple-element.24.back_ref, f32[384,128]{1,0:T(8,128)S(1)} %copy-done.18, bf16[2048,768]{1,0:T(8,128)(2,1)} %bitcast.31, bf16[2048,768]{1,0:T(8,128)(2,1)} %bitcast.33), custom_call_target="tpu_custom_call" | custom-call | flops 3145728000 | bytes 8388608 | tf_op jit(solution)/shard_map/send_back/pallas_call | solution.py:340
  138.0 0.0 copy-start.1
  138.0 1.3 copy-done.1
  139.3 6.1 %all-to-all-start.2 = ((bf16[64,56,256]{2,1,0:T(8,128)(2,1)}), bf16[64,56,256]{2,1,0:T(8,128)(2,1)S(1)}, u32[]{:S(2)}, u32[]{:S(2)}) async-start(bf16[64,56,256]{2,1,0:T(8,128)(2,1)} %bitcast.20), calls=%async_computation.2 | async-start | bytes 3670016 | tf_op jit(solution)/shard_map/all_to_all | solution.py:269
  145.4 1.3 collective-permute-start.3
  146.7 2.5 %collective-permute-start.4 = (bf16[384,512]{1,0:T(8,128)(2,1)}, bf16[384,512]{1,0:T(8,128)(2,1)S(1)}, u32[]{:S(2)}, u32[]{:S(2)}) collective-permute-start(bf16[384,512]{1,0:T(8,128)(2,1)} %get-tuple-element.37), channel_id=1, source_target_pairs={{0,128},{64,192},{128,0},{192,64},{1,129},{65,193},{129,1},{193,65... | collective-permute-start | bytes 1179656 | tf_op jit(solution)/shard_map/ppermute | solution.py:275
  149.2 1.1 collective-permute-start.5
  150.3 0.3 collective-permute-start
  150.6 0.9 collective-permute-start.1
  151.5 15.0 %collective-permute-done.3.s1 = bf16[384,512]{1,0:T(8,128)(2,1)S(1)} collective-permute-done((bf16[384,512]{1,0:T(8,128)(2,1)}, bf16[384,512]{1,0:T(8,128)(2,1)S(1)}, u32[]{:S(2)}, u32[]{:S(2)}) %collective-permute-start.3) | collective-permute-done | bytes 393248 | tf_op jit(solution)/shard_map/ppermute | solution.py:275
  166.4 1.3 collective-permute-start.2
  167.7 0.1 copy.16.ids_ref
  167.8 0.1 copy.17.prob_ref
  168.0 16.2 %collective-permute-done.4.s2 = bf16[384,512]{1,0:T(8,128)(2,1)S(1)} collective-permute-done((bf16[384,512]{1,0:T(8,128)(2,1)}, bf16[384,512]{1,0:T(8,128)(2,1)S(1)}, u32[]{:S(2)}, u32[]{:S(2)}) %collective-permute-start.4) | collective-permute-done | bytes 393248 | tf_op jit(solution)/shard_map/ppermute | solution.py:275
  184.2 0.0 collective-permute-done.5.s3
  184.2 1.7 copy-done
  185.9 3.3 %down_grad.1 = bf16[768,512]{1,0:T(8,128)(2,1)} custom-call(s32[1]{0:T(128)} %bitcast.dp_ref, bf16[4,768,384]{2,1,0:T(8,128)(2,1)S(1)} %bitcast.18, bf16[384,512]{1,0:T(8,128)(2,1)S(1)} %get-tuple-element.35.s0, bf16[384,512]{1,0:T(8,128)(2,1)S(1)} %collective-permute-done.3.s1, bf16[384,512]{1,0:T(8,128)(2,1)S(1)} %collective-permute-done.4.s2, ...), custom_call_target="tpu_custom_call" | custom-call | flops 1258291200 | bytes 8388608 | tf_op jit(solution)/shard_map/down_grad/pallas_call | solution.py:358
  189.2 1.6 all-to-all-done.2
  190.8 1.0 copy-done.12
  191.8 2.5 %combine.1 = (bf16[128,2048]{1,0:T(8,128)(2,1)}, bf16[128,2]{1,0:T(8,128)(2,1)S(1)}) custom-call(s32[128,2]{1,0:T(8,128)S(1)} %copy.16.ids_ref, bf16[128,2]{1,0:T(8,128)(2,1)S(1)} %copy.17.prob_ref, bf16[400,448]{1,0:T(8,128)(2,1)S(1)} %copy-done.12, bf16[3584,256]{1,0:T(8,128)(2,1)S(1)} %bitcast.19), custom_call_target="tpu_custom_call" | custom-call | flops 1048576000 | bytes 8388608 | tf_op jit(solution)/shard_map/combine/pallas_call | solution.py:371
  194.3 0.6 copy.18
  194.9 3.0 %collective-permute-done.x1 = bf16[512,384]{1,0:T(8,128)(2,1)} collective-permute-done((bf16[512,384]{1,0:T(8,128)(2,1)}, bf16[512,384]{1,0:T(8,128)(2,1)}, u32[]{:S(2)}, u32[]{:S(2)}) %collective-permute-start) | collective-permute-done | bytes 393248 | tf_op jit(solution)/shard_map/ppermute | solution.py:275
  198.0 18.0 %collective-permute-done.1.x2 = bf16[512,384]{1,0:T(8,128)(2,1)} collective-permute-done((bf16[512,384]{1,0:T(8,128)(2,1)}, bf16[512,384]{1,0:T(8,128)(2,1)}, u32[]{:S(2)}, u32[]{:S(2)}) %collective-permute-start.1) | collective-permute-done | bytes 393248 | tf_op jit(solution)/shard_map/ppermute | solution.py:275
  215.9 0.0 collective-permute-done.2.x3
  216.0 0.0 copy-done.20
  216.0 7.1 %gate_up_grad.1 = (bf16[512,768]{1,0:T(8,128)(2,1)}, bf16[512,768]{1,0:T(8,128)(2,1)}) custom-call(s32[1]{0:T(128)} %bitcast.dp_ref, bf16[4,2,384,768]{3,2,1,0:T(8,128)(2,1)} %bitcast.28, bf16[512,384]{1,0:T(8,128)(2,1)S(1)} %copy-done.20, bf16[512,384]{1,0:T(8,128)(2,1)} %collective-permute-done.x1, bf16[512,384]{1,0:T(8,128)(2,1)} %collective-permute-done.1.x2, ...), custom_call_target="tpu_custom_call" | custom-call | flops 2516582400 | bytes 8388608 | tf_op jit(solution)/shard_map/gate_up_grad/pallas_call | solution.py:364
  (12 shorter events, 0.0 us)
Async XLA Ops:
  7.2 0.7 copy-start.2
  7.8 1.0 copy-start.5
  11.2 53.0 %copy-start.13 = (bf16[192,192]{1,0:T(8,128)(2,1)S(1)}, bf16[192,192]{1,0:T(8,128)(2,1)}, u32[]{:S(2)}) copy-start(bf16[192,192]{1,0:T(8,128)(2,1)} %constant.14.clone.perm_ref) | copy-start | bytes 221188
  11.2 53.0 %all-to-all-start.1 = ((bf16[64,24,512]{2,1,0:T(8,128)(2,1)}), bf16[64,24,512]{2,1,0:T(8,128)(2,1)S(1)}, u32[]{:S(2)}, u32[]{:S(2)}) async-start(bf16[64,24,512]{2,1,0:T(8,128)(2,1)} %bitcast.6), calls=%async_computation.1 | async-start | bytes 3145728 | tf_op jit(solution)/shard_map/all_to_all | solution.py:269
  24.5 159.7 %all-gather.5.cloned.1.call-start = ((), (), s32[]{:S(2)}) async-start(), calls=%async_computation.4 | async-start | bytes 2949120 | tf_op jit(solution)/shard_map/all_gather | solution.py:320
  64.3 11.3 %copy-start.3 = (s32[128,2]{0,1:T(2,128)S(1)}, s32[128,2]{0,1:T(2,128)}, u32[]{:S(2)}) copy-start(s32[128,2]{0,1:T(2,128)} %param.14) | copy-start | bytes 3076
  64.3 11.3 %copy-start.4 = (bf16[128,2]{0,1:T(2,128)(2,1)S(1)}, bf16[128,2]{0,1:T(2,128)(2,1)}, u32[]{:S(2)}) copy-start(bf16[128,2]{0,1:T(2,128)(2,1)} %param.13) | copy-start | bytes 1540
  64.3 11.4 %copy-start.6 = (bf16[128,2048]{1,0:T(8,128)(2,1)S(1)}, bf16[128,2048]{1,0:T(8,128)(2,1)}, u32[]{:S(2)}) copy-start(bf16[128,2048]{1,0:T(8,128)(2,1)} %x_ref.2) | copy-start | bytes 1572868
  71.5 0.8 copy-start.7
  72.2 0.8 copy-start.8
  73.0 0.8 copy-start.9
  73.8 1.0 copy-start.15
  74.8 0.7 copy-start.19
  75.6 140.4 %all-gather.3.cloned.1.call-start = ((), (), s32[]{:S(2)}) async-start(), calls=%async_computation.3 | async-start | bytes 5898240 | tf_op jit(solution)/shard_map/all_gather | solution.py:336
  76.8 45.9 %copy-start.16 = (f32[384,768]{1,0:T(8,128)S(1)}, f32[384,768]{1,0:T(8,128)}, u32[]{:S(2)}) copy-start(f32[384,768]{1,0:T(8,128)} %copy-done.15) | copy-start | bytes 3538948
  122.7 7.6 %copy-start.11 = (bf16[448,432]{1,0:T(8,128)(2,1)S(1)}, bf16[448,432]{1,0:T(8,128)(2,1)}, u32[]{:S(2)}) copy-start(bf16[448,432]{1,0:T(8,128)(2,1)} %constant.16.clone.mix_ref) | copy-start | bytes 1161220
  122.7 7.6 %copy-start.14 = (bf16[48,256]{1,0:T(8,128)(2,1)S(1)}, bf16[48,256]{1,0:T(8,128)(2,1)}, u32[]{:S(2)}) copy-start(bf16[48,256]{1,0:T(8,128)(2,1)} %constant.17.clone.mark_ref) | copy-start | bytes 73732
  128.7 0.8 copy-start.10
  129.5 0.7 copy-start.17
  130.2 0.9 copy-start.18
  138.0 1.3 copy-start.1
  139.3 51.5 %all-to-all-start.2 = ((bf16[64,56,256]{2,1,0:T(8,128)(2,1)}), bf16[64,56,256]{2,1,0:T(8,128)(2,1)S(1)}, u32[]{:S(2)}, u32[]{:S(2)}) async-start(bf16[64,56,256]{2,1,0:T(8,128)(2,1)} %bitcast.20), calls=%async_computation.2 | async-start | bytes 3670016 | tf_op jit(solution)/shard_map/all_to_all | solution.py:269
  145.4 21.0 %collective-permute-start.3 = (bf16[384,512]{1,0:T(8,128)(2,1)}, bf16[384,512]{1,0:T(8,128)(2,1)S(1)}, u32[]{:S(2)}, u32[]{:S(2)}) collective-permute-start(bf16[384,512]{1,0:T(8,128)(2,1)} %get-tuple-element.36), channel_id=1, source_target_pairs={{0,64},{64,128},{128,192},{192,0},{1,65},{65,129},{129,193},{193,1... | collective-permute-start | bytes 1179656 | tf_op jit(solution)/shard_map/ppermute | solution.py:275
  146.7 37.5 %collective-permute-start.4 = (bf16[384,512]{1,0:T(8,128)(2,1)}, bf16[384,512]{1,0:T(8,128)(2,1)S(1)}, u32[]{:S(2)}, u32[]{:S(2)}) collective-permute-start(bf16[384,512]{1,0:T(8,128)(2,1)} %get-tuple-element.37), channel_id=1, source_target_pairs={{0,128},{64,192},{128,0},{192,64},{1,129},{65,193},{129,1},{193,65... | collective-permute-start | bytes 1179656 | tf_op jit(solution)/shard_map/ppermute | solution.py:275
  149.2 35.0 %collective-permute-start.5 = (bf16[384,512]{1,0:T(8,128)(2,1)}, bf16[384,512]{1,0:T(8,128)(2,1)S(1)}, u32[]{:S(2)}, u32[]{:S(2)}) collective-permute-start(bf16[384,512]{1,0:T(8,128)(2,1)} %copy-done.10), channel_id=1, source_target_pairs={{0,192},{64,0},{128,64},{192,128},{1,193},{65,1},{129,65},{193,129... | collective-permute-start | bytes 1179656 | tf_op jit(solution)/shard_map/ppermute | solution.py:275
  150.3 47.6 %collective-permute-start = (bf16[512,384]{1,0:T(8,128)(2,1)}, bf16[512,384]{1,0:T(8,128)(2,1)}, u32[]{:S(2)}, u32[]{:S(2)}) collective-permute-start(bf16[512,384]{1,0:T(8,128)(2,1)} %copy-done.9), channel_id=1, source_target_pairs={{0,64},{64,128},{128,192},{192,0},{1,65},{65,129},{129,193},{193,1... | collective-permute-start | bytes 1179656 | tf_op jit(solution)/shard_map/ppermute | solution.py:275
  150.6 65.3 %collective-permute-start.1 = (bf16[512,384]{1,0:T(8,128)(2,1)}, bf16[512,384]{1,0:T(8,128)(2,1)}, u32[]{:S(2)}, u32[]{:S(2)}) collective-permute-start(bf16[512,384]{1,0:T(8,128)(2,1)} %copy-done.8), channel_id=1, source_target_pairs={{0,128},{64,192},{128,0},{192,64},{1,129},{65,193},{129,1},{193,65... | collective-permute-start | bytes 1179656 | tf_op jit(solution)/shard_map/ppermute | solution.py:275
  166.4 49.5 %collective-permute-start.2 = (bf16[512,384]{1,0:T(8,128)(2,1)}, bf16[512,384]{1,0:T(8,128)(2,1)}, u32[]{:S(2)}, u32[]{:S(2)}) collective-permute-start(bf16[512,384]{1,0:T(8,128)(2,1)} %copy-done.7), channel_id=1, source_target_pairs={{0,192},{64,0},{128,64},{192,128},{1,193},{65,1},{129,65},{193,129... | collective-permute-start | bytes 1179656 | tf_op jit(solution)/shard_map/ppermute | solution.py:275
  184.2 1.7 copy-start
  190.8 1.0 copy-start.12
  191.8 24.1 %copy-start.20 = (bf16[512,384]{1,0:T(8,128)(2,1)S(1)}, bf16[512,384]{1,0:T(8,128)(2,1)}, u32[]{:S(2)}) copy-start(bf16[512,384]{1,0:T(8,128)(2,1)} %copy-done.19) | copy-start | bytes 1179652
Sparse Core Ops, SparseCore 0:
  75.7 32.0 all-gather.4
  130.3 82.3 all-gather.2
where the time goes:
time: 231 us; the launch traced here: 230 us
  waiting for transfers between devices  93.6 us (41%)
  blocking collectives  45.9 us (20%)
  Pallas kernels  36.4 us (16%)
  starting transfers between devices  26.8 us (12%)
  between operations  14.2 us (6%)
  local copies, waits for them, and re-layouts  13 us (6%)
    ppermute x6, waiting for transfers between devices, spread(): lax.ppermute(pieces[k], 'dp', [(i, (i + k) % DP) for i in range(DP)])  52.2 us
    all_to_all x1, blocking collectives, exchange(): lax.all_to_all(values, 'expert', split_axis=0, concat_axis=0, tiled=True)  45.9 us
    all_to_all x2, waiting for transfers between devices, exchange(): lax.all_to_all(values, 'expert', split_axis=0, concat_axis=0, tiled=True)  41.3 us
    all_to_all x2, starting transfers between devices, exchange(): lax.all_to_all(values, 'expert', split_axis=0, concat_axis=0, tiled=True)  19.4 us
    unnamed x45, local copies, waits for them, and re-layouts  13 us
    ppermute x6, starting transfers between devices, spread(): lax.ppermute(pieces[k], 'dp', [(i, (i + k) % DP) for i in range(DP)])  7.35 us
    pallas_call x1, Pallas kernels, body(): call(forward_kernel, 'forward', (NFB,), [whole(UNMIX.shape), whole((N * S...  7.2 us
    pallas_call x1, Pallas kernels, body(): call(gate_up_grad_kernel, 'gate_up_grad', (DP,), [pl.BlockSpec((1, 2, ROW...  7.1 us
  transfers between devices with their start and end apart: 10, of which 6 were waited for; matrix products, arithmetic and copies ran while one was open for 0% of the time, Pallas kernels for 9%

commit v1 on v0

--- a/solution.py
+++ b/solution.py
@@ -5,6 +5,7 @@
 from jax.experimental import pallas as pl
 from jax.experimental.pallas import tpu as pltpu
 from jax.sharding import PartitionSpec as P
+
 
 F32 = jnp.float32
 BF16 = jnp.bfloat16
@@ -241,17 +242,20 @@
 
 
 def shape(dims, kind=BF16):
-    return jax.ShapeDtypeStruct(dims, kind)
+    return pltpu.HBM(dims, kind)
+
+
+def in_hbm(values):
+    return pltpu.with_memory_space_constraint(values, pltpu.HBM)
 
 
 def whole(dims):
     return pl.BlockSpec(dims, lambda *_: (0,) * len(dims))
 
 
-def call(kernel, name, grid, in_specs, out_specs, out_shape, scratch=(), scalars=0, flops=0):
+def call(kernel, grid, in_specs, out_specs, out_shape, scratch=(), scalars=0, flops=0):
     return pl.pallas_call(
         kernel,
-        name=name,
         grid_spec=pltpu.PrefetchScalarGridSpec(
             num_scalar_prefetch=scalars,
             grid=grid,
@@ -260,13 +264,17 @@
             scratch_shapes=list(scratch),
         ),
         out_shape=out_shape,
-        compiler_params=pltpu.CompilerParams(vmem_limit_bytes=48 * 1024 * 1024),
+        compiler_params=pltpu.CompilerParams(vmem_limit_bytes=24 * 1024 * 1024),
         cost_estimate=pl.CostEstimate(flops=flops, bytes_accessed=8 << 20, transcendentals=0),
     )
 
 
 def exchange(values):
     return lax.all_to_all(values, "expert", split_axis=0, concat_axis=0, tiled=True)
+
+
+def gather(values):
+    return lax.all_gather(values, "dp", axis=0, tiled=True)
 
 
 def spread(pieces):
@@ -277,7 +285,7 @@
 
 
 def body(tokens, cotangent, gate_probs, expert_ids, gate_weight, up_weight, down_weight):
-    gate_w, up_w, down_w = gate_weight[0], up_weight[0], down_weight[0]
+    gate_w, up_w, down_w = in_hbm(gate_weight[0]), in_hbm(up_weight[0]), in_hbm(down_weight[0])
     unmix = jnp.asarray(UNMIX, BF16)
     back_perm = jnp.asarray(BACK, BF16)
     mix = jnp.asarray(MIX, BF16)
@@ -287,19 +295,19 @@
     probs_t = gate_probs.T
 
     send_x = call(
-        send_tokens_kernel, "send_tokens", (1,), [whole((2, TOK)), whole((TOK, D))],
+        send_tokens_kernel, (1,), [whole((2, TOK)), whole((TOK, D))],
         whole((N * SPAN, SEG)), shape((N * SPAN, SEG)), flops=800 << 20,
     )(ids_t, tokens)
     got_x = exchange(send_x.reshape(N, SPAN, SEG)).reshape(N * SPAN, SEG)
     send_c = call(
-        send_scaled_kernel, "send_scaled", (1,),
+        send_scaled_kernel, (1,),
         [whole((2, TOK)), whole((2, TOK)), whole((TOK, D))],
         whole((N * SPAN, SEG)), shape((N * SPAN, SEG)), flops=800 << 20,
     )(ids_t, probs_t, cotangent)
     got_c = exchange(send_c.reshape(N, SPAN, SEG)).reshape(N * SPAN, SEG)
 
     gate, up, hidden_t, *x_pieces = call(
-        forward_kernel, "forward", (NFB,),
+        forward_kernel, (NFB,),
         [
             whole(UNMIX.shape),
             whole((N * SPAN, SEG)),
@@ -317,10 +325,10 @@
         scratch=[pltpu.VMEM((NSEG, ROWS, SEG), BF16)], scalars=1, flops=3000 << 20,
     )(dp, unmix, got_x, gate_w, up_w)
     x_pieces = spread(x_pieces)
-    hidden_all = lax.all_gather(hidden_t, "dp", axis=0, tiled=True).reshape(DP, FF, ROWS)
+    hidden_all = gather(hidden_t).reshape(DP, FF, ROWS)
 
     back, q, *s_pieces = call(
-        backward_kernel, "backward", (NFB,),
+        backward_kernel, (NFB,),
         [
             whole(UNMIX.shape),
             whole((N * SPAN, SEG)),
@@ -332,13 +340,13 @@
         + [whole((ROWS, SEG))] * DP,
         [shape((2, ROWS, FF)), shape((ROWS, 128), F32)] + [shape((ROWS, SEG))] * DP,
         scratch=[pltpu.VMEM((NSEG, ROWS, SEG), BF16)], scalars=1, flops=2000 << 20,
-    )(dp, unmix, got_c, down_w, gate, up)
-    back_all = lax.all_gather(back.reshape(2 * ROWS, FF), "dp", axis=0, tiled=True)
+    )(dp, unmix, got_c, down_w, in_hbm(gate), in_hbm(up))
+    back_all = gather(back.reshape(2 * ROWS, FF))
     back_all = back_all.reshape(DP, 2, ROWS, FF)
     s_pieces = spread(s_pieces)
 
     send_b = call(
-        return_kernel, "send_back", (NSEG,),
+        return_kernel, (NSEG,),
         [
             whole(MIX.shape),
             whole(MARK.shape),
@@ -349,27 +357,27 @@
         ],
         whole((N * BSPAN, BSEG)), shape((N * BSPAN, BSEG)),
         scratch=[pltpu.VMEM((NBSEG, ROWS, BSEG), BF16)], flops=3000 << 20,
-    )(mix, mark, back, q, gate_w, up_w)
+    )(mix, mark, in_hbm(back), in_hbm(q), gate_w, up_w)
     got_b = exchange(send_b.reshape(N, BSPAN, BSEG)).reshape(N * BSPAN, BSEG)
 
     def other(i, dp_ref):
         return lax.rem(dp_ref[0] - i + DP, DP)
 
     grad_down = call(
-        down_grad_kernel, "down_grad", (DP,),
+        down_grad_kernel, (DP,),
         [pl.BlockSpec((1, FF, ROWS), lambda i, r: (other(i, r), 0, 0))] + [whole((ROWS, SEG))] * DP,
         whole((FF, SEG)), shape((FF, SEG)),
         scratch=[pltpu.VMEM((FF, SEG), F32)], scalars=1, flops=1200 << 20,
-    )(dp, hidden_all, *s_pieces)
+    )(dp, in_hbm(hidden_all), *s_pieces)
     grad_gate, grad_up = call(
-        gate_up_grad_kernel, "gate_up_grad", (DP,),
+        gate_up_grad_kernel, (DP,),
         [pl.BlockSpec((1, 2, ROWS, FF), lambda i, r: (other(i, r), 0, 0, 0))]
         + [whole((SEG, ROWS))] * DP,
         [whole((SEG, FF))] * 2, [shape((SEG, FF))] * 2,
         scratch=[pltpu.VMEM((2, SEG, FF), F32)], scalars=1, flops=2400 << 20,
-    )(dp, back_all, *x_pieces)
+    )(dp, in_hbm(back_all), *x_pieces)
     grad_tokens, grad_probs = call(
-        combine_kernel, "combine", (1,),
+        combine_kernel, (1,),
         [whole((TOK, 2)), whole((TOK, 2)), whole(BACK.shape), whole((N * BSPAN, BSEG))],
         [whole((TOK, D)), whole((TOK, 2))], [shape((TOK, D)), shape((TOK, 2))],
         scratch=[pltpu.VMEM((ROWS, D), BF16), pltpu.VMEM((N, BSEG), F32)], flops=1000 << 20,
@@ -394,4 +402,5 @@
         P("expert", "dp", None),
         P("expert", None, "dp"),
     )
+
     return jax.shard_map(body, mesh=mesh, in_specs=in_specs, out_specs=out_specs, check_vma=False)

time: 231 us -> 227 us (0.983)
  local copies, waits for them, and re-layouts: 13 us -> 4.34 us
  Pallas kernels: 36.4 us -> 41.6 us
    unnamed x45 -> x25, local copies, waits for them, and re-layouts: 13 us -> 4.34 us
    pallas_call x8, Pallas kernels: 36.4 us -> 41.6 us  [the longest x1 8.15 us: body(): call(return_kernel, (NSEG,), [whole(MIX.shape), whole(MARK.shape), whole(...]
  transfers between devices with their start and end apart: 10 -> 10, of which waited for: 6 -> 6; matrix products, arithmetic and copies ran while one was open for 0% -> 1% of each run, Pallas kernels for 9% -> 11%
where the time goes in v1:
time: 227 us
  waiting for transfers between devices  93.7 us (41%)
  blocking collectives  45.9 us (20%)
  Pallas kernels  41.6 us (18%)
  starting transfers between devices  27 us (12%)
  between operations  14.1 us (6%)
  local copies, waits for them, and re-layouts  4.34 us (2%)
    ppermute x6, waiting for transfers between devices, spread(): lax.ppermute(pieces[k], 'dp', [(i, (i + k) % DP) for i in range(DP)])  52.3 us
    all_to_all x1, blocking collectives, exchange(): lax.all_to_all(values, 'expert', split_axis=0, concat_axis=0, tiled=True)  45.9 us
    all_to_all x2, waiting for transfers between devices, exchange(): lax.all_to_all(values, 'expert', split_axis=0, concat_axis=0, tiled=True)  41.5 us
    all_to_all x2, starting transfers between devices, exchange(): lax.all_to_all(values, 'expert', split_axis=0, concat_axis=0, tiled=True)  19.5 us
    pallas_call x1, Pallas kernels, body(): call(return_kernel, (NSEG,), [whole(MIX.shape), whole(MARK.shape), whole(...  8.15 us
    pallas_call x1, Pallas kernels, body(): call(forward_kernel, (NFB,), [whole(UNMIX.shape), whole((N * SPAN, SEG)),...  7.9 us
    ppermute x6, starting transfers between devices, spread(): lax.ppermute(pieces[k], 'dp', [(i, (i + k) % DP) for i in range(DP)])  7.38 us
    pallas_call x1, Pallas kernels, body(): call(gate_up_grad_kernel, (DP,), [pl.BlockSpec((1, 2, ROWS, FF), lambda i...  7.1 us
  transfers between devices with their start and end apart: 10, of which 6 were waited for; matrix products, arithmetic and copies ran while one was open for 1% of the time, Pallas kernels for 11%

profile of v1, /device:TPU:1, one launch (start us, length us, event | category | flops | bytes accessed | tf_op | source)
XLA Modules:
  0.0 226.6 jit_solution(4114112826275423013)
XLA Ops:
  7.2 0.0 copy-start.1
  7.2 0.7 copy-done.1
  7.8 0.0 copy-start.4
  7.8 1.0 copy-done.4
  8.9 2.3 %shard_map.147 = bf16[1536,512]{1,0:T(8,128)(2,1)} custom-call(s32[2,128]{1,0:T(2,128)S(1)} %bitcast.21, bf16[128,2048]{1,0:T(8,128)(2,1)S(1)} %copy-done.4), custom_call_target="tpu_custom_call" | custom-call | flops 838860800 | bytes 8388608 | tf_op jit(solution)/shard_map/pallas_call | solution.py:297
  11.2 0.0 copy-start.8
  11.2 13.3 %all-to-all-start.1 = ((bf16[64,24,512]{2,1,0:T(8,128)(2,1)}), bf16[64,24,512]{2,1,0:T(8,128)(2,1)S(1)}, u32[]{:S(2)}, u32[]{:S(2)}) async-start(bf16[64,24,512]{2,1,0:T(8,128)(2,1)} %bitcast.26), calls=%async_computation.1 | async-start | bytes 3145728 | tf_op jit(solution)/shard_map/all_to_all | solution.py:273
  24.5 0.0 all-gather.5.cloned.1.call-start
  24.6 39.7 %all-to-all-done.1 = bf16[64,24,512]{2,1,0:T(8,128)(2,1)S(1)} async-done(((bf16[64,24,512]{2,1,0:T(8,128)(2,1)}), bf16[64,24,512]{2,1,0:T(8,128)(2,1)S(1)}, u32[]{:S(2)}, u32[]{:S(2)}) %all-to-all-start.1) | async-done | bytes 1572896 | tf_op jit(solution)/shard_map/all_to_all | solution.py:273
  64.3 0.0 copy-done.8
  64.3 0.0 copy-start.2
  64.3 0.0 copy-start.3
  64.3 0.0 copy-start.5
  64.3 7.9 %shard_map.148 = (f32[384,768]{1,0:T(8,128)}, f32[384,768]{1,0:T(8,128)}, bf16[768,384]{1,0:T(8,128)(2,1)}, bf16[512,384]{1,0:T(8,128)(2,1)}, bf16[512,384]{1,0:...) custom-call(s32[1]{0:T(128)} %bitcast.dp_ref, bf16[192,192]{1,0:T(8,128)(2,1)S(1)} %copy-done.8, ...), custom_call_target="tpu_custom_call" | custom-call | flops 3145728000 | bytes 8388608 | tf_op jit(solution)/shard_map/pallas_call | solution.py:309
  72.2 0.0 all-gather.5.cloned.1.call-update
  72.2 0.0 all-gather.3.cloned.1.call-start
  72.3 0.0 copy-done.2
  72.3 0.0 copy-done.3
  72.3 0.0 copy-done.5
  72.3 2.3 %shard_map.146 = bf16[1536,512]{1,0:T(8,128)(2,1)} custom-call(s32[2,128]{1,0:T(2,128)S(1)} %bitcast.22, bf16[2,128]{1,0:T(2,128)(2,1)S(1)} %bitcast.23, bf16[128,2048]{1,0:T(8,128)(2,1)S(1)} %copy-done.5), custom_call_target="tpu_custom_call" | custom-call | flops 838860800 | bytes 8388608 | tf_op jit(solution)/shard_map/pallas_call | solution.py:302
  74.6 45.9 %all_to_all.15 = bf16[64,24,512]{2,1,0:T(8,128)(2,1)S(1)} all-to-all(bf16[64,24,512]{2,1,0:T(8,128)(2,1)} %bitcast.27), channel_id=1, replica_groups=mesh['dp'=4,'expert'=64] {'expert'}, dimensions={0} | all-to-all | bytes 3145728 | tf_op jit(solution)/shard_map/all_to_all | solution.py:273
  120.5 0.0 copy-start.6
  120.5 0.0 copy-start.9
  120.5 6.4 %shard_map.149 = (bf16[2,384,768]{2,1,0:T(8,128)(2,1)}, f32[384,128]{1,0:T(8,128)}, bf16[384,512]{1,0:T(8,128)(2,1)}, bf16[384,512]{1,0:T(8,128)(2,1)}, bf16[384...) custom-call(s32[1]{0:T(128)} %bitcast.dp_ref, bf16[192,192]{1,0:T(8,128)(2,1)S(1)} %copy-done.8, ...), custom_call_target="tpu_custom_call" | custom-call | flops 2097152000 | bytes 8388608 | tf_op jit(solution)/shard_map/pallas_call | solution.py:330
  126.9 0.0 all-gather.3.cloned.1.call-update
  126.9 0.0 copy-done.6
  126.9 0.0 copy-done.9
  126.9 8.2 %shard_map.150 = bf16[3584,256]{1,0:T(8,128)(2,1)} custom-call(bf16[448,432]{1,0:T(8,128)(2,1)S(1)} %copy-done.6, bf16[48,256]{1,0:T(8,128)(2,1)S(1)} %copy-done.9, bf16[2,384,768]{2,1,0:T(8,128)(2,1)} %get-tuple-element.24.back_ref, f32[384,128]{1,0:T(8,128)} %get-tuple-element.25.q_ref, bf16[2048,768]{1,0:T(8,128)(2,1)} %bitcast.33, bf16[2048,768]{1,0:T(8,128)(2,1)} %bitcast.35), custom_call_target="tpu_custom_call" | custom-call | flops 3145728000 | bytes 8388608 | tf_op jit(solution)/shard_map/pallas_call | solution.py:348
  135.1 0.0 copy-start
  135.1 6.2 %all-to-all-start.2 = ((bf16[64,56,256]{2,1,0:T(8,128)(2,1)}), bf16[64,56,256]{2,1,0:T(8,128)(2,1)S(1)}, u32[]{:S(2)}, u32[]{:S(2)}) async-start(bf16[64,56,256]{2,1,0:T(8,128)(2,1)} %bitcast.25), calls=%async_computation.2 | async-start | bytes 3670016 | tf_op jit(solution)/shard_map/all_to_all | solution.py:273
  141.3 1.3 collective-permute-start.3
  142.6 2.5 %collective-permute-start.4 = (bf16[384,512]{1,0:T(8,128)(2,1)}, bf16[384,512]{1,0:T(8,128)(2,1)S(1)}, u32[]{:S(2)}, u32[]{:S(2)}) collective-permute-start(bf16[384,512]{1,0:T(8,128)(2,1)} %get-tuple-element.37), channel_id=1, source_target_pairs={{0,128},{64,192},{128,0},{192,64},{1,129},{65,193},{129,1},{193,65... | collective-permute-start | bytes 1179656 | tf_op jit(solution)/shard_map/ppermute | solution.py:283
  145.1 1.2 collective-permute-start.5
  146.2 0.3 collective-permute-start
  146.5 0.9 collective-permute-start.1
  147.4 14.9 %collective-permute-done.3.s1 = bf16[384,512]{1,0:T(8,128)(2,1)S(1)} collective-permute-done((bf16[384,512]{1,0:T(8,128)(2,1)}, bf16[384,512]{1,0:T(8,128)(2,1)S(1)}, u32[]{:S(2)}, u32[]{:S(2)}) %collective-permute-start.3) | collective-permute-done | bytes 393248 | tf_op jit(solution)/shard_map/ppermute | solution.py:283
  162.3 1.3 collective-permute-start.2
  163.6 0.1 copy.16.ids_ref
  163.7 0.1 copy.17.prob_ref
  163.9 16.2 %collective-permute-done.4.s2 = bf16[384,512]{1,0:T(8,128)(2,1)S(1)} collective-permute-done((bf16[384,512]{1,0:T(8,128)(2,1)}, bf16[384,512]{1,0:T(8,128)(2,1)S(1)}, u32[]{:S(2)}, u32[]{:S(2)}) %collective-permute-start.4) | collective-permute-done | bytes 393248 | tf_op jit(solution)/shard_map/ppermute | solution.py:283
  180.1 0.0 collective-permute-done.5.s3
  180.1 0.0 all-gather.5.cloned.1.call-done
  180.1 0.0 copy-done
  180.1 4.8 %shard_map.153 = bf16[768,512]{1,0:T(8,128)(2,1)} custom-call(s32[1]{0:T(128)} %bitcast.dp_ref, bf16[4,768,384]{2,1,0:T(8,128)(2,1)} %bitcast.24, bf16[384,512]{1,0:T(8,128)(2,1)S(1)} %copy-done, bf16[384,512]{1,0:T(8,128)(2,1)S(1)} %collective-permute-done.3.s1, bf16[384,512]{1,0:T(8,128)(2,1)S(1)} %collective-permute-done.4.s2, ...), custom_call_target="tpu_custom_call" | custom-call | flops 1258291200 | bytes 8388608 | tf_op jit(solution)/shard_map/pallas_call | solution.py:366
  184.9 1.8 all-to-all-done.2
  186.7 0.0 copy-start.7
  186.7 1.0 copy-done.7
  187.7 0.0 copy-start.10
  187.7 2.5 %shard_map.151 = (bf16[128,2048]{1,0:T(8,128)(2,1)}, bf16[128,2]{1,0:T(8,128)(2,1)}) custom-call(s32[128,2]{1,0:T(8,128)S(1)} %copy.16.ids_ref, bf16[128,2]{1,0:T(8,128)(2,1)S(1)} %copy.17.prob_ref, bf16[400,448]{1,0:T(8,128)(2,1)S(1)} %copy-done.7, bf16[3584,256]{1,0:T(8,128)(2,1)S(1)} %bitcast.18), custom_call_target="tpu_custom_call" | custom-call | flops 1048576000 | bytes 8388608 | tf_op jit(solution)/shard_map/pallas_call | solution.py:379
  190.2 1.3 copy.18
  191.6 2.3 %collective-permute-done.x1 = bf16[512,384]{1,0:T(8,128)(2,1)} collective-permute-done((bf16[512,384]{1,0:T(8,128)(2,1)}, bf16[512,384]{1,0:T(8,128)(2,1)}, u32[]{:S(2)}, u32[]{:S(2)}) %collective-permute-start) | collective-permute-done | bytes 393248 | tf_op jit(solution)/shard_map/ppermute | solution.py:283
  193.9 18.8 %collective-permute-done.1.x2 = bf16[512,384]{1,0:T(8,128)(2,1)} collective-permute-done((bf16[512,384]{1,0:T(8,128)(2,1)}, bf16[512,384]{1,0:T(8,128)(2,1)}, u32[]{:S(2)}, u32[]{:S(2)}) %collective-permute-start.1) | collective-permute-done | bytes 393248 | tf_op jit(solution)/shard_map/ppermute | solution.py:283
  212.7 0.0 collective-permute-done.2.x3
  212.7 0.0 all-gather.3.cloned.1.call-done
  212.7 0.0 copy-done.10
  212.7 7.1 %shard_map.152 = (bf16[512,768]{1,0:T(8,128)(2,1)}, bf16[512,768]{1,0:T(8,128)(2,1)}) custom-call(s32[1]{0:T(128)} %bitcast.dp_ref, bf16[4,2,384,768]{3,2,1,0:T(8,128)(2,1)} %bitcast.30, bf16[512,384]{1,0:T(8,128)(2,1)S(1)} %copy-done.10, bf16[512,384]{1,0:T(8,128)(2,1)} %collective-permute-done.x1, bf16[512,384]{1,0:T(8,128)(2,1)} %collective-permute-done.1.x2, ...), custom_call_target="tpu_custom_call" | custom-call | flops 2516582400 | bytes 8388608 | tf_op jit(solution)/shard_map/pallas_call | solution.py:372
Async XLA Ops:
  7.2 0.7 copy-start.1
  7.8 1.0 copy-start.4
  11.2 53.0 %copy-start.8 = (bf16[192,192]{1,0:T(8,128)(2,1)S(1)}, bf16[192,192]{1,0:T(8,128)(2,1)}, u32[]{:S(2)}) copy-start(bf16[192,192]{1,0:T(8,128)(2,1)} %constant.14.clone.perm_ref) | copy-start | bytes 221188
  11.2 53.0 %all-to-all-start.1 = ((bf16[64,24,512]{2,1,0:T(8,128)(2,1)}), bf16[64,24,512]{2,1,0:T(8,128)(2,1)S(1)}, u32[]{:S(2)}, u32[]{:S(2)}) async-start(bf16[64,24,512]{2,1,0:T(8,128)(2,1)} %bitcast.26), calls=%async_computation.1 | async-start | bytes 3145728 | tf_op jit(solution)/shard_map/all_to_all | solution.py:273
  24.5 155.6 %all-gather.5.cloned.1.call-start = ((), (), s32[]{:S(2)}) async-start(), calls=%async_computation.4 | async-start | bytes 2949120 | tf_op jit(solution)/shard_map/all_gather | solution.py:277
  64.3 8.0 %copy-start.2 = (s32[128,2]{0,1:T(2,128)S(1)}, s32[128,2]{0,1:T(2,128)}, u32[]{:S(2)}) copy-start(s32[128,2]{0,1:T(2,128)} %param.14) | copy-start | bytes 3076
  64.3 8.0 %copy-start.3 = (bf16[128,2]{0,1:T(2,128)(2,1)S(1)}, bf16[128,2]{0,1:T(2,128)(2,1)}, u32[]{:S(2)}) copy-start(bf16[128,2]{0,1:T(2,128)(2,1)} %param.13) | copy-start | bytes 1540
  64.3 8.0 %copy-start.5 = (bf16[128,2048]{1,0:T(8,128)(2,1)S(1)}, bf16[128,2048]{1,0:T(8,128)(2,1)}, u32[]{:S(2)}) copy-start(bf16[128,2048]{1,0:T(8,128)(2,1)} %x_ref.2) | copy-start | bytes 1572868
  72.2 140.5 %all-gather.3.cloned.1.call-start = ((), (), s32[]{:S(2)}) async-start(), calls=%async_computation.3 | async-start | bytes 5898240 | tf_op jit(solution)/shard_map/all_gather | solution.py:277
  120.5 6.4 %copy-start.6 = (bf16[448,432]{1,0:T(8,128)(2,1)S(1)}, bf16[448,432]{1,0:T(8,128)(2,1)}, u32[]{:S(2)}) copy-start(bf16[448,432]{1,0:T(8,128)(2,1)} %constant.16.clone.mix_ref) | copy-start | bytes 1161220
  120.5 6.4 %copy-start.9 = (bf16[48,256]{1,0:T(8,128)(2,1)S(1)}, bf16[48,256]{1,0:T(8,128)(2,1)}, u32[]{:S(2)}) copy-start(bf16[48,256]{1,0:T(8,128)(2,1)} %constant.17.clone.mark_ref) | copy-start | bytes 73732
  135.1 45.0 %copy-start = (bf16[384,512]{1,0:T(8,128)(2,1)S(1)}, bf16[384,512]{1,0:T(8,128)(2,1)}, u32[]{:S(2)}) copy-start(bf16[384,512]{1,0:T(8,128)(2,1)} %get-tuple-element.35.s0) | copy-start | bytes 1179652
  135.1 51.6 %all-to-all-start.2 = ((bf16[64,56,256]{2,1,0:T(8,128)(2,1)}), bf16[64,56,256]{2,1,0:T(8,128)(2,1)S(1)}, u32[]{:S(2)}, u32[]{:S(2)}) async-start(bf16[64,56,256]{2,1,0:T(8,128)(2,1)} %bitcast.25), calls=%async_computation.2 | async-start | bytes 3670016 | tf_op jit(solution)/shard_map/all_to_all | solution.py:273
  141.3 21.0 %collective-permute-start.3 = (bf16[384,512]{1,0:T(8,128)(2,1)}, bf16[384,512]{1,0:T(8,128)(2,1)S(1)}, u32[]{:S(2)}, u32[]{:S(2)}) collective-permute-start(bf16[384,512]{1,0:T(8,128)(2,1)} %get-tuple-element.36), channel_id=1, source_target_pairs={{0,64},{64,128},{128,192},{192,0},{1,65},{65,129},{129,193},{193,1... | collective-permute-start | bytes 1179656 | tf_op jit(solution)/shard_map/ppermute | solution.py:283
  142.6 37.5 %collective-permute-start.4 = (bf16[384,512]{1,0:T(8,128)(2,1)}, bf16[384,512]{1,0:T(8,128)(2,1)S(1)}, u32[]{:S(2)}, u32[]{:S(2)}) collective-permute-start(bf16[384,512]{1,0:T(8,128)(2,1)} %get-tuple-element.37), channel_id=1, source_target_pairs={{0,128},{64,192},{128,0},{192,64},{1,129},{65,193},{129,1},{193,65... | collective-permute-start | bytes 1179656 | tf_op jit(solution)/shard_map/ppermute | solution.py:283
  145.1 35.0 %collective-permute-start.5 = (bf16[384,512]{1,0:T(8,128)(2,1)}, bf16[384,512]{1,0:T(8,128)(2,1)S(1)}, u32[]{:S(2)}, u32[]{:S(2)}) collective-permute-start(bf16[384,512]{1,0:T(8,128)(2,1)} %get-tuple-element.38), channel_id=1, source_target_pairs={{0,192},{64,0},{128,64},{192,128},{1,193},{65,1},{129,65},{193,129... | collective-permute-start | bytes 1179656 | tf_op jit(solution)/shard_map/ppermute | solution.py:283
  146.2 47.6 %collective-permute-start = (bf16[512,384]{1,0:T(8,128)(2,1)}, bf16[512,384]{1,0:T(8,128)(2,1)}, u32[]{:S(2)}, u32[]{:S(2)}) collective-permute-start(bf16[512,384]{1,0:T(8,128)(2,1)} %get-tuple-element.29), channel_id=1, source_target_pairs={{0,64},{64,128},{128,192},{192,0},{1,65},{65,129},{129,193},{193,1... | collective-permute-start | bytes 1179656 | tf_op jit(solution)/shard_map/ppermute | solution.py:283
  146.5 66.1 %collective-permute-start.1 = (bf16[512,384]{1,0:T(8,128)(2,1)}, bf16[512,384]{1,0:T(8,128)(2,1)}, u32[]{:S(2)}, u32[]{:S(2)}) collective-permute-start(bf16[512,384]{1,0:T(8,128)(2,1)} %get-tuple-element.30), channel_id=1, source_target_pairs={{0,128},{64,192},{128,0},{192,64},{1,129},{65,193},{129,1},{193,65... | collective-permute-start | bytes 1179656 | tf_op jit(solution)/shard_map/ppermute | solution.py:283
  162.3 50.3 %collective-permute-start.2 = (bf16[512,384]{1,0:T(8,128)(2,1)}, bf16[512,384]{1,0:T(8,128)(2,1)}, u32[]{:S(2)}, u32[]{:S(2)}) collective-permute-start(bf16[512,384]{1,0:T(8,128)(2,1)} %get-tuple-element.31), channel_id=1, source_target_pairs={{0,192},{64,0},{128,64},{192,128},{1,193},{65,1},{129,65},{193,129... | collective-permute-start | bytes 1179656 | tf_op jit(solution)/shard_map/ppermute | solution.py:283
  186.7 1.0 copy-start.7
  187.7 25.0 %copy-start.10 = (bf16[512,384]{1,0:T(8,128)(2,1)S(1)}, bf16[512,384]{1,0:T(8,128)(2,1)}, u32[]{:S(2)}) copy-start(bf16[512,384]{1,0:T(8,128)(2,1)} %get-tuple-element.28.x0) | copy-start | bytes 1179652
Sparse Core Ops, SparseCore 0:
  72.3 32.0 all-gather.4
  127.0 83.2 all-gather.2

commit v2 on v1

--- a/solution.py
+++ b/solution.py
@@ -130,16 +130,14 @@
             rows_ref[s, g * GROWS : (g + 1) * GROWS, :] = part[s * GROWS : (s + 1) * GROWS]
 
 
-def forward_kernel(
-    dp_ref, perm_ref, got_ref, gate_w, up_w, gate_ref, up_ref, hidden_t, x0, x1, x2, x3, rows
-):
-    @pl.when(pl.program_id(0) == 0)
-    def _():
-        unmix_rows(perm_ref, got_ref, rows)
-        for k, ref in enumerate((x0, x1, x2, x3)):
-            which = lax.rem(dp_ref[0] + k, DP)
-            ref[...] = rows[which].astype(F32).T.astype(BF16)
-
+def unmix_kernel(dp_ref, perm_ref, got_ref, rows, x0, x1, x2, x3):
+    unmix_rows(perm_ref, got_ref, rows)
+    for k, ref in enumerate((x0, x1, x2, x3)):
+        which = lax.rem(dp_ref[0] + k, DP)
+        ref[...] = rows[which].astype(F32).T.astype(BF16)
+
+
+def forward_kernel(rows, gate_w, up_w, gate_ref, up_ref, hidden_t):
     gate = sum(mm(rows[s], gate_w[s * SEG : (s + 1) * SEG, :]) for s in range(NSEG))
     up = sum(mm(rows[s], up_w[s * SEG : (s + 1) * SEG, :]) for s in range(NSEG))
     gate_ref[...] = gate
@@ -187,7 +185,9 @@
             out_ref[g * GROUP * BSPAN : (g + 1) * GROUP * BSPAN, :] = mm(mix, stacked).astype(BF16)
 
 
-def combine_kernel(ids_ref, prob_ref, perm_ref, got_ref, tok_ref, gprob_ref, rows, probs):
+def combine_kernel(
+    ids_ref, ids_t_ref, prob_ref, perm_ref, got_ref, tok_ref, gprob_ref, rows, probs
+):
     perm = perm_ref[...]
     for g in range(NGROUP):
         part = mm(perm, got_ref[g * GROUP * BSPAN : (g + 1) * GROUP * BSPAN, :])
@@ -196,49 +196,32 @@
                 s * GROWS : (s + 1) * GROWS
             ].astype(BF16)
         probs[g * GROUP : (g + 1) * GROUP, :] = part[NBSEG * GROWS : NBSEG * GROWS + GROUP]
-    places = places_in_rows(ids_ref)
-    at = [target * PER + slot for target, slot in places]
+    at = [target * PER + slot for target, slot in places_in_rows(ids_ref)]
     columns = iota((TOK, ROWS), 1)
     pick = jnp.where((columns == at[0]) | (columns == at[1]), 1.0, 0.0).astype(BF16)
     tok_ref[...] = mm(pick, rows[...]).astype(BF16)
-    home = probs[...].astype(BF16)
-    result = []
-    for k, (target, slot) in enumerate(places):
-        owner = (iota((TOK, N), 1) == target).astype(F32).astype(BF16)
-        line = mm(owner, home)
-        value = jnp.sum(jnp.where(iota((TOK, BSEG), 1) == slot, line, 0.0), axis=1, keepdims=True)
-        result.append(value / prob_ref[:, k : k + 1].astype(F32))
-    gprob_ref[...] = jnp.where(iota((TOK, 2), 1) == 0, result[0], result[1]).astype(BF16)
-
-
-def down_grad_kernel(dp_ref, hidden_t, s0, s1, s2, s3, out_ref, acc):
-    step = pl.program_id(0)
-    for k, ref in enumerate((s0, s1, s2, s3)):
-
-        @pl.when(step == k)
-        def _():
-            term = mm(hidden_t[0], ref[...])
-            acc[...] = term if k == 0 else acc[...] + term
-
-    @pl.when(step == DP - 1)
-    def _():
-        out_ref[...] = acc[...].astype(BF16)
-
-
-def gate_up_grad_kernel(dp_ref, back_ref, x0, x1, x2, x3, gate_out, up_out, acc):
-    step = pl.program_id(0)
-    for k, ref in enumerate((x0, x1, x2, x3)):
-
-        @pl.when(step == k)
-        def _():
-            for m in range(2):
-                term = mm(ref[...], back_ref[0, m])
-                acc[m] = term if k == 0 else acc[m] + term
-
-    @pl.when(step == DP - 1)
-    def _():
-        gate_out[...] = acc[0].astype(BF16)
-        up_out[...] = acc[1].astype(BF16)
+    home = probs[...][:, :TOK].T.astype(BF16)
+    for k, (target, slot) in enumerate(places_in_lanes(ids_t_ref)):
+        owner = (iota((N, TOK), 0) == target).astype(F32).astype(BF16)
+        line = mm(home, owner)
+        value = jnp.sum(jnp.where(iota((TOK, TOK), 0) == slot, line, 0.0), axis=0, keepdims=True)
+        gprob_ref[k : k + 1, :] = (value / prob_ref[k : k + 1, :].astype(F32)).astype(BF16)
+
+
+def down_grad_kernel(h0, h1, h3, h2_low, h2_high, s0, s1, s2, s3, out_ref):
+    acc = mm(h0[...], s0[...]) + mm(h1[...], s1[...]) + mm(h3[...], s3[...])
+    half = FF // 2
+    out_ref[:half] = (acc[:half] + mm(h2_low[...], s2[...])).astype(BF16)
+    out_ref[half:] = (acc[half:] + mm(h2_high[...], s2[...])).astype(BF16)
+
+
+def grad_first_kernel(b0, b1, b3, x0, x1, x3, acc):
+    acc[0] = mm(x0[...], b0[0]) + mm(x1[...], b1[0]) + mm(x3[...], b3[0])
+
+
+def grad_last_kernel(acc, gate_b, up_b, x2, gate_out, up_out):
+    gate_out[...] = (acc[0] + mm(x2[...], gate_b[0])).astype(BF16)
+    up_out[...] = (acc[1] + mm(x2[...], up_b[0])).astype(BF16)
 
 
 def shape(dims, kind=BF16):
@@ -273,15 +256,21 @@
     return lax.all_to_all(values, "expert", split_axis=0, concat_axis=0, tiled=True)
 
 
-def gather(values):
-    return lax.all_gather(values, "dp", axis=0, tiled=True)
+def shift(values, k):
+    return lax.ppermute(values, "dp", [(i, (i + k) % DP) for i in range(DP)])
 
 
 def spread(pieces):
-    moved = [pieces[0]]
-    for k in range(1, DP):
-        moved.append(lax.ppermute(pieces[k], "dp", [(i, (i + k) % DP) for i in range(DP)]))
-    return moved
+    return [pieces[0]] + [shift(pieces[k], k) for k in range(1, DP)]
+
+
+def around(values):
+    after = shift(values, 1)
+    before = shift(values, DP - 1)
+    half = values.shape[0] // 2
+    low = shift(after[:half], 1)
+    high = shift(before[half:], DP - 1)
+    return after, before, low, high
 
 
 def body(tokens, cotangent, gate_probs, expert_ids, gate_weight, up_weight, down_weight):
@@ -297,7 +286,7 @@
     send_x = call(
         send_tokens_kernel, (1,), [whole((2, TOK)), whole((TOK, D))],
         whole((N * SPAN, SEG)), shape((N * SPAN, SEG)), flops=800 << 20,
-    )(ids_t, tokens)
+    )(in_hbm(ids_t), in_hbm(tokens))
     got_x = exchange(send_x.reshape(N, SPAN, SEG)).reshape(N * SPAN, SEG)
     send_c = call(
         send_scaled_kernel, (1,),
@@ -306,11 +295,18 @@
     )(ids_t, probs_t, cotangent)
     got_c = exchange(send_c.reshape(N, SPAN, SEG)).reshape(N * SPAN, SEG)
 
-    gate, up, hidden_t, *x_pieces = call(
+    rows, *x_pieces = call(
+        unmix_kernel, (1,),
+        [whole(UNMIX.shape), whole((N * SPAN, SEG))],
+        [whole((NSEG, ROWS, SEG))] + [whole((SEG, ROWS))] * DP,
+        [shape((NSEG, ROWS, SEG))] + [shape((SEG, ROWS))] * DP,
+        scalars=1, flops=300 << 20,
+    )(dp, unmix, got_x)
+    x_pieces = spread(x_pieces)
+    gate, up, hidden_t = call(
         forward_kernel, (NFB,),
         [
-            whole(UNMIX.shape),
-            whole((N * SPAN, SEG)),
+            whole((NSEG, ROWS, SEG)),
             pl.BlockSpec((D, FB), lambda i, *_: (0, i)),
             pl.BlockSpec((D, FB), lambda i, *_: (0, i)),
         ],
@@ -318,14 +314,11 @@
             pl.BlockSpec((ROWS, FB), lambda i, *_: (0, i)),
             pl.BlockSpec((ROWS, FB), lambda i, *_: (0, i)),
             pl.BlockSpec((FB, ROWS), lambda i, *_: (i, 0)),
-        ]
-        + [whole((SEG, ROWS))] * DP,
-        [shape((ROWS, FF), F32), shape((ROWS, FF), F32), shape((FF, ROWS))]
-        + [shape((SEG, ROWS))] * DP,
-        scratch=[pltpu.VMEM((NSEG, ROWS, SEG), BF16)], scalars=1, flops=3000 << 20,
-    )(dp, unmix, got_x, gate_w, up_w)
-    x_pieces = spread(x_pieces)
-    hidden_all = gather(hidden_t).reshape(DP, FF, ROWS)
+        ],
+        [shape((ROWS, FF), F32), shape((ROWS, FF), F32), shape((FF, ROWS))],
+        flops=3000 << 20,
+    )(in_hbm(rows), gate_w, up_w)
+    h1, h3, h_low, h_high = around(hidden_t)
 
     back, q, *s_pieces = call(
         backward_kernel, (NFB,),
@@ -341,8 +334,7 @@
         [shape((2, ROWS, FF)), shape((ROWS, 128), F32)] + [shape((ROWS, SEG))] * DP,
         scratch=[pltpu.VMEM((NSEG, ROWS, SEG), BF16)], scalars=1, flops=2000 << 20,
     )(dp, unmix, got_c, down_w, in_hbm(gate), in_hbm(up))
-    back_all = gather(back.reshape(2 * ROWS, FF))
-    back_all = back_all.reshape(DP, 2, ROWS, FF)
+    b1, b3, b_low, b_high = around(back)
     s_pieces = spread(s_pieces)
 
     send_b = call(
@@ -360,29 +352,41 @@
     )(mix, mark, in_hbm(back), in_hbm(q), gate_w, up_w)
     got_b = exchange(send_b.reshape(N, BSPAN, BSEG)).reshape(N * BSPAN, BSEG)
 
-    def other(i, dp_ref):
-        return lax.rem(dp_ref[0] - i + DP, DP)
-
     grad_down = call(
-        down_grad_kernel, (DP,),
-        [pl.BlockSpec((1, FF, ROWS), lambda i, r: (other(i, r), 0, 0))] + [whole((ROWS, SEG))] * DP,
-        whole((FF, SEG)), shape((FF, SEG)),
-        scratch=[pltpu.VMEM((FF, SEG), F32)], scalars=1, flops=1200 << 20,
-    )(dp, in_hbm(hidden_all), *s_pieces)
+        down_grad_kernel, (1,),
+        [whole((FF, ROWS))] * 3 + [whole((FF // 2, ROWS))] * 2 + [whole((ROWS, SEG))] * DP,
+        whole((FF, SEG)), shape((FF, SEG)), flops=1200 << 20,
+    )(hidden_t, h1, h3, h_low, h_high, *s_pieces)
+    acc = call(
+        grad_first_kernel, (2,),
+        [pl.BlockSpec((1, ROWS, FF), lambda i: (i, 0, 0))] * 3 + [whole((SEG, ROWS))] * 3,
+        pl.BlockSpec((1, SEG, FF), lambda i: (i, 0, 0)), shape((2, SEG, FF), F32),
+        flops=1800 << 20,
+    )(back, b1, b3, x_pieces[0], x_pieces[1], x_pieces[3])
     grad_gate, grad_up = call(
-        gate_up_grad_kernel, (DP,),
-        [pl.BlockSpec((1, 2, ROWS, FF), lambda i, r: (other(i, r), 0, 0, 0))]
-        + [whole((SEG, ROWS))] * DP,
-        [whole((SEG, FF))] * 2, [shape((SEG, FF))] * 2,
-        scratch=[pltpu.VMEM((2, SEG, FF), F32)], scalars=1, flops=2400 << 20,
-    )(dp, in_hbm(back_all), *x_pieces)
+        grad_last_kernel, (NFB,),
+        [
+            pl.BlockSpec((2, SEG, FB), lambda i: (0, 0, i)),
+            pl.BlockSpec((1, ROWS, FB), lambda i: (0, 0, i)),
+            pl.BlockSpec((1, ROWS, FB), lambda i: (0, 0, i)),
+            whole((SEG, ROWS)),
+        ],
+        [pl.BlockSpec((SEG, FB), lambda i: (0, i))] * 2, [shape((SEG, FF))] * 2,
+        flops=600 << 20,
+    )(in_hbm(acc), b_low, b_high, x_pieces[2])
     grad_tokens, grad_probs = call(
         combine_kernel, (1,),
-        [whole((TOK, 2)), whole((TOK, 2)), whole(BACK.shape), whole((N * BSPAN, BSEG))],
-        [whole((TOK, D)), whole((TOK, 2))], [shape((TOK, D)), shape((TOK, 2))],
+        [
+            whole((TOK, 2)),
+            whole((2, TOK)),
+            whole((2, TOK)),
+            whole(BACK.shape),
+            whole((N * BSPAN, BSEG)),
+        ],
+        [whole((TOK, D)), whole((2, TOK))], [shape((TOK, D)), shape((2, TOK))],
         scratch=[pltpu.VMEM((ROWS, D), BF16), pltpu.VMEM((N, BSEG), F32)], flops=1000 << 20,
-    )(expert_ids, gate_probs, back_perm, got_b)
-    return grad_tokens, grad_probs, grad_gate[None], grad_up[None], grad_down[None]
+    )(expert_ids, ids_t, probs_t, in_hbm(back_perm), got_b)
+    return grad_tokens, grad_probs.T, grad_gate[None], grad_up[None], grad_down[None]
 
 
 def solution(mesh):

time: 227 us -> 231 us (1.018)
  blocking collectives: 45.9 us -> 0 us
  waiting for transfers between devices: 93.7 us -> 127 us
  starting transfers between devices: 27 us -> 40.9 us
  between operations: 14.1 us -> 0.79 us
  local copies, waits for them, and re-layouts: 4.34 us -> 12.1 us
  Pallas kernels: 41.6 us -> 47.8 us
    all_to_all x1 -> x0, blocking collectives: 45.9 us -> none  [exchange(): lax.all_to_all(values, 'expert', split_axis=0, concat_axis=0, tiled=True)]
    all_to_all x2 -> x3, waiting for transfers between devices: 41.5 us -> 67.6 us  [exchange(): lax.all_to_all(values, 'expert', split_axis=0, concat_axis=0, tiled=True)]
    ppermute x6 -> x14, starting transfers between devices: 7.38 us -> 15.1 us  [shift(): return lax.ppermute(values, 'dp', [(i, (i + k) % DP) for i in range(DP)])]
    ppermute x6 -> x14, waiting for transfers between devices: 52.3 us -> 59.2 us  [shift(): return lax.ppermute(values, 'dp', [(i, (i + k) % DP) for i in range(DP)])]
    all_to_all x2 -> x3, starting transfers between devices: 19.5 us -> 25.8 us  [exchange(): lax.all_to_all(values, 'expert', split_axis=0, concat_axis=0, tiled=True)]
    unnamed x25 -> x39, local copies, waits for them, and re-layouts: 4.34 us -> 10.3 us
    pallas_call x4 -> x6, Pallas kernels: 22.4 us -> 27.6 us  [the longest x1 6.9 us: body(): call(forward_kernel, (NFB,), [whole((NSEG, ROWS, SEG)), pl.BlockSpec((D,...]
  transfers between devices with their start and end apart: 10 -> 17, of which waited for: 6 -> 9; matrix products, arithmetic and copies ran while one was open for 1% -> 1% of each run, Pallas kernels for 11% -> 11%
where the time goes in v2:
time: 231 us; the launch traced here: 228 us
  waiting for transfers between devices  127 us (55%)
  Pallas kernels  47.8 us (21%)
  starting transfers between devices  40.9 us (18%)
  local copies, waits for them, and re-layouts  12.1 us (5%)
    all_to_all x3, waiting for transfers between devices, exchange(): lax.all_to_all(values, 'expert', split_axis=0, concat_axis=0, tiled=True)  67.6 us
    ppermute x14, waiting for transfers between devices, shift(): return lax.ppermute(values, 'dp', [(i, (i + k) % DP) for i in range(DP)])  59.2 us
    all_to_all x3, starting transfers between devices, exchange(): lax.all_to_all(values, 'expert', split_axis=0, concat_axis=0, tiled=True)  25.8 us
    ppermute x14, starting transfers between devices, shift(): return lax.ppermute(values, 'dp', [(i, (i + k) % DP) for i in range(DP)])  15.1 us
    unnamed x39, local copies, waits for them, and re-layouts  10.3 us
    pallas_call x1, Pallas kernels, body(): call(return_kernel, (NSEG,), [whole(MIX.shape), whole(MARK.shape), whole(...  8.09 us
    pallas_call x1, Pallas kernels, body(): call(forward_kernel, (NFB,), [whole((NSEG, ROWS, SEG)), pl.BlockSpec((D,...  6.9 us
    pallas_call x1, Pallas kernels, body(): call(backward_kernel, (NFB,), [whole(UNMIX.shape), whole((N * SPAN, SEG))...  6.41 us
  transfers between devices with their start and end apart: 17, of which 9 were waited for; matrix products, arithmetic and copies ran while one was open for 1% of the time, Pallas kernels for 11%

profile of v2, /device:TPU:1, one launch (start us, length us, event | category | flops | bytes accessed | tf_op | source)
XLA Modules:
  0.0 228.4 jit_solution(14205369619632353479)
XLA Ops:
  0.6 3.4 %shard_map.147 = bf16[1536,512]{1,0:T(8,128)(2,1)} custom-call(s32[2,128]{1,0:T(2,128)} %bitcast.18, bf16[128,2048]{1,0:T(8,128)(2,1)} %x_ref.3), custom_call_target="tpu_custom_call" | custom-call | flops 838860800 | bytes 8388608 | tf_op jit(solution)/shard_map/pallas_call | solution.py:286
  4.0 13.3 %all-to-all-start.1 = ((bf16[64,24,512]{2,1,0:T(8,128)(2,1)}), bf16[64,24,512]{2,1,0:T(8,128)(2,1)S(1)}, u32[]{:S(2)}, u32[]{:S(2)}) async-start(bf16[64,24,512]{2,1,0:T(8,128)(2,1)} %bitcast.25), calls=%async_computation.1 | async-start | bytes 3145728 | tf_op jit(solution)/shard_map/all_to_all | solution.py:256
  17.3 0.0 copy-done.14
  17.3 0.0 copy-done.15
  17.3 0.0 copy-done.16
  17.3 2.3 %shard_map.146 = bf16[1536,512]{1,0:T(8,128)(2,1)} custom-call(s32[2,128]{1,0:T(2,128)S(1)} %bitcast.19, bf16[2,128]{1,0:T(2,128)(2,1)S(1)} %bitcast.21, bf16[128,2048]{1,0:T(8,128)(2,1)S(1)} %copy-done.15), custom_call_target="tpu_custom_call" | custom-call | flops 838860800 | bytes 8388608 | tf_op jit(solution)/shard_map/pallas_call | solution.py:291
  19.6 37.4 %all-to-all-done.1 = bf16[64,24,512]{2,1,0:T(8,128)(2,1)S(1)} async-done(((bf16[64,24,512]{2,1,0:T(8,128)(2,1)}), bf16[64,24,512]{2,1,0:T(8,128)(2,1)S(1)}, u32[]{:S(2)}, u32[]{:S(2)}) %all-to-all-start.1) | async-done | bytes 1572896 | tf_op jit(solution)/shard_map/all_to_all | solution.py:256
  57.0 6.2 %all-to-all-start = ((bf16[64,24,512]{2,1,0:T(8,128)(2,1)}), bf16[64,24,512]{2,1,0:T(8,128)(2,1)S(1)}, u32[]{:S(2)}, u32[]{:S(2)}) async-start(bf16[64,24,512]{2,1,0:T(8,128)(2,1)} %bitcast.24), calls=%async_computation | async-start | bytes 3145728 | tf_op jit(solution)/shard_map/all_to_all | solution.py:256
  63.3 0.0 copy-done.12
  63.3 2.6 %shard_map.148 = (bf16[4,384,512]{2,1,0:T(8,128)(2,1)}, bf16[512,384]{1,0:T(8,128)(2,1)}, bf16[512,384]{1,0:T(8,128)(2,1)}, bf16[512,384]{1,0:T(8,128)(2,1)}, bf16[512,384]{1,0:T(8,128)(2,1)}) custom-call(s32[1]{0:T(128)} %bitcast.2.dp_ref, bf16[192,192]{1,0:T(8,128)(2,1)S(1)} %copy-done.12, bf16[1536,512]{1,0:T(8,128)(2,1)S(1)} %bitcast.16), custom_call_target="tpu_custom_call" | custom-call | flops 314572800 | bytes 8388608 | tf_op jit(solution)/shard_map/pallas_call | solution.py:298
  65.9 6.9 %shard_map.149 = (f32[384,768]{1,0:T(8,128)}, f32[384,768]{1,0:T(8,128)}, bf16[768,384]{1,0:T(8,128)(2,1)}) custom-call(bf16[4,384,512]{2,1,0:T(8,128)(2,1)} %get-tuple-element.23.rows, bf16[2048,768]{1,0:T(8,128)(2,1)} %bitcast.28, bf16[2048,768]{1,0:T(8,128)(2,1)} %bitcast.30), custom_call_target="tpu_custom_call" | custom-call | flops 3145728000 | bytes 8388608 | tf_op jit(solution)/shard_map/pallas_call | solution.py:306
  72.8 30.2 %all-to-all-done = bf16[64,24,512]{2,1,0:T(8,128)(2,1)S(1)} async-done(((bf16[64,24,512]{2,1,0:T(8,128)(2,1)}), bf16[64,24,512]{2,1,0:T(8,128)(2,1)S(1)}, u32[]{:S(2)}, u32[]{:S(2)}) %all-to-all-start) | async-done | bytes 1572896 | tf_op jit(solution)/shard_map/all_to_all | solution.py:256
  103.0 6.4 %shard_map.150 = (bf16[2,384,768]{2,1,0:T(8,128)(2,1)}, f32[384,128]{1,0:T(8,128)}, bf16[384,512]{1,0:T(8,128)(2,1)}, bf16[384,512]{1,0:T(8,128)(2,1)}, bf16[384...) custom-call(s32[1]{0:T(128)} %bitcast.2.dp_ref, bf16[192,192]{1,0:T(8,128)(2,1)S(1)} %copy-done.12, ...), custom_call_target="tpu_custom_call" | custom-call | flops 2097152000 | bytes 8388608 | tf_op jit(solution)/shard_map/pallas_call | solution.py:323
  109.5 0.0 copy-done.17
  109.5 8.1 %shard_map.151 = bf16[3584,256]{1,0:T(8,128)(2,1)} custom-call(bf16[448,432]{1,0:T(8,128)(2,1)S(1)} %copy-done.17, bf16[48,256]{1,0:T(8,128)(2,1)S(1)} %copy-done.18, bf16[2,384,768]{2,1,0:T(8,128)(2,1)} %get-tuple-element.26.back_ref.b0, f32[384,128]{1,0:T(8,128)} %get-tuple-element.27.q_ref, bf16[2048,768]{1,0:T(8,128)(2,1)} %bitcast.29, ...), custom_call_target="tpu_custom_call" | custom-call | flops 3145728000 | bytes 8388608 | tf_op jit(solution)/shard_map/pallas_call | solution.py:340
  117.6 6.3 %all-to-all-start.2 = ((bf16[64,56,256]{2,1,0:T(8,128)(2,1)}), bf16[64,56,256]{2,1,0:T(8,128)(2,1)}, u32[]{:S(2)}, u32[]{:S(2)}) async-start(bf16[64,56,256]{2,1,0:T(8,128)(2,1)} %bitcast.23), calls=%async_computation.2 | async-start | bytes 3670016 | tf_op jit(solution)/shard_map/all_to_all | solution.py:256
  123.8 1.3 collective-permute-start
  125.1 1.5 collective-permute-start.1
  126.6 1.3 collective-permute-start.8
  127.8 0.2 collective-permute-start.7
  128.0 0.0 collective-permute-start.11
  128.1 36.7 %collective-permute-done.8.h3 = bf16[768,384]{1,0:T(8,128)(2,1)S(1)} collective-permute-done((bf16[768,384]{1,0:T(8,128)(2,1)}, bf16[768,384]{1,0:T(8,128)(2,1)S(1)}, u32[]{:S(2)}, u32[]{:S(2)}) %collective-permute-start.8) | collective-permute-done | bytes 589856 | tf_op jit(solution)/shard_map/ppermute | solution.py:260
  164.8 2.5 %collective-permute-start.12 = (bf16[384,512]{1,0:T(8,128)(2,1)}, bf16[384,512]{1,0:T(8,128)(2,1)S(1)}, u32[]{:S(2)}, u32[]{:S(2)}) collective-permute-start(bf16[384,512]{1,0:T(8,128)(2,1)} %get-tuple-element.39), channel_id=1, source_target_pairs={{0,128},{64,192},{128,0},{192,64},{1,129},{65,193},{129,1},{193,65... | collective-permute-start | bytes 1179656 | tf_op jit(solution)/shard_map/ppermute | solution.py:260
  167.2 0.0 collective-permute-done.7.h1
  167.2 1.1 collective-permute-start.13
  168.4 0.0 collective-permute-done.b1
  168.4 0.1 collective-permute-start.10
  168.6 0.0 collective-permute-done.1.b3
  168.6 1.5 collective-permute-start.9
  170.1 0.9 slice.16
  170.9 0.9 slice.17
  171.9 1.5 collective-permute-done.11.s1
  173.4 0.8 copy-done.1
  174.1 0.0 collective-permute-start.4
  174.1 8.7 %collective-permute-done.12.s2 = bf16[384,512]{1,0:T(8,128)(2,1)S(1)} collective-permute-done((bf16[384,512]{1,0:T(8,128)(2,1)}, bf16[384,512]{1,0:T(8,128)(2,1)S(1)}, u32[]{:S(2)}, u32[]{:S(2)}) %collective-permute-start.12) | collective-permute-done | bytes 393248 | tf_op jit(solution)/shard_map/ppermute | solution.py:260
  182.8 0.7 copy-done.3
  183.6 0.0 collective-permute-start.5
  183.6 1.7 collective-permute-done.13.s3
  185.3 0.7 copy-done.5
  186.1 1.8 collective-permute-start.2
  187.9 3.6 %collective-permute-done.10.h2_high = bf16[384,384]{1,0:T(8,128)(2,1)S(1)} collective-permute-done((bf16[384,384]{1,0:T(8,128)(2,1)S(1)}, bf16[384,384]{1,0:T(8,128)(2,1)S(1)}, u32[]{:S(2)}, u32[]{:S(2)}) %collective-permute-start.10) | collective-permute-done | bytes 294944 | tf_op jit(solution)/shard_map/ppermute | solution.py:260
  191.6 0.7 copy-done.8
  192.3 3.4 %collective-permute-start.3 = (bf16[512,384]{1,0:T(8,128)(2,1)}, bf16[512,384]{1,0:T(8,128)(2,1)}, u32[]{:S(2)}, u32[]{:S(2)}) collective-permute-start(bf16[512,384]{1,0:T(8,128)(2,1)} %get-tuple-element.32), channel_id=1, source_target_pairs={{0,192},{64,0},{128,64},{192,128},{1,193},{65,1},{129,65},{193,129... | collective-permute-start | bytes 1179656 | tf_op jit(solution)/shard_map/ppermute | solution.py:260
  195.7 0.0 collective-permute-done.9.h2_low
  195.7 0.7 copy-done.10
  196.4 0.4 collective-permute-start.6
  196.8 0.7 copy.16.ids_ref
  197.5 1.0 copy-done
  198.5 1.0 copy-done.2
  199.5 1.0 copy-done.4
  200.5 1.0 copy-done.6
  201.5 1.0 copy-done.9
  202.5 1.0 copy-done.11
  203.4 3.8 %shard_map.155 = bf16[768,512]{1,0:T(8,128)(2,1)} custom-call(bf16[768,384]{1,0:T(8,128)(2,1)} %get-tuple-element.36.h0, bf16[768,384]{1,0:T(8,128)(2,1)S(1)} %collective-permute-done.7.h1, bf16[768,384]{1,0:T(8,128)(2,1)S(1)} %collective-permute-done.8.h3, bf16[384,384]{1,0:T(8,128)(2,1)S(1)} %copy-done.11, bf16[384,384]{1,0:T(8,128)(2,1)S(1)} %copy-done.9, ...), custom_call_target="tpu_custom_call" | custom-call | flops 1258291200 | bytes 8388608 | tf_op jit(solution)/shard_map/pallas_call | solution.py:355
  207.2 2.1 collective-permute-done.2.x1
  209.3 4.8 %collective-permute-done.3.x3 = bf16[512,384]{1,0:T(8,128)(2,1)} collective-permute-done((bf16[512,384]{1,0:T(8,128)(2,1)}, bf16[512,384]{1,0:T(8,128)(2,1)}, u32[]{:S(2)}, u32[]{:S(2)}) %collective-permute-start.3) | collective-permute-done | bytes 393248 | tf_op jit(solution)/shard_map/ppermute | solution.py:260
  214.1 0.0 copy-done.7
  214.1 5.2 %shard_map.153.acc = f32[2,512,768]{2,1,0:T(8,128)} custom-call(bf16[2,384,768]{2,1,0:T(8,128)(2,1)} %get-tuple-element.26.back_ref.b0, bf16[2,384,768]{2,1,0:T(8,128)(2,1)S(1)} %collective-permute-done.b1, bf16[2,384,768]{2,1,0:T(8,128)(2,1)S(1)} %collective-permute-done.1.b3, bf16[512,384]{1,0:T(8,128)(2,1)S(1)} %copy-done.7, ...), custom_call_target="tpu_custom_call" | custom-call | flops 1887436800 | bytes 8388608 | tf_op jit(solution)/shard_map/pallas_call | solution.py:360
  219.3 0.0 collective-permute-done.6.x2
  219.3 0.0 collective-permute-done.4.gate_b
  219.4 0.0 collective-permute-done.5.up_b
  219.4 5.0 %shard_map.154 = (bf16[512,768]{1,0:T(8,128)(2,1)}, bf16[512,768]{1,0:T(8,128)(2,1)}) custom-call(f32[2,512,768]{2,1,0:T(8,128)} %shard_map.153.acc, bf16[1,384,768]{2,1,0:T(8,128)(2,1)} %collective-permute-done.4.gate_b, bf16[1,384,768]{2,1,0:T(8,128)(2,1)} %collective-permute-done.5.up_b, bf16[512,384]{1,0:T(8,128)(2,1)} %collective-permute-done.6.x2), custom_call_target="tpu_custom_call" | custom-call | flops 629145600 | bytes 8388608 | tf_op jit(solution)/shard_map/pallas_call | solution.py:366
  224.4 0.0 all-to-all-done.2
  224.4 4.1 %shard_map.152 = (bf16[128,2048]{1,0:T(8,128)(2,1)}, bf16[2,128]{1,0:T(2,128)(2,1)}) custom-call(s32[128,2]{1,0:T(8,128)S(1)} %copy-done.13, s32[2,128]{1,0:T(2,128)S(1)} %bitcast.20, bf16[2,128]{1,0:T(2,128)(2,1)S(1)} %bitcast.22, bf16[400,448]{1,0:T(8,128)(2,1)} %constant.15.clone.perm_ref, bf16[3584,256]{1,0:T(8,128)(2,1)} %bitcast.11.got_ref), custom_call_target="tpu_custom_call" | custom-call | flops 1048576000 | bytes 8388608 | tf_op jit(solution)/shard_map/pallas_call | solution.py:377
  (23 shorter events, 0.1 us)
Async XLA Ops:
  4.0 13.3 %copy-start.14 = (s32[128,2]{0,1:T(2,128)S(1)}, s32[128,2]{0,1:T(2,128)}, u32[]{:S(2)}) copy-start(s32[128,2]{0,1:T(2,128)} %param.14) | copy-start | bytes 3076
  4.0 13.3 %copy-start.15 = (bf16[128,2048]{1,0:T(8,128)(2,1)S(1)}, bf16[128,2048]{1,0:T(8,128)(2,1)}, u32[]{:S(2)}) copy-start(bf16[128,2048]{1,0:T(8,128)(2,1)} %x_ref.2) | copy-start | bytes 1572868
  4.0 13.3 %copy-start.16 = (bf16[128,2]{0,1:T(2,128)(2,1)S(1)}, bf16[128,2]{0,1:T(2,128)(2,1)}, u32[]{:S(2)}) copy-start(bf16[128,2]{0,1:T(2,128)(2,1)} %param.13) | copy-start | bytes 1540
  4.0 53.0 %all-to-all-start.1 = ((bf16[64,24,512]{2,1,0:T(8,128)(2,1)}), bf16[64,24,512]{2,1,0:T(8,128)(2,1)S(1)}, u32[]{:S(2)}, u32[]{:S(2)}) async-start(bf16[64,24,512]{2,1,0:T(8,128)(2,1)} %bitcast.25), calls=%async_computation.1 | async-start | bytes 3145728 | tf_op jit(solution)/shard_map/all_to_all | solution.py:256
  57.0 6.2 %copy-start.12 = (bf16[192,192]{1,0:T(8,128)(2,1)S(1)}, bf16[192,192]{1,0:T(8,128)(2,1)}, u32[]{:S(2)}) copy-start(bf16[192,192]{1,0:T(8,128)(2,1)} %constant.14.clone.perm_ref) | copy-start | bytes 221188
  57.0 46.0 %all-to-all-start = ((bf16[64,24,512]{2,1,0:T(8,128)(2,1)}), bf16[64,24,512]{2,1,0:T(8,128)(2,1)S(1)}, u32[]{:S(2)}, u32[]{:S(2)}) async-start(bf16[64,24,512]{2,1,0:T(8,128)(2,1)} %bitcast.24), calls=%async_computation | async-start | bytes 3145728 | tf_op jit(solution)/shard_map/all_to_all | solution.py:256
  103.0 6.4 %copy-start.17 = (bf16[448,432]{1,0:T(8,128)(2,1)S(1)}, bf16[448,432]{1,0:T(8,128)(2,1)}, u32[]{:S(2)}) copy-start(bf16[448,432]{1,0:T(8,128)(2,1)} %constant.16.clone.mix_ref) | copy-start | bytes 1161220
  103.0 6.4 %copy-start.18 = (bf16[48,256]{1,0:T(8,128)(2,1)S(1)}, bf16[48,256]{1,0:T(8,128)(2,1)}, u32[]{:S(2)}) copy-start(bf16[48,256]{1,0:T(8,128)(2,1)} %constant.17.clone.mark_ref) | copy-start | bytes 73732
  117.6 106.8 %all-to-all-start.2 = ((bf16[64,56,256]{2,1,0:T(8,128)(2,1)}), bf16[64,56,256]{2,1,0:T(8,128)(2,1)}, u32[]{:S(2)}, u32[]{:S(2)}) async-start(bf16[64,56,256]{2,1,0:T(8,128)(2,1)} %bitcast.23), calls=%async_computation.2 | async-start | bytes 3670016 | tf_op jit(solution)/shard_map/all_to_all | solution.py:256
  123.8 44.6 %collective-permute-start = (bf16[2,384,768]{2,1,0:T(8,128)(2,1)}, bf16[2,384,768]{2,1,0:T(8,128)(2,1)S(1)}, u32[]{:S(2)}, u32[]{:S(2)}) collective-permute-start(bf16[2,384,768]{2,1,0:T(8,128)(2,1)} %get-tuple-element.26.back_ref.b0), channel_id=1, source_target_pairs={{0,64},{64,128},{128,192},{192,0},{1,65},{65,129},{129,193},{193,1... | collective-permute-start | bytes 3538952 | tf_op jit(solution)/shard_map/ppermute | solution.py:260
  125.1 43.5 %collective-permute-start.1 = (bf16[2,384,768]{2,1,0:T(8,128)(2,1)}, bf16[2,384,768]{2,1,0:T(8,128)(2,1)S(1)}, u32[]{:S(2)}, u32[]{:S(2)}) collective-permute-start(bf16[2,384,768]{2,1,0:T(8,128)(2,1)} %get-tuple-element.26.back_ref.b0), channel_id=1, source_target_pairs={{0,192},{64,0},{128,64},{192,128},{1,193},{65,1},{129,65},{193,129... | collective-permute-start | bytes 3538952 | tf_op jit(solution)/shard_map/ppermute | solution.py:260
  126.6 38.2 %collective-permute-start.8 = (bf16[768,384]{1,0:T(8,128)(2,1)}, bf16[768,384]{1,0:T(8,128)(2,1)S(1)}, u32[]{:S(2)}, u32[]{:S(2)}) collective-permute-start(bf16[768,384]{1,0:T(8,128)(2,1)} %get-tuple-element.36.h0), channel_id=1, source_target_pairs={{0,192},{64,0},{128,64},{192,128},{1,193},{65,1},{129,65},{193,129... | collective-permute-start | bytes 1769480 | tf_op jit(solution)/shard_map/ppermute | solution.py:260
  127.8 39.4 %collective-permute-start.7 = (bf16[768,384]{1,0:T(8,128)(2,1)}, bf16[768,384]{1,0:T(8,128)(2,1)S(1)}, u32[]{:S(2)}, u32[]{:S(2)}) collective-permute-start(bf16[768,384]{1,0:T(8,128)(2,1)} %get-tuple-element.36.h0), channel_id=1, source_target_pairs={{0,64},{64,128},{128,192},{192,0},{1,65},{65,129},{129,193},{193,1... | collective-permute-start | bytes 1769480 | tf_op jit(solution)/shard_map/ppermute | solution.py:260
  128.0 45.3 %collective-permute-start.11 = (bf16[384,512]{1,0:T(8,128)(2,1)}, bf16[384,512]{1,0:T(8,128)(2,1)S(1)}, u32[]{:S(2)}, u32[]{:S(2)}) collective-permute-start(bf16[384,512]{1,0:T(8,128)(2,1)} %get-tuple-element.38), channel_id=1, source_target_pairs={{0,64},{64,128},{128,192},{192,0},{1,65},{65,129},{129,193},{193,1... | collective-permute-start | bytes 1179656 | tf_op jit(solution)/shard_map/ppermute | solution.py:260
  164.8 18.1 %collective-permute-start.12 = (bf16[384,512]{1,0:T(8,128)(2,1)}, bf16[384,512]{1,0:T(8,128)(2,1)S(1)}, u32[]{:S(2)}, u32[]{:S(2)}) collective-permute-start(bf16[384,512]{1,0:T(8,128)(2,1)} %get-tuple-element.39), channel_id=1, source_target_pairs={{0,128},{64,192},{128,0},{192,64},{1,129},{65,193},{129,1},{193,65... | collective-permute-start | bytes 1179656 | tf_op jit(solution)/shard_map/ppermute | solution.py:260
  167.2 18.1 %collective-permute-start.13 = (bf16[384,512]{1,0:T(8,128)(2,1)}, bf16[384,512]{1,0:T(8,128)(2,1)S(1)}, u32[]{:S(2)}, u32[]{:S(2)}) collective-permute-start(bf16[384,512]{1,0:T(8,128)(2,1)} %get-tuple-element.40), channel_id=1, source_target_pairs={{0,192},{64,0},{128,64},{192,128},{1,193},{65,1},{129,65},{193,129... | collective-permute-start | bytes 1179656 | tf_op jit(solution)/shard_map/ppermute | solution.py:260
  168.4 23.1 %collective-permute-start.10 = (bf16[384,384]{1,0:T(8,128)(2,1)S(1)}, bf16[384,384]{1,0:T(8,128)(2,1)S(1)}, u32[]{:S(2)}, u32[]{:S(2)}) collective-permute-start(bf16[384,384]{1,0:T(8,128)(2,1)S(1)} %slice.19), channel_id=1, source_target_pairs={{0,192},{64,0},{128,64},{192,128},{1,193},{65,1},{129,65},{193,129... | collective-permute-start | bytes 884744 | tf_op jit(solution)/shard_map/ppermute | solution.py:260
  168.6 27.1 %collective-permute-start.9 = (bf16[384,384]{1,0:T(8,128)(2,1)S(1)}, bf16[384,384]{1,0:T(8,128)(2,1)S(1)}, u32[]{:S(2)}, u32[]{:S(2)}) collective-permute-start(bf16[384,384]{1,0:T(8,128)(2,1)S(1)} %slice.18), channel_id=1, source_target_pairs={{0,64},{64,128},{128,192},{192,0},{1,65},{65,129},{129,193},{193,1... | collective-permute-start | bytes 884744 | tf_op jit(solution)/shard_map/ppermute | solution.py:260
  173.4 0.8 copy-start.1
  174.1 45.2 %collective-permute-start.4 = (bf16[1,384,768]{2,1,0:T(8,128)(2,1)}, bf16[1,384,768]{2,1,0:T(8,128)(2,1)}, u32[]{:S(2)}, u32[]{:S(2)}) collective-permute-start(bf16[1,384,768]{2,1,0:T(8,128)(2,1)} %slice.16), channel_id=1, source_target_pairs={{0,64},{64,128},{128,192},{192,0},{1,65},{65,129},{129,193},{193,1... | collective-permute-start | bytes 1769480 | tf_op jit(solution)/shard_map/ppermute | solution.py:260
  182.8 0.7 copy-start.3
  183.6 35.8 %collective-permute-start.5 = (bf16[1,384,768]{2,1,0:T(8,128)(2,1)}, bf16[1,384,768]{2,1,0:T(8,128)(2,1)}, u32[]{:S(2)}, u32[]{:S(2)}) collective-permute-start(bf16[1,384,768]{2,1,0:T(8,128)(2,1)} %slice.17), channel_id=1, source_target_pairs={{0,192},{64,0},{128,64},{192,128},{1,193},{65,1},{129,65},{193,129... | collective-permute-start | bytes 1769480 | tf_op jit(solution)/shard_map/ppermute | solution.py:260
  185.3 0.7 copy-start.5
  186.1 23.2 %collective-permute-start.2 = (bf16[512,384]{1,0:T(8,128)(2,1)}, bf16[512,384]{1,0:T(8,128)(2,1)}, u32[]{:S(2)}, u32[]{:S(2)}) collective-permute-start(bf16[512,384]{1,0:T(8,128)(2,1)} %get-tuple-element.31), channel_id=1, source_target_pairs={{0,64},{64,128},{128,192},{192,0},{1,65},{65,129},{129,193},{193,1... | collective-permute-start | bytes 1179656 | tf_op jit(solution)/shard_map/ppermute | solution.py:260
  191.6 0.7 copy-start.8
  192.3 21.8 %collective-permute-start.3 = (bf16[512,384]{1,0:T(8,128)(2,1)}, bf16[512,384]{1,0:T(8,128)(2,1)}, u32[]{:S(2)}, u32[]{:S(2)}) collective-permute-start(bf16[512,384]{1,0:T(8,128)(2,1)} %get-tuple-element.32), channel_id=1, source_target_pairs={{0,192},{64,0},{128,64},{192,128},{1,193},{65,1},{129,65},{193,129... | collective-permute-start | bytes 1179656 | tf_op jit(solution)/shard_map/ppermute | solution.py:260
  195.7 0.7 copy-start.10
  196.4 23.0 %collective-permute-start.6 = (bf16[512,384]{1,0:T(8,128)(2,1)}, bf16[512,384]{1,0:T(8,128)(2,1)}, u32[]{:S(2)}, u32[]{:S(2)}) collective-permute-start(bf16[512,384]{1,0:T(8,128)(2,1)} %get-tuple-element.33), channel_id=1, source_target_pairs={{0,128},{64,192},{128,0},{192,64},{1,129},{65,193},{129,1},{193,65... | collective-permute-start | bytes 1179656 | tf_op jit(solution)/shard_map/ppermute | solution.py:260
  197.5 1.0 copy-start
  198.5 1.0 copy-start.2
  199.5 1.0 copy-start.4
  200.5 1.0 copy-start.6
  201.5 1.0 copy-start.9
  202.5 1.0 copy-start.11
  203.4 10.7 %copy-start.7 = (bf16[512,384]{1,0:T(8,128)(2,1)S(1)}, bf16[512,384]{1,0:T(8,128)(2,1)}, u32[]{:S(2)}) copy-start(bf16[512,384]{1,0:T(8,128)(2,1)} %get-tuple-element.30.x0) | copy-start | bytes 1179652
  219.3 5.0 %copy-start.13 = (s32[128,2]{1,0:T(8,128)S(1)}, s32[128,2]{1,0:T(8,128)}, u32[]{:S(2)}) copy-start(s32[128,2]{1,0:T(8,128)} %copy.16.ids_ref) | copy-start | bytes 3076

commit v3 on v2

v3 whole, which is shorter than its diff:
```python
import jax
import jax.numpy as jnp
import numpy as np
from jax import lax
from jax.experimental import pallas as pl
from jax.experimental.pallas import tpu as pltpu
from jax.sharding import PartitionSpec as P


F32 = jnp.float32
BF16 = jnp.bfloat16
N = 64
CAP = 3
PER = 2 * CAP
ROWS = N * PER
D = 2048
FF = 768
TOK = 128
DP = 4
SEG = 512
NSEG = D // SEG
SPAN = NSEG * PER
TILE = 128
NU = D // (4 * TILE)
BROWS = 8
BCOLS = (3 * NU + 1) * TILE
GROUP = 8
GROWS = GROUP * PER
NGROUP = N // GROUP
FB = 256
NFB = FF // FB


def permutations():
    unmix = np.zeros((NSEG * GROWS, GROUP * SPAN), np.float32)
    pack = np.zeros((3 * GROUP * BROWS, 4 * GROWS), np.float32)
    probs = np.zeros((GROUP * BROWS, GROWS), np.float32)
    for d in range(GROUP):
        for j in range(PER):
            row = d * PER + j
            probs[d * BROWS + j, row] = 1
            for s in range(NSEG):
                unmix[s * GROWS + row, d * SPAN + s * PER + j] = 1
            for v in range(4):
                c, r = divmod(v * PER + j, BROWS)
                pack[(c * GROUP + d) * BROWS + r, v * GROWS + row] = 1
    return unmix, pack, np.ascontiguousarray(pack.T), probs


UNMIX, PACK, UNPACK, PROBS = permutations()


def mm(a, b):
    return jnp.dot(a, b, preferred_element_type=F32)


def mm_t(a, b):
    return lax.dot_general(a, b, (((1,), (1,)), ((), ())), preferred_element_type=F32)


def iota(shape, dim):
    return lax.broadcasted_iota(jnp.int32, shape, dim)


def split_slot(ids):
    is_copy = (ids >= N).astype(jnp.int32)
    base = ids - N * is_copy
    target = jnp.where(ids >= N, jnp.bitwise_xor(base, N // 2), base)
    return target, is_copy * CAP


def places_in_lanes(ids_ref):
    ids = [ids_ref[k : k + 1, :] for k in range(2)]
    hot = [(iota((2 * N, TOK), 0) == v).astype(F32) for v in ids]
    before = (iota((TOK, TOK), 0) < iota((TOK, TOK), 1)).astype(F32).astype(BF16)
    count = mm((hot[0] + hot[1]).astype(BF16), before)
    out = []
    for k in range(2):
        rank = jnp.sum(count * hot[k], axis=0, keepdims=True).astype(jnp.int32)
        target, first = split_slot(ids[k])
        out.append((target, first + rank))
    return out


def places_in_rows(ids_ref):
    ids = [ids_ref[:, k : k + 1] for k in range(2)]
    hot = [(iota((TOK, 2 * N), 1) == v).astype(F32) for v in ids]
    before = (iota((TOK, TOK), 1) < iota((TOK, TOK), 0)).astype(F32).astype(BF16)
    count = mm(before, (hot[0] + hot[1]).astype(BF16))
    out = []
    for k in range(2):
        rank = jnp.sum(count * hot[k], axis=1, keepdims=True).astype(jnp.int32)
        target, first = split_slot(ids[k])
        out.append((target, first + rank))
    return out


def send_rows(ids_ref, weights, x_ref, out_ref):
    lanes = []
    for target, slot in places_in_lanes(ids_ref):
        at = target * SPAN + slot
        lanes.append(jnp.concatenate([at + s * PER for s in range(NSEG)], axis=1))
    stacked = jnp.concatenate([x_ref[:, s * SEG : (s + 1) * SEG] for s in range(NSEG)], axis=0)
    block = 384
    for c in range(N * SPAN // block):
        rows = iota((block, NSEG * TOK), 0) + c * block
        pick = jnp.where(
            rows == lanes[0], weights[0], jnp.where(rows == lanes[1], weights[1], 0.0)
        ).astype(BF16)
        out_ref[c * block : (c + 1) * block, :] = mm(pick, stacked).astype(BF16)


def send_tokens_kernel(ids_ref, x_ref, out_ref):
    send_rows(ids_ref, (1.0, 1.0), x_ref, out_ref)


def send_scaled_kernel(ids_ref, prob_ref, x_ref, out_ref):
    probs = [prob_ref[k : k + 1, :].astype(F32) for k in range(2)]
    weights = [jnp.concatenate([v] * NSEG, axis=1) for v in probs]
    send_rows(ids_ref, weights, x_ref, out_ref)


def unmix_rows(perm_ref, got_ref, rows_ref):
    perm = perm_ref[...]
    for g in range(NGROUP):
        part = mm(perm, got_ref[g * GROUP * SPAN : (g + 1) * GROUP * SPAN, :]).astype(BF16)
        for s in range(NSEG):
            rows_ref[s, g * GROWS : (g + 1) * GROWS, :] = part[s * GROWS : (s + 1) * GROWS]


def unmix_kernel(dp_ref, perm_ref, got_ref, rows, x0, x1, x2, x3):
    unmix_rows(perm_ref, got_ref, rows)
    for k, ref in enumerate((x0, x1, x2, x3)):
        which = lax.rem(dp_ref[0] + k, DP)
        ref[...] = rows[which].astype(F32).T.astype(BF16)


def forward_kernel(
    rows, gate_hbm, up_hbm, gate_ref, up_ref, hidden_low, hidden_high, gate_w, up_w, sems
):
    half = FF // 2
    copies = []
    for i in range(2):
        at = pl.ds(i * half, half)
        for m, (source, target) in enumerate(((gate_hbm, gate_w), (up_hbm, up_w))):
            copies.append(
                pltpu.make_async_copy(source.at[:, at], target.at[:, at], sems.at[2 * i + m])
            )
            copies[-1].start()
    for i, out in enumerate((hidden_low, hidden_high)):
        at = slice(i * half, (i + 1) * half)
        copies[2 * i].wait()
        gate = sum(mm(rows[s], gate_w[s * SEG : (s + 1) * SEG, at]) for s in range(NSEG))
        copies[2 * i + 1].wait()
        up = sum(mm(rows[s], up_w[s * SEG : (s + 1) * SEG, at]) for s in range(NSEG))
        gate_ref[:, at] = gate
        up_ref[:, at] = up
        out[...] = (gate * jax.nn.sigmoid(gate) * up).T.astype(BF16)


def backward_kernel(
    dp_ref, perm_ref, got_ref, down_hbm, gate_hbm, up_hbm,
    back_ref, q_ref, gate_out, up_out, s0, s1, s2, s3, rows, down_w, gate_ref, up_ref, sems, loads,
):
    arriving = []
    for i in range(NFB):
        at = pl.ds(i * FB, FB)
        pairs = (
            (down_hbm.at[at], down_w.at[at]),
            (gate_hbm.at[:, at], gate_ref.at[:, at]),
            (up_hbm.at[:, at], up_ref.at[:, at]),
        )
        for m, (source, target) in enumerate(pairs):
            arriving.append(pltpu.make_async_copy(source, target, loads.at[3 * i + m]))
            arriving[-1].start()
    unmix_rows(perm_ref, got_ref, rows)
    copies = []
    for k, ref in enumerate((s0, s1, s2, s3)):
        which = lax.rem(dp_ref[0] + k, DP)
        copies.append(pltpu.make_async_copy(rows.at[which], ref, sems.at[k]))
    total = jnp.zeros((ROWS, 1), F32)
    for i in range(NFB):
        at = slice(i * FB, (i + 1) * FB)
        for copy in arriving[3 * i : 3 * i + 3]:
            copy.wait()
        back_hidden = sum(mm_t(rows[s], down_w[at, s * SEG : (s + 1) * SEG]) for s in range(NSEG))
        gate = gate_ref[:, at]
        up = up_ref[:, at]
        sig = jax.nn.sigmoid(gate)
        activated = gate * sig
        hidden = (activated * up).astype(BF16).astype(F32)
        back_ref[0, :, at] = (back_hidden * up * sig * (1.0 + gate * (1.0 - sig))).astype(BF16)
        back_ref[1, :, at] = (back_hidden * activated).astype(BF16)
        total += jnp.sum(hidden * back_hidden, axis=1, keepdims=True)
        if i == 0:
            for copy in copies:
                copy.start()
    for m, ref in enumerate((gate_out, up_out)):
        copies.append(pltpu.make_async_copy(back_ref.at[m], ref, sems.at[DP + m]))
        copies[-1].start()
    q_ref[...] = jnp.broadcast_to(total, q_ref.shape)
    for copy in copies:
        copy.wait()


def send_back_kernel(pack_ref, probs_ref, back_ref, q_ref, gate_w, up_w, out_ref, rows, sent, sems):
    for i in range(NSEG):
        at = slice(i * SEG, (i + 1) * SEG)
        rows[:, at] = (mm_t(back_ref[0], gate_w[at, :]) + mm_t(back_ref[1], up_w[at, :])).astype(BF16)
    pack = pack_ref[...]
    height = GROUP * BROWS
    copies = []
    for g in range(NGROUP):
        lo, hi = g * GROWS, (g + 1) * GROWS
        stacked = jnp.concatenate(
            [
                jnp.concatenate(
                    [rows[lo:hi, (4 * u + v) * TILE : (4 * u + v + 1) * TILE] for u in range(NU)],
                    axis=1,
                )
                for v in range(4)
            ],
            axis=0,
        )
        part = mm(pack, stacked).astype(BF16)
        top = g * height
        for u in range(NU):
            for c in range(3):
                col = (3 * u + c) * TILE
                sent[top : top + height, col : col + TILE] = part[
                    c * height : (c + 1) * height, u * TILE : (u + 1) * TILE
                ]
        sent[top : top + height, 3 * NU * TILE :] = mm(
            probs_ref[...], q_ref[lo:hi, :].astype(BF16)
        ).astype(BF16)
        half = slice(top, top + height)
        copies.append(pltpu.make_async_copy(sent.at[half], out_ref.at[half], sems.at[g]))
        copies[-1].start()
    for copy in copies:
        copy.wait()


def combine_kernel(ids_ref, ids_t_ref, prob_ref, perm_ref, got_ref, tok_ref, gprob_ref, rows):
    perm = perm_ref[...]
    height = GROUP * BROWS
    for g in range(NGROUP):
        top = g * height
        stacked = jnp.concatenate(
            [
                jnp.concatenate(
                    [
                        got_ref[top : top + height, (3 * u + c) * TILE : (3 * u + c + 1) * TILE]
                        for u in range(NU)
                    ],
                    axis=1,
                )
                for c in range(3)
            ],
            axis=0,
        )
        part = mm(perm, stacked).astype(BF16)
        for u in range(NU):
            for v in range(4):
                col = (4 * u + v) * TILE
                rows[g * GROWS : (g + 1) * GROWS, col : col + TILE] = part[
                    v * GROWS : (v + 1) * GROWS, u * TILE : (u + 1) * TILE
                ]
    at = [target * PER + slot for target, slot in places_in_rows(ids_ref)]
    columns = iota((TOK, ROWS), 1)
    pick = jnp.where((columns == at[0]) | (columns == at[1]), 1.0, 0.0).astype(BF16)
    tok_ref[...] = mm(pick, rows[...]).astype(BF16)
    home = got_ref[:, 3 * NU * TILE :].astype(F32)
    line = iota((N * BROWS, TOK), 0)
    for k, (target, slot) in enumerate(places_in_lanes(ids_t_ref)):
        hit = jnp.where(line == target * BROWS + slot, home, 0.0)
        value = jnp.sum(hit, axis=0, keepdims=True)
        gprob_ref[k : k + 1, :] = (value / prob_ref[k : k + 1, :].astype(F32)).astype(BF16)


def down_grad_kernel(*refs):
    out_ref = refs[-1]
    pieces = refs[2 * DP : 3 * DP]
    half = FF // 2
    for m in range(2):
        acc = sum(mm(refs[m * DP + k][...], pieces[k][...]) for k in range(DP))
        out_ref[m * half : (m + 1) * half] = acc.astype(BF16)


def grad_first_kernel(g0, g1, g3, u0, u1, u3, x0, x1, x3, acc):
    acc[0] = mm(x0[...], g0[...]) + mm(x1[...], g1[...]) + mm(x3[...], g3[...])
    acc[1] = mm(x0[...], u0[...]) + mm(x1[...], u1[...]) + mm(x3[...], u3[...])


def grad_last_kernel(acc, gate_b, up_b, x2, gate_out, up_out):
    gate_out[...] = (acc[0] + mm(x2[...], gate_b[...])).astype(BF16)
    up_out[...] = (acc[1] + mm(x2[...], up_b[...])).astype(BF16)


def shape(dims, kind=BF16):
    return pltpu.HBM(dims, kind)


def near(dims, kind=BF16):
    return pltpu.VMEM(dims, kind)


def in_hbm(values):
    return pltpu.with_memory_space_constraint(values, pltpu.HBM)


def in_vmem(values):
    return pltpu.with_memory_space_constraint(values, pltpu.VMEM)


def call(kernel, out_shape, scratch=(), scalars=0, far=(), by_hand=(), flops=0):
    def run(*args):
        space = [pl.ANY if i in far else pltpu.VMEM for i in range(len(args))]
        space[:scalars] = [pltpu.SMEM] * scalars
        outs = [pl.ANY if i in by_hand else pltpu.VMEM for i in range(len(out_shape))]
        return pl.pallas_call(
            kernel,
            in_specs=[pl.BlockSpec(memory_space=v) for v in space],
            out_specs=[pl.BlockSpec(memory_space=v) for v in outs],
            out_shape=list(out_shape),
            scratch_shapes=list(scratch),
            compiler_params=pltpu.CompilerParams(vmem_limit_bytes=24 * 1024 * 1024),
            cost_estimate=pl.CostEstimate(flops=flops, bytes_accessed=8 << 20, transcendentals=0),
        )(*args)

    return run


def exchange(values):
    return lax.all_to_all(values, "expert", split_axis=0, concat_axis=0, tiled=True)


def shift(values, k):
    return lax.ppermute(values, "dp", [(i, (i + k) % DP) for i in range(DP)])


def spread(pieces):
    return [pieces[0]] + [shift(pieces[k], k) for k in range(1, DP)]


def around(low, high):
    low1 = shift(low, 1)
    high3 = shift(high, DP - 1)
    low3 = shift(low, DP - 1)
    high1 = shift(high, 1)
    low2 = shift(low1, 1)
    high2 = shift(high3, DP - 1)
    return (low, low1, low2, low3), (high, high1, high2, high3)


def body(tokens, cotangent, gate_probs, expert_ids, gate_weight, up_weight, down_weight):
    dp = lax.axis_index("dp").astype(jnp.int32).reshape(1)
    ids_t = expert_ids.T
    probs_t = gate_probs.T

    (send_x,) = call(send_tokens_kernel, [shape((N * SPAN, SEG))], flops=800 << 20)(
        in_hbm(ids_t), in_hbm(tokens)
    )
    got_x = exchange(send_x.reshape(N, SPAN, SEG)).reshape(N * SPAN, SEG)
    (send_c,) = call(send_scaled_kernel, [shape((N * SPAN, SEG))], flops=800 << 20)(
        ids_t, probs_t, cotangent
    )
    got_c = exchange(send_c.reshape(N, SPAN, SEG)).reshape(N * SPAN, SEG)

    unmix, pack, unpack, probs_perm = [jnp.asarray(v, BF16) for v in (UNMIX, PACK, UNPACK, PROBS)]

    rows, *x_pieces = call(
        unmix_kernel,
        [near((NSEG, ROWS, SEG))] + [shape((SEG, ROWS))] * DP,
        scalars=1, flops=300 << 20,
    )(dp, unmix, got_x)
    x_pieces = spread(x_pieces)
    gate, up, hidden_low, hidden_high = call(
        forward_kernel,
        [shape((ROWS, FF), F32)] * 2 + [shape((FF // 2, ROWS))] * 2,
        scratch=[
            pltpu.VMEM((D, FF), BF16),
            pltpu.VMEM((D, FF), BF16),
            pltpu.SemaphoreType.DMA((4,)),
        ],
        far=(1, 2), flops=3000 << 20,
    )(in_vmem(rows), in_hbm(gate_weight[0]), in_hbm(up_weight[0]))
    h_low, h_high = around(hidden_low, hidden_high)

    back_near, q, back_gate, back_up, *s_pieces = call(
        backward_kernel,
        [near((2, ROWS, FF)), near((ROWS, TILE), F32)]
        + [shape((ROWS, FF))] * 2
        + [shape((ROWS, SEG))] * DP,
        scratch=[
            pltpu.VMEM((NSEG, ROWS, SEG), BF16),
            pltpu.VMEM((FF, D), BF16),
            pltpu.VMEM((ROWS, FF), F32),
            pltpu.VMEM((ROWS, FF), F32),
            pltpu.SemaphoreType.DMA((DP + 2,)),
            pltpu.SemaphoreType.DMA((3 * NFB,)),
        ],
        scalars=1, far=(3, 4, 5), by_hand=(2, 3, 4, 5, 6, 7), flops=2000 << 20,
    )(dp, unmix, got_c, in_hbm(down_weight[0]), in_hbm(gate), in_hbm(up))
    b_gate, b_up = around(back_gate, back_up)
    s_pieces = spread(s_pieces)

    (send_b,) = call(
        send_back_kernel, [shape((N * BROWS, BCOLS))],
        scratch=[
            pltpu.VMEM((ROWS, D), BF16),
            pltpu.VMEM((N * BROWS, BCOLS), BF16),
            pltpu.SemaphoreType.DMA((NGROUP,)),
        ],
        by_hand=(0,), flops=3000 << 20,
    )(pack, probs_perm, in_vmem(back_near), in_vmem(q), in_vmem(gate_weight[0]), in_vmem(up_weight[0]))
    got_b = exchange(send_b.reshape(N, BROWS, BCOLS)).reshape(N * BROWS, BCOLS)

    (acc,) = call(grad_first_kernel, [near((2, SEG, FF), F32)], flops=1800 << 20)(
        *(b[k] for b in (b_gate, b_up) for k in (0, 1, 3)), x_pieces[0], x_pieces[1], x_pieces[3]
    )
    (grad_down,) = call(down_grad_kernel, [shape((FF, SEG))], flops=1200 << 20)(
        *h_low, *h_high, *s_pieces
    )
    grad_gate, grad_up = call(grad_last_kernel, [shape((SEG, FF))] * 2, flops=600 << 20)(
        in_vmem(acc), b_gate[2], b_up[2], x_pieces[2]
    )
    grad_tokens, grad_probs = call(
        combine_kernel, [shape((TOK, D)), shape((2, TOK))],
        scratch=[pltpu.VMEM((ROWS, D), BF16)], flops=1000 << 20,
    )(expert_ids, ids_t, probs_t, unpack, got_b)
    return grad_tokens, grad_probs.T, grad_gate[None], grad_up[None], grad_down[None]


def solution(mesh):
    in_specs = (
        P(("dp", "expert"), None),
        P(("dp", "expert"), None),
        P(("dp", "expert"), None),
        P(("dp", "expert"), None),
        P("expert", None, None),
        P("expert", None, None),
        P("expert", None, None),
    )
    out_specs = (
        P(("dp", "expert"), None),
        P(("dp", "expert"), None),
        P("expert", "dp", None),
        P("expert", "dp", None),
        P("expert", None, "dp"),
    )

    return jax.shard_map(body, mesh=mesh, in_specs=in_specs, out_specs=out_specs, check_vma=False)
```

time: 231 us -> 224 us (0.970)
  the two profiles are of different devices: /device:TPU:1 before, /device:TPU:10 now
where the time goes in v3:
time: 224 us; the launch traced here: 223 us
  waiting for transfers between devices  116 us (52%)
  starting transfers between devices  50.9 us (23%)
  Pallas kernels  37.7 us (17%)
  local copies, waits for them, and re-layouts  18 us (8%)
    all_to_all x3, waiting for transfers between devices, exchange(): lax.all_to_all(values, 'expert', split_axis=0, concat_axis=0, tiled=True)  65.7 us
    ppermute x18, waiting for transfers between devices, shift(): return lax.ppermute(values, 'dp', [(i, (i + k) % DP) for i in range(DP)])  50.1 us
    pallas_call x10, Pallas kernels, run(): pl.pallas_call(kernel, in_specs=[pl.BlockSpec(memory_space=v) for v in sp...  37.7 us
    all_to_all x3, starting transfers between devices, exchange(): lax.all_to_all(values, 'expert', split_axis=0, concat_axis=0, tiled=True)  27.3 us
    ppermute x18, starting transfers between devices, shift(): return lax.ppermute(values, 'dp', [(i, (i + k) % DP) for i in range(DP)])  23.6 us
    unnamed x69, local copies, waits for them, and re-layouts  18 us
  transfers between devices with their start and end apart: 21, of which 9 were waited for; matrix products, arithmetic and copies ran while one was open for 0% of the time, Pallas kernels for 10%

profile of v3, /device:TPU:10, one launch (start us, length us, event | category | flops | bytes accessed | tf_op | source)
XLA Modules:
  0.0 223.2 jit_solution(9390288567327702548)
XLA Ops:
  0.6 3.3 %shard_map.147 = bf16[1536,512]{1,0:T(8,128)(2,1)} custom-call(s32[2,128]{1,0:T(2,128)} %bitcast.19, bf16[128,2048]{1,0:T(8,128)(2,1)} %x_ref.3), custom_call_target="tpu_custom_call" | custom-call | flops 838860800 | bytes 8388608 | tf_op jit(solution)/shard_map/pallas_call | solution.py:320
  4.0 12.2 %all-to-all-start.1 = ((bf16[64,24,512]{2,1,0:T(8,128)(2,1)}), bf16[64,24,512]{2,1,0:T(8,128)(2,1)S(1)}, u32[]{:S(2)}, u32[]{:S(2)}) async-start(bf16[64,24,512]{2,1,0:T(8,128)(2,1)} %bitcast.30), calls=%async_computation.1 | async-start | bytes 3145728 | tf_op jit(solution)/shard_map/all_to_all | solution.py:334
  16.2 2.3 %shard_map.146 = bf16[1536,512]{1,0:T(8,128)(2,1)} custom-call(s32[2,128]{1,0:T(2,128)S(1)} %bitcast.20, bf16[2,128]{1,0:T(2,128)(2,1)S(1)} %bitcast.26, bf16[128,2048]{1,0:T(8,128)(2,1)S(1)} %copy-done.29), custom_call_target="tpu_custom_call" | custom-call | flops 838860800 | bytes 8388608 | tf_op jit(solution)/shard_map/pallas_call | solution.py:320
  18.6 36.1 %all-to-all-done.1 = bf16[64,24,512]{2,1,0:T(8,128)(2,1)S(1)} async-done(((bf16[64,24,512]{2,1,0:T(8,128)(2,1)}), bf16[64,24,512]{2,1,0:T(8,128)(2,1)S(1)}, u32[]{:S(2)}, u32[]{:S(2)}) %all-to-all-start.1) | async-done | bytes 1572896 | tf_op jit(solution)/shard_map/all_to_all | solution.py:334
  54.7 7.5 %all-to-all-start = ((bf16[64,24,512]{2,1,0:T(8,128)(2,1)}), bf16[64,24,512]{2,1,0:T(8,128)(2,1)S(1)}, u32[]{:S(2)}, u32[]{:S(2)}) async-start(bf16[64,24,512]{2,1,0:T(8,128)(2,1)} %bitcast.29), calls=%async_computation | async-start | bytes 3145728 | tf_op jit(solution)/shard_map/all_to_all | solution.py:334
  62.2 2.2 shard_map.148
  64.4 6.7 %shard_map.149 = (f32[384,768]{1,0:T(8,128)}, f32[384,768]{1,0:T(8,128)}, bf16[384,384]{1,0:T(8,128)(2,1)}, bf16[384,384]{1,0:T(8,128)(2,1)}) custom-call(bf16[4,384,512]{2,1,0:T(8,128)(2,1)S(1)} %get-tuple-element.26.rows, bf16[2048,768]{1,0:T(8,128)(2,1)} %bitcast.22, bf16[2048,768]{1,0:T(8,128)(2,1)} %bitcast.24), custom_call_target="tpu_custom_call" | custom-call | flops 3145728000 | bytes 8388608 | tf_op jit(solution)/shard_map/pallas_call | solution.py:320
  71.1 29.5 %all-to-all-done = bf16[64,24,512]{2,1,0:T(8,128)(2,1)S(1)} async-done(((bf16[64,24,512]{2,1,0:T(8,128)(2,1)}), bf16[64,24,512]{2,1,0:T(8,128)(2,1)S(1)}, u32[]{:S(2)}, u32[]{:S(2)}) %all-to-all-start) | async-done | bytes 1572896 | tf_op jit(solution)/shard_map/all_to_all | solution.py:334
  100.7 6.1 %shard_map.150 = (bf16[2,384,768]{2,1,0:T(8,128)(2,1)S(1)}, f32[384,128]{1,0:T(8,128)S(1)}, bf16[384,768]{1,0:T(8,128)(2,1)}, bf16[384,768]{1,0:T(8,128)(2,1)}, ...) custom-call(s32[1]{0:T(128)} %bitcast.2.dp_ref, ...), custom_call_target="tpu_custom_call" | custom-call | flops 2097152000 | bytes 8388608 | tf_op jit(solution)/shard_map/pallas_call | solution.py:320
  106.8 4.1 %shard_map.151 = bf16[512,1664]{1,0:T(8,128)(2,1)} custom-call(bf16[192,192]{1,0:T(8,128)(2,1)S(1)} %copy-done.32, bf16[64,48]{1,0:T(8,128)(2,1)S(1)} %copy-done.33, bf16[2,384,768]{2,1,0:T(8,128)(2,1)S(1)} %get-tuple-element.29.back_ref, f32[384,128]{1,0:T(8,128)S(1)} %get-tuple-element.30.q_ref, bf16[2048,768]{1,0:T(8,128)(2,1)S(1)} %bitcast.23, ...), custom_call_target="tpu_custom_call" | custom-call | flops 3145728000 | bytes 8388608 | tf_op jit(solution)/shard_map/pallas_call | solution.py:320
  110.9 0.0 copy-start
  110.9 7.5 %all-to-all-start.2 = ((bf16[64,8,1664]{2,1,0:T(8,128)(2,1)}), bf16[64,8,1664]{2,1,0:T(8,128)(2,1)S(1)}, u32[]{:S(2)}, u32[]{:S(2)}) async-start(bf16[64,8,1664]{2,1,0:T(8,128)(2,1)} %bitcast.28), calls=%async_computation.2 | async-start | bytes 3407872 | tf_op jit(solution)/shard_map/all_to_all | solution.py:334
  118.4 1.6 collective-permute-start.9
  120.0 0.5 collective-permute-start.13
  120.5 1.5 collective-permute-start.15
  122.0 2.3 %collective-permute-start.16 = (bf16[384,512]{1,0:T(8,128)(2,1)}, bf16[384,512]{1,0:T(8,128)(2,1)S(1)}, u32[]{:S(2)}, u32[]{:S(2)}) collective-permute-start(bf16[384,512]{1,0:T(8,128)(2,1)} %get-tuple-element.45), channel_id=1, source_target_pairs={{0,128},{64,192},{128,0},{192,64},{1,129},{65,193},{129,1},{193,65... | collective-permute-start | bytes 1179656 | tf_op jit(solution)/shard_map/ppermute | solution.py:338
  124.4 0.9 collective-permute-start.11
  125.3 3.3 %collective-permute-done.9.refs_1_ = bf16[384,384]{1,0:T(8,128)(2,1)S(1)} collective-permute-done((bf16[384,384]{1,0:T(8,128)(2,1)}, bf16[384,384]{1,0:T(8,128)(2,1)S(1)}, u32[]{:S(2)}, u32[]{:S(2)}) %collective-permute-start.9) | collective-permute-done | bytes 294944 | tf_op jit(solution)/shard_map/ppermute | solution.py:338
  128.6 1.5 collective-permute-start.12
  130.1 7.7 %collective-permute-done.13.refs_7_ = bf16[384,384]{1,0:T(8,128)(2,1)S(1)} collective-permute-done((bf16[384,384]{1,0:T(8,128)(2,1)}, bf16[384,384]{1,0:T(8,128)(2,1)S(1)}, u32[]{:S(2)}, u32[]{:S(2)}) %collective-permute-start.13) | collective-permute-done | bytes 294944 | tf_op jit(solution)/shard_map/ppermute | solution.py:338
  137.8 0.4 collective-permute-start.17
  138.2 6.7 %collective-permute-done.11.refs_3_ = bf16[384,384]{1,0:T(8,128)(2,1)S(1)} collective-permute-done((bf16[384,384]{1,0:T(8,128)(2,1)}, bf16[384,384]{1,0:T(8,128)(2,1)S(1)}, u32[]{:S(2)}, u32[]{:S(2)}) %collective-permute-start.11) | collective-permute-done | bytes 294944 | tf_op jit(solution)/shard_map/ppermute | solution.py:338
  144.8 0.7 copy-done.17
  145.6 1.3 collective-permute-start
  146.8 5.0 %collective-permute-done.12.refs_5_ = bf16[384,384]{1,0:T(8,128)(2,1)S(1)} collective-permute-done((bf16[384,384]{1,0:T(8,128)(2,1)}, bf16[384,384]{1,0:T(8,128)(2,1)S(1)}, u32[]{:S(2)}, u32[]{:S(2)}) %collective-permute-start.12) | collective-permute-done | bytes 294944 | tf_op jit(solution)/shard_map/ppermute | solution.py:338
  151.8 0.7 copy-done.19
  152.6 1.7 collective-permute-start.3
  154.3 0.7 copy-done.2
  155.0 0.3 collective-permute-start.4
  155.4 0.7 copy-done.4
  156.1 1.7 collective-permute-start.5
  157.8 0.8 copy-done.6
  158.6 0.3 collective-permute-start.10
  158.9 0.7 copy-done.13
  159.6 13.3 %collective-permute-done.4.x1 = bf16[512,384]{1,0:T(8,128)(2,1)S(1)} collective-permute-done((bf16[512,384]{1,0:T(8,128)(2,1)}, bf16[512,384]{1,0:T(8,128)(2,1)S(1)}, u32[]{:S(2)}, u32[]{:S(2)}) %collective-permute-start.4) | collective-permute-done | bytes 393248 | tf_op jit(solution)/shard_map/ppermute | solution.py:338
  172.9 0.7 copy-done.9
  173.6 1.7 collective-permute-start.1
  175.4 0.8 copy-done.11
  176.1 1.1 collective-permute-start.2
  177.3 2.0 collective-permute-done.10.refs_2_
  179.2 0.7 copy-done.21
  180.0 1.1 collective-permute-start.14
  181.0 0.7 copy-done.15
  181.7 0.9 collective-permute-start.6
  182.7 1.4 collective-permute-start.7
  184.0 12.1 %collective-permute-done.14.refs_6_ = bf16[384,384]{1,0:T(8,128)(2,1)S(1)} collective-permute-done((bf16[384,384]{1,0:T(8,128)(2,1)S(1)}, bf16[384,384]{1,0:T(8,128)(2,1)S(1)}, u32[]{:S(2)}, u32[]{:S(2)}) %collective-permute-start.14) | collective-permute-done | bytes 294944 | tf_op jit(solution)/shard_map/ppermute | solution.py:338
  196.2 0.7 copy-done.23
  196.9 3.3 %collective-permute-start.8 = (bf16[512,384]{1,0:T(8,128)(2,1)}, bf16[512,384]{1,0:T(8,128)(2,1)}, u32[]{:S(2)}, u32[]{:S(2)}) collective-permute-start(bf16[512,384]{1,0:T(8,128)(2,1)} %get-tuple-element.38), channel_id=1, source_target_pairs={{0,128},{64,192},{128,0},{192,64},{1,129},{65,193},{129,1},{193,65... | collective-permute-start | bytes 1179656 | tf_op jit(solution)/shard_map/ppermute | solution.py:338
  200.2 0.1 copy.16.ids_ref
  200.4 1.0 copy-done.1
  201.3 1.0 copy-done.3
  202.3 1.0 copy-done.5
  203.3 1.0 copy-done.7
  204.3 1.0 copy-done.14
  205.3 1.0 copy-done.16
  206.3 1.0 copy-done.18
  207.2 1.0 copy-done.20
  208.2 1.0 copy-done.22
  209.1 1.0 copy-done.24
  210.1 3.8 %shard_map.155 = bf16[768,512]{1,0:T(8,128)(2,1)} custom-call(bf16[384,384]{1,0:T(8,128)(2,1)} %get-tuple-element.41.refs_0_, bf16[384,384]{1,0:T(8,128)(2,1)S(1)} %copy-done.14, bf16[384,384]{1,0:T(8,128)(2,1)S(1)} %copy-done.22, bf16[384,384]{1,0:T(8,128)(2,1)S(1)} %copy-done.18, bf16[384,384]{1,0:T(8,128)(2,1)} %get-tuple-element.42.refs_4_, ...), custom_call_target="tpu_custom_call" | custom-call | flops 1258291200 | bytes 8388608 | tf_op jit(solution)/shard_map/pallas_call | solution.py:320
  214.0 4.4 %shard_map.153.acc = f32[2,512,768]{2,1,0:T(8,128)S(1)} custom-call(bf16[384,768]{1,0:T(8,128)(2,1)S(1)} %copy-done, bf16[384,768]{1,0:T(8,128)(2,1)} %collective-permute-done.g1, bf16[384,768]{1,0:T(8,128)(2,1)} %collective-permute-done.1.g3, bf16[384,768]{1,0:T(8,128)(2,1)} %get-tuple-element.34.u0, bf16[384,768]{1,0:T(8,128)(2,1)} %collective-permute-done.2.u1, ...), custom_call_target="tpu_custom_call" | custom-call | flops 1887436800 | bytes 8388608 | tf_op jit(solution)/shard_map/pallas_call | solution.py:320
  218.3 0.0 copy-start.31
  218.4 2.9 %shard_map.154 = (bf16[512,768]{1,0:T(8,128)(2,1)}, bf16[512,768]{1,0:T(8,128)(2,1)}) custom-call(f32[2,512,768]{2,1,0:T(8,128)S(1)} %shard_map.153.acc, bf16[384,768]{1,0:T(8,128)(2,1)S(1)} %collective-permute-done.6.gate_b, bf16[384,768]{1,0:T(8,128)(2,1)S(1)} %collective-permute-done.7.up_b, bf16[512,384]{1,0:T(8,128)(2,1)} %collective-permute-done.8.x2), custom_call_target="tpu_custom_call" | custom-call | flops 629145600 | bytes 8388608 | tf_op jit(solution)/shard_map/pallas_call | solution.py:320
  221.3 2.0 shard_map.152
  (57 shorter events, 0.1 us)
Async XLA Ops:
  4.0 12.3 %copy-start.26 = (s32[128,2]{0,1:T(2,128)S(1)}, s32[128,2]{0,1:T(2,128)}, u32[]{:S(2)}) copy-start(s32[128,2]{0,1:T(2,128)} %param.14) | copy-start | bytes 3076
  4.0 12.3 %copy-start.29 = (bf16[128,2048]{1,0:T(8,128)(2,1)S(1)}, bf16[128,2048]{1,0:T(8,128)(2,1)}, u32[]{:S(2)}) copy-start(bf16[128,2048]{1,0:T(8,128)(2,1)} %x_ref.2) | copy-start | bytes 1572868
  4.0 12.3 %copy-start.30 = (bf16[128,2]{0,1:T(2,128)(2,1)S(1)}, bf16[128,2]{0,1:T(2,128)(2,1)}, u32[]{:S(2)}) copy-start(bf16[128,2]{0,1:T(2,128)(2,1)} %param.13) | copy-start | bytes 1540
  4.0 50.7 %all-to-all-start.1 = ((bf16[64,24,512]{2,1,0:T(8,128)(2,1)}), bf16[64,24,512]{2,1,0:T(8,128)(2,1)S(1)}, u32[]{:S(2)}, u32[]{:S(2)}) async-start(bf16[64,24,512]{2,1,0:T(8,128)(2,1)} %bitcast.30), calls=%async_computation.1 | async-start | bytes 3145728 | tf_op jit(solution)/shard_map/all_to_all | solution.py:334
  54.7 7.5 %copy-start.25 = (bf16[192,192]{1,0:T(8,128)(2,1)S(1)}, bf16[192,192]{1,0:T(8,128)(2,1)}, u32[]{:S(2)}) copy-start(bf16[192,192]{1,0:T(8,128)(2,1)} %constant.14.clone.perm_ref) | copy-start | bytes 221188
  54.7 46.0 %all-to-all-start = ((bf16[64,24,512]{2,1,0:T(8,128)(2,1)}), bf16[64,24,512]{2,1,0:T(8,128)(2,1)S(1)}, u32[]{:S(2)}, u32[]{:S(2)}) async-start(bf16[64,24,512]{2,1,0:T(8,128)(2,1)} %bitcast.29), calls=%async_computation | async-start | bytes 3145728 | tf_op jit(solution)/shard_map/all_to_all | solution.py:334
  100.7 6.1 %copy-start.27 = (bf16[1,2048,768]{2,1,0:T(8,128)(2,1)S(1)}, bf16[1,2048,768]{2,1,0:T(8,128)(2,1)}, u32[]{:S(2)}) copy-start(bf16[1,2048,768]{2,1,0:T(8,128)(2,1)} %param.15) | copy-start | bytes 9437188
  100.7 6.1 %copy-start.28 = (bf16[1,2048,768]{2,1,0:T(8,128)(2,1)S(1)}, bf16[1,2048,768]{2,1,0:T(8,128)(2,1)}, u32[]{:S(2)}) copy-start(bf16[1,2048,768]{2,1,0:T(8,128)(2,1)} %param.16) | copy-start | bytes 9437188
  100.7 6.1 %copy-start.32 = (bf16[192,192]{1,0:T(8,128)(2,1)S(1)}, bf16[192,192]{1,0:T(8,128)(2,1)}, u32[]{:S(2)}) copy-start(bf16[192,192]{1,0:T(8,128)(2,1)} %constant.15.clone.pack_ref) | copy-start | bytes 221188
  100.7 6.1 %copy-start.33 = (bf16[64,48]{1,0:T(8,128)(2,1)S(1)}, bf16[64,48]{1,0:T(8,128)(2,1)}, u32[]{:S(2)}) copy-start(bf16[64,48]{1,0:T(8,128)(2,1)} %constant.17.clone.probs_ref) | copy-start | bytes 18436
  110.9 34.7 %copy-start = (bf16[384,768]{1,0:T(8,128)(2,1)S(1)}, bf16[384,768]{1,0:T(8,128)(2,1)}, u32[]{:S(2)}) copy-start(bf16[384,768]{1,0:T(8,128)(2,1)} %get-tuple-element.33.g0) | copy-start | bytes 1769476
  110.9 110.4 %all-to-all-start.2 = ((bf16[64,8,1664]{2,1,0:T(8,128)(2,1)}), bf16[64,8,1664]{2,1,0:T(8,128)(2,1)S(1)}, u32[]{:S(2)}, u32[]{:S(2)}) async-start(bf16[64,8,1664]{2,1,0:T(8,128)(2,1)} %bitcast.28), calls=%async_computation.2 | async-start | bytes 3407872 | tf_op jit(solution)/shard_map/all_to_all | solution.py:334
  118.4 10.2 %collective-permute-start.9 = (bf16[384,384]{1,0:T(8,128)(2,1)}, bf16[384,384]{1,0:T(8,128)(2,1)S(1)}, u32[]{:S(2)}, u32[]{:S(2)}) collective-permute-start(bf16[384,384]{1,0:T(8,128)(2,1)} %get-tuple-element.41.refs_0_), channel_id=1, source_target_pairs={{0,64},{64,128},{128,192},{192,0},{1,65},{65,129},{129,193},{193,1... | collective-permute-start | bytes 884744 | tf_op jit(solution)/shard_map/ppermute | solution.py:338
  120.0 17.8 %collective-permute-start.13 = (bf16[384,384]{1,0:T(8,128)(2,1)}, bf16[384,384]{1,0:T(8,128)(2,1)S(1)}, u32[]{:S(2)}, u32[]{:S(2)}) collective-permute-start(bf16[384,384]{1,0:T(8,128)(2,1)} %get-tuple-element.42.refs_4_), channel_id=1, source_target_pairs={{0,192},{64,0},{128,64},{192,128},{1,193},{65,1},{129,65},{193,129... | collective-permute-start | bytes 884744 | tf_op jit(solution)/shard_map/ppermute | solution.py:338
  120.5 33.7 %collective-permute-start.15 = (bf16[384,512]{1,0:T(8,128)(2,1)}, bf16[384,512]{1,0:T(8,128)(2,1)S(1)}, u32[]{:S(2)}, u32[]{:S(2)}) collective-permute-start(bf16[384,512]{1,0:T(8,128)(2,1)} %get-tuple-element.44), channel_id=1, source_target_pairs={{0,64},{64,128},{128,192},{192,0},{1,65},{65,129},{129,193},{193,1... | collective-permute-start | bytes 1179656 | tf_op jit(solution)/shard_map/ppermute | solution.py:338
  122.0 33.3 %collective-permute-start.16 = (bf16[384,512]{1,0:T(8,128)(2,1)}, bf16[384,512]{1,0:T(8,128)(2,1)S(1)}, u32[]{:S(2)}, u32[]{:S(2)}) collective-permute-start(bf16[384,512]{1,0:T(8,128)(2,1)} %get-tuple-element.45), channel_id=1, source_target_pairs={{0,128},{64,192},{128,0},{192,64},{1,129},{65,193},{129,1},{193,65... | collective-permute-start | bytes 1179656 | tf_op jit(solution)/shard_map/ppermute | solution.py:338
  124.4 20.5 %collective-permute-start.11 = (bf16[384,384]{1,0:T(8,128)(2,1)}, bf16[384,384]{1,0:T(8,128)(2,1)S(1)}, u32[]{:S(2)}, u32[]{:S(2)}) collective-permute-start(bf16[384,384]{1,0:T(8,128)(2,1)} %get-tuple-element.41.refs_0_), channel_id=1, source_target_pairs={{0,192},{64,0},{128,64},{192,128},{1,193},{65,1},{129,65},{193,129... | collective-permute-start | bytes 884744 | tf_op jit(solution)/shard_map/ppermute | solution.py:338
  128.6 23.2 %collective-permute-start.12 = (bf16[384,384]{1,0:T(8,128)(2,1)}, bf16[384,384]{1,0:T(8,128)(2,1)S(1)}, u32[]{:S(2)}, u32[]{:S(2)}) collective-permute-start(bf16[384,384]{1,0:T(8,128)(2,1)} %get-tuple-element.42.refs_4_), channel_id=1, source_target_pairs={{0,64},{64,128},{128,192},{192,0},{1,65},{65,129},{129,193},{193,1... | collective-permute-start | bytes 884744 | tf_op jit(solution)/shard_map/ppermute | solution.py:338
  137.8 20.0 %collective-permute-start.17 = (bf16[384,512]{1,0:T(8,128)(2,1)}, bf16[384,512]{1,0:T(8,128)(2,1)S(1)}, u32[]{:S(2)}, u32[]{:S(2)}) collective-permute-start(bf16[384,512]{1,0:T(8,128)(2,1)} %get-tuple-element.46), channel_id=1, source_target_pairs={{0,192},{64,0},{128,64},{192,128},{1,193},{65,1},{129,65},{193,129... | collective-permute-start | bytes 1179656 | tf_op jit(solution)/shard_map/ppermute | solution.py:338
  144.8 0.7 copy-start.17
  145.6 36.2 %collective-permute-start = (bf16[384,768]{1,0:T(8,128)(2,1)S(1)}, bf16[384,768]{1,0:T(8,128)(2,1)}, u32[]{:S(2)}, u32[]{:S(2)}) collective-permute-start(bf16[384,768]{1,0:T(8,128)(2,1)S(1)} %copy-done), channel_id=1, source_target_pairs={{0,64},{64,128},{128,192},{192,0},{1,65},{65,129},{129,193},{193,1... | collective-permute-start | bytes 1769480 | tf_op jit(solution)/shard_map/ppermute | solution.py:338
  151.8 0.7 copy-start.19
  152.6 30.1 %collective-permute-start.3 = (bf16[384,768]{1,0:T(8,128)(2,1)}, bf16[384,768]{1,0:T(8,128)(2,1)}, u32[]{:S(2)}, u32[]{:S(2)}) collective-permute-start(bf16[384,768]{1,0:T(8,128)(2,1)} %get-tuple-element.34.u0), channel_id=1, source_target_pairs={{0,192},{64,0},{128,64},{192,128},{1,193},{65,1},{129,65},{193,129... | collective-permute-start | bytes 1769480 | tf_op jit(solution)/shard_map/ppermute | solution.py:338
  154.3 0.7 copy-start.2
  155.0 17.9 %collective-permute-start.4 = (bf16[512,384]{1,0:T(8,128)(2,1)}, bf16[512,384]{1,0:T(8,128)(2,1)S(1)}, u32[]{:S(2)}, u32[]{:S(2)}) collective-permute-start(bf16[512,384]{1,0:T(8,128)(2,1)} %get-tuple-element.36), channel_id=1, source_target_pairs={{0,64},{64,128},{128,192},{192,0},{1,65},{65,129},{129,193},{193,1... | collective-permute-start | bytes 1179656 | tf_op jit(solution)/shard_map/ppermute | solution.py:338
  155.4 0.7 copy-start.4
  156.1 19.3 %collective-permute-start.5 = (bf16[512,384]{1,0:T(8,128)(2,1)}, bf16[512,384]{1,0:T(8,128)(2,1)S(1)}, u32[]{:S(2)}, u32[]{:S(2)}) collective-permute-start(bf16[512,384]{1,0:T(8,128)(2,1)} %get-tuple-element.37), channel_id=1, source_target_pairs={{0,192},{64,0},{128,64},{192,128},{1,193},{65,1},{129,65},{193,129... | collective-permute-start | bytes 1179656 | tf_op jit(solution)/shard_map/ppermute | solution.py:338
  157.8 0.8 copy-start.6
  158.6 20.6 %collective-permute-start.10 = (bf16[384,384]{1,0:T(8,128)(2,1)S(1)}, bf16[384,384]{1,0:T(8,128)(2,1)S(1)}, u32[]{:S(2)}, u32[]{:S(2)}) collective-permute-start(bf16[384,384]{1,0:T(8,128)(2,1)S(1)} %collective-permute-done.9.refs_1_), channel_id=1, source_target_pairs={{0,64},{64,128},{128,192},{192,0},{1,65},{65,129},{129,193},{193,1... | collective-permute-start | bytes 884744 | tf_op jit(solution)/shard_map/ppermute | solution.py:338
  158.9 0.7 copy-start.13
  172.9 0.7 copy-start.9
  173.6 40.3 %collective-permute-start.1 = (bf16[384,768]{1,0:T(8,128)(2,1)S(1)}, bf16[384,768]{1,0:T(8,128)(2,1)}, u32[]{:S(2)}, u32[]{:S(2)}) collective-permute-start(bf16[384,768]{1,0:T(8,128)(2,1)S(1)} %copy-done), channel_id=1, source_target_pairs={{0,192},{64,0},{128,64},{192,128},{1,193},{65,1},{129,65},{193,129... | collective-permute-start | bytes 1769480 | tf_op jit(solution)/shard_map/ppermute | solution.py:338
  175.4 0.8 copy-start.11
  176.1 37.8 %collective-permute-start.2 = (bf16[384,768]{1,0:T(8,128)(2,1)}, bf16[384,768]{1,0:T(8,128)(2,1)}, u32[]{:S(2)}, u32[]{:S(2)}) collective-permute-start(bf16[384,768]{1,0:T(8,128)(2,1)} %get-tuple-element.34.u0), channel_id=1, source_target_pairs={{0,64},{64,128},{128,192},{192,0},{1,65},{65,129},{129,193},{193,1... | collective-permute-start | bytes 1769480 | tf_op jit(solution)/shard_map/ppermute | solution.py:338
  179.2 0.7 copy-start.21
  180.0 16.2 %collective-permute-start.14 = (bf16[384,384]{1,0:T(8,128)(2,1)S(1)}, bf16[384,384]{1,0:T(8,128)(2,1)S(1)}, u32[]{:S(2)}, u32[]{:S(2)}) collective-permute-start(bf16[384,384]{1,0:T(8,128)(2,1)S(1)} %collective-permute-done.13.refs_7_), channel_id=1, source_target_pairs={{0,192},{64,0},{128,64},{192,128},{1,193},{65,1},{129,65},{193,129... | collective-permute-start | bytes 884744 | tf_op jit(solution)/shard_map/ppermute | solution.py:338
  181.0 0.7 copy-start.15
  181.7 36.6 %collective-permute-start.6 = (bf16[384,768]{1,0:T(8,128)(2,1)}, bf16[384,768]{1,0:T(8,128)(2,1)S(1)}, u32[]{:S(2)}, u32[]{:S(2)}) collective-permute-start(bf16[384,768]{1,0:T(8,128)(2,1)} %collective-permute-done.g1), channel_id=1, source_target_pairs={{0,64},{64,128},{128,192},{192,0},{1,65},{65,129},{129,193},{193,1... | collective-permute-start | bytes 1769480 | tf_op jit(solution)/shard_map/ppermute | solution.py:338
  182.7 35.7 %collective-permute-start.7 = (bf16[384,768]{1,0:T(8,128)(2,1)}, bf16[384,768]{1,0:T(8,128)(2,1)S(1)}, u32[]{:S(2)}, u32[]{:S(2)}) collective-permute-start(bf16[384,768]{1,0:T(8,128)(2,1)} %collective-permute-done.3.u3), channel_id=1, source_target_pairs={{0,192},{64,0},{128,64},{192,128},{1,193},{65,1},{129,65},{193,129... | collective-permute-start | bytes 1769480 | tf_op jit(solution)/shard_map/ppermute | solution.py:338
  196.2 0.7 copy-start.23
  196.9 21.5 %collective-permute-start.8 = (bf16[512,384]{1,0:T(8,128)(2,1)}, bf16[512,384]{1,0:T(8,128)(2,1)}, u32[]{:S(2)}, u32[]{:S(2)}) collective-permute-start(bf16[512,384]{1,0:T(8,128)(2,1)} %get-tuple-element.38), channel_id=1, source_target_pairs={{0,128},{64,192},{128,0},{192,64},{1,129},{65,193},{129,1},{193,65... | collective-permute-start | bytes 1179656 | tf_op jit(solution)/shard_map/ppermute | solution.py:338
  200.4 1.0 copy-start.1
  201.3 1.0 copy-start.3
  202.3 1.0 copy-start.5
  203.3 1.0 copy-start.7
  204.3 1.0 copy-start.14
  205.3 1.0 copy-start.16
  206.3 1.0 copy-start.18
  207.2 1.0 copy-start.20
  208.2 1.0 copy-start.22
  209.1 1.0 copy-start.24
  210.1 3.8 %copy-start.8 = (bf16[512,384]{1,0:T(8,128)(2,1)S(1)}, bf16[512,384]{1,0:T(8,128)(2,1)}, u32[]{:S(2)}) copy-start(bf16[512,384]{1,0:T(8,128)(2,1)} %get-tuple-element.35.x0) | copy-start | bytes 1179652
  210.1 3.8 %copy-start.10 = (bf16[512,384]{1,0:T(8,128)(2,1)S(1)}, bf16[512,384]{1,0:T(8,128)(2,1)}, u32[]{:S(2)}) copy-start(bf16[512,384]{1,0:T(8,128)(2,1)} %copy-done.9) | copy-start | bytes 1179652
  210.1 3.8 %copy-start.12 = (bf16[512,384]{1,0:T(8,128)(2,1)S(1)}, bf16[512,384]{1,0:T(8,128)(2,1)}, u32[]{:S(2)}) copy-start(bf16[512,384]{1,0:T(8,128)(2,1)} %copy-done.11) | copy-start | bytes 1179652
  218.3 2.9 %copy-start.31 = (bf16[192,192]{1,0:T(8,128)(2,1)S(1)}, bf16[192,192]{1,0:T(8,128)(2,1)}, u32[]{:S(2)}) copy-start(bf16[192,192]{1,0:T(8,128)(2,1)} %constant.16.clone.perm_ref) | copy-start | bytes 221188

commit v4 on v3

--- a/solution.py
+++ b/solution.py
@@ -153,8 +153,8 @@
         gate = sum(mm(rows[s], gate_w[s * SEG : (s + 1) * SEG, at]) for s in range(NSEG))
         copies[2 * i + 1].wait()
         up = sum(mm(rows[s], up_w[s * SEG : (s + 1) * SEG, at]) for s in range(NSEG))
-        gate_ref[:, at] = gate
-        up_ref[:, at] = up
+        gate_ref[:, at] = gate.astype(BF16)
+        up_ref[:, at] = up.astype(BF16)
         out[...] = (gate * jax.nn.sigmoid(gate) * up).T.astype(BF16)
 
 
@@ -184,8 +184,8 @@
         for copy in arriving[3 * i : 3 * i + 3]:
             copy.wait()
         back_hidden = sum(mm_t(rows[s], down_w[at, s * SEG : (s + 1) * SEG]) for s in range(NSEG))
-        gate = gate_ref[:, at]
-        up = up_ref[:, at]
+        gate = gate_ref[:, at].astype(F32)
+        up = up_ref[:, at].astype(F32)
         sig = jax.nn.sigmoid(gate)
         activated = gate * sig
         hidden = (activated * up).astype(BF16).astype(F32)
@@ -195,9 +195,14 @@
         if i == 0:
             for copy in copies:
                 copy.start()
-    for m, ref in enumerate((gate_out, up_out)):
-        copies.append(pltpu.make_async_copy(back_ref.at[m], ref, sems.at[DP + m]))
-        copies[-1].start()
+        for m, ref in enumerate((gate_out, up_out)):
+            part = pl.ds(i * FB, FB)
+            copies.append(
+                pltpu.make_async_copy(
+                    back_ref.at[m, :, part], ref.at[:, part], sems.at[DP + 2 * i + m]
+                )
+            )
+            copies[-1].start()
     q_ref[...] = jnp.broadcast_to(total, q_ref.shape)
     for copy in copies:
         copy.wait()
@@ -376,7 +381,7 @@
     x_pieces = spread(x_pieces)
     gate, up, hidden_low, hidden_high = call(
         forward_kernel,
-        [shape((ROWS, FF), F32)] * 2 + [shape((FF // 2, ROWS))] * 2,
+        [shape((ROWS, FF))] * 2 + [shape((FF // 2, ROWS))] * 2,
         scratch=[
             pltpu.VMEM((D, FF), BF16),
             pltpu.VMEM((D, FF), BF16),
@@ -394,9 +399,9 @@
         scratch=[
             pltpu.VMEM((NSEG, ROWS, SEG), BF16),
             pltpu.VMEM((FF, D), BF16),
-            pltpu.VMEM((ROWS, FF), F32),
-            pltpu.VMEM((ROWS, FF), F32),
-            pltpu.SemaphoreType.DMA((DP + 2,)),
+            pltpu.VMEM((ROWS, FF), BF16),
+            pltpu.VMEM((ROWS, FF), BF16),
+            pltpu.SemaphoreType.DMA((DP + 2 * NFB,)),
             pltpu.SemaphoreType.DMA((3 * NFB,)),
         ],
         scalars=1, far=(3, 4, 5), by_hand=(2, 3, 4, 5, 6, 7), flops=2000 << 20,
@@ -416,7 +421,7 @@
     got_b = exchange(send_b.reshape(N, BROWS, BCOLS)).reshape(N * BROWS, BCOLS)
 
     (acc,) = call(grad_first_kernel, [near((2, SEG, FF), F32)], flops=1800 << 20)(
-        *(b[k] for b in (b_gate, b_up) for k in (0, 1, 3)), x_pieces[0], x_pieces[1], x_pieces[3]
+        *(b[k] for b in (b_gate, b_up, x_pieces) for k in (0, 1, 3))
     )
     (grad_down,) = call(down_grad_kernel, [shape((FF, SEG))], flops=1200 << 20)(
         *h_low, *h_high, *s_pieces

time: 224 us -> 224 us (level)
  no operation moved by 1% of the time
where the time goes in v4:
time: 224 us; the launch traced here: 223 us
  waiting for transfers between devices  116 us (52%)
  starting transfers between devices  50.8 us (23%)
  Pallas kernels  37.3 us (17%)
  local copies, waits for them, and re-layouts  18.1 us (8%)
    all_to_all x3, waiting for transfers between devices, exchange(): lax.all_to_all(values, 'expert', split_axis=0, concat_axis=0, tiled=True)  65.8 us
    ppermute x18, waiting for transfers between devices, shift(): return lax.ppermute(values, 'dp', [(i, (i + k) % DP) for i in range(DP)])  49.9 us
    pallas_call x10, Pallas kernels, run(): pl.pallas_call(kernel, in_specs=[pl.BlockSpec(memory_space=v) for v in sp...  37.3 us
    all_to_all x3, starting transfers between devices, exchange(): lax.all_to_all(values, 'expert', split_axis=0, concat_axis=0, tiled=True)  27.2 us
    ppermute x18, starting transfers between devices, shift(): return lax.ppermute(values, 'dp', [(i, (i + k) % DP) for i in range(DP)])  23.7 us
    unnamed x69, local copies, waits for them, and re-layouts  18.1 us
  transfers between devices with their start and end apart: 21, of which 9 were waited for; matrix products, arithmetic and copies ran while one was open for 0% of the time, Pallas kernels for 10%

profile of v4, /device:TPU:10, one launch (start us, length us, event | category | flops | bytes accessed | tf_op | source)
XLA Modules:
  0.0 222.8 jit_solution(434785238172616058)
XLA Ops:
  0.6 3.3 %shard_map.147 = bf16[1536,512]{1,0:T(8,128)(2,1)} custom-call(s32[2,128]{1,0:T(2,128)} %bitcast.19, bf16[128,2048]{1,0:T(8,128)(2,1)} %x_ref.3), custom_call_target="tpu_custom_call" | custom-call | flops 838860800 | bytes 8388608 | tf_op jit(solution)/shard_map/pallas_call | solution.py:325
  4.0 12.2 %all-to-all-start.1 = ((bf16[64,24,512]{2,1,0:T(8,128)(2,1)}), bf16[64,24,512]{2,1,0:T(8,128)(2,1)S(1)}, u32[]{:S(2)}, u32[]{:S(2)}) async-start(bf16[64,24,512]{2,1,0:T(8,128)(2,1)} %bitcast.30), calls=%async_computation.1 | async-start | bytes 3145728 | tf_op jit(solution)/shard_map/all_to_all | solution.py:339
  16.2 2.3 %shard_map.146 = bf16[1536,512]{1,0:T(8,128)(2,1)} custom-call(s32[2,128]{1,0:T(2,128)S(1)} %bitcast.20, bf16[2,128]{1,0:T(2,128)(2,1)S(1)} %bitcast.26, bf16[128,2048]{1,0:T(8,128)(2,1)S(1)} %copy-done.29), custom_call_target="tpu_custom_call" | custom-call | flops 838860800 | bytes 8388608 | tf_op jit(solution)/shard_map/pallas_call | solution.py:325
  18.6 36.1 %all-to-all-done.1 = bf16[64,24,512]{2,1,0:T(8,128)(2,1)S(1)} async-done(((bf16[64,24,512]{2,1,0:T(8,128)(2,1)}), bf16[64,24,512]{2,1,0:T(8,128)(2,1)S(1)}, u32[]{:S(2)}, u32[]{:S(2)}) %all-to-all-start.1) | async-done | bytes 1572896 | tf_op jit(solution)/shard_map/all_to_all | solution.py:339
  54.7 7.4 %all-to-all-start = ((bf16[64,24,512]{2,1,0:T(8,128)(2,1)}), bf16[64,24,512]{2,1,0:T(8,128)(2,1)S(1)}, u32[]{:S(2)}, u32[]{:S(2)}) async-start(bf16[64,24,512]{2,1,0:T(8,128)(2,1)} %bitcast.29), calls=%async_computation | async-start | bytes 3145728 | tf_op jit(solution)/shard_map/all_to_all | solution.py:339
  62.1 2.2 shard_map.148
  64.3 6.6 %shard_map.149 = (bf16[384,768]{1,0:T(8,128)(2,1)}, bf16[384,768]{1,0:T(8,128)(2,1)}, bf16[384,384]{1,0:T(8,128)(2,1)}, bf16[384,384]{1,0:T(8,128)(2,1)}) custom-call(bf16[4,384,512]{2,1,0:T(8,128)(2,1)S(1)} %get-tuple-element.26.rows, bf16[2048,768]{1,0:T(8,128)(2,1)} %bitcast.22, bf16[2048,768]{1,0:T(8,128)(2,1)} %bitcast.24), custom_call_target="tpu_custom_call" | custom-call | flops 3145728000 | bytes 8388608 | tf_op jit(solution)/shard_map/pallas_call | solution.py:325
  70.9 29.6 %all-to-all-done = bf16[64,24,512]{2,1,0:T(8,128)(2,1)S(1)} async-done(((bf16[64,24,512]{2,1,0:T(8,128)(2,1)}), bf16[64,24,512]{2,1,0:T(8,128)(2,1)S(1)}, u32[]{:S(2)}, u32[]{:S(2)}) %all-to-all-start) | async-done | bytes 1572896 | tf_op jit(solution)/shard_map/all_to_all | solution.py:339
  100.6 5.8 %shard_map.150 = (bf16[2,384,768]{2,1,0:T(8,128)(2,1)S(1)}, f32[384,128]{1,0:T(8,128)S(1)}, bf16[384,768]{1,0:T(8,128)(2,1)}, bf16[384,768]{1,0:T(8,128)(2,1)}, ...) custom-call(s32[1]{0:T(128)} %bitcast.2.dp_ref, ...), custom_call_target="tpu_custom_call" | custom-call | flops 2097152000 | bytes 8388608 | tf_op jit(solution)/shard_map/pallas_call | solution.py:325
  106.4 4.1 %shard_map.151 = bf16[512,1664]{1,0:T(8,128)(2,1)} custom-call(bf16[192,192]{1,0:T(8,128)(2,1)S(1)} %copy-done.32, bf16[64,48]{1,0:T(8,128)(2,1)S(1)} %copy-done.33, bf16[2,384,768]{2,1,0:T(8,128)(2,1)S(1)} %get-tuple-element.29.back_ref, f32[384,128]{1,0:T(8,128)S(1)} %get-tuple-element.30.q_ref, bf16[2048,768]{1,0:T(8,128)(2,1)S(1)} %bitcast.23, ...), custom_call_target="tpu_custom_call" | custom-call | flops 3145728000 | bytes 8388608 | tf_op jit(solution)/shard_map/pallas_call | solution.py:325
  110.5 0.0 copy-start
  110.5 7.5 %all-to-all-start.2 = ((bf16[64,8,1664]{2,1,0:T(8,128)(2,1)}), bf16[64,8,1664]{2,1,0:T(8,128)(2,1)S(1)}, u32[]{:S(2)}, u32[]{:S(2)}) async-start(bf16[64,8,1664]{2,1,0:T(8,128)(2,1)} %bitcast.28), calls=%async_computation.2 | async-start | bytes 3407872 | tf_op jit(solution)/shard_map/all_to_all | solution.py:339
  118.0 1.6 collective-permute-start.9
  119.6 0.5 collective-permute-start.13
  120.1 1.5 collective-permute-start.15
  121.6 2.3 %collective-permute-start.16 = (bf16[384,512]{1,0:T(8,128)(2,1)}, bf16[384,512]{1,0:T(8,128)(2,1)S(1)}, u32[]{:S(2)}, u32[]{:S(2)}) collective-permute-start(bf16[384,512]{1,0:T(8,128)(2,1)} %get-tuple-element.45), channel_id=1, source_target_pairs={{0,128},{64,192},{128,0},{192,64},{1,129},{65,193},{129,1},{193,65... | collective-permute-start | bytes 1179656 | tf_op jit(solution)/shard_map/ppermute | solution.py:343
  124.0 0.9 collective-permute-start.11
  124.9 3.3 %collective-permute-done.9.refs_1_ = bf16[384,384]{1,0:T(8,128)(2,1)S(1)} collective-permute-done((bf16[384,384]{1,0:T(8,128)(2,1)}, bf16[384,384]{1,0:T(8,128)(2,1)S(1)}, u32[]{:S(2)}, u32[]{:S(2)}) %collective-permute-start.9) | collective-permute-done | bytes 294944 | tf_op jit(solution)/shard_map/ppermute | solution.py:343
  128.2 1.5 collective-permute-start.12
  129.7 7.7 %collective-permute-done.13.refs_7_ = bf16[384,384]{1,0:T(8,128)(2,1)S(1)} collective-permute-done((bf16[384,384]{1,0:T(8,128)(2,1)}, bf16[384,384]{1,0:T(8,128)(2,1)S(1)}, u32[]{:S(2)}, u32[]{:S(2)}) %collective-permute-start.13) | collective-permute-done | bytes 294944 | tf_op jit(solution)/shard_map/ppermute | solution.py:343
  137.4 0.4 collective-permute-start.17
  137.8 6.6 %collective-permute-done.11.refs_3_ = bf16[384,384]{1,0:T(8,128)(2,1)S(1)} collective-permute-done((bf16[384,384]{1,0:T(8,128)(2,1)}, bf16[384,384]{1,0:T(8,128)(2,1)S(1)}, u32[]{:S(2)}, u32[]{:S(2)}) %collective-permute-start.11) | collective-permute-done | bytes 294944 | tf_op jit(solution)/shard_map/ppermute | solution.py:343
  144.4 0.8 copy-done.17
  145.2 1.3 collective-permute-start
  146.5 4.9 %collective-permute-done.12.refs_5_ = bf16[384,384]{1,0:T(8,128)(2,1)S(1)} collective-permute-done((bf16[384,384]{1,0:T(8,128)(2,1)}, bf16[384,384]{1,0:T(8,128)(2,1)S(1)}, u32[]{:S(2)}, u32[]{:S(2)}) %collective-permute-start.12) | collective-permute-done | bytes 294944 | tf_op jit(solution)/shard_map/ppermute | solution.py:343
  151.4 0.8 copy-done.19
  152.2 1.7 collective-permute-start.3
  153.9 0.7 copy-done.2
  154.6 0.3 collective-permute-start.4
  154.9 0.8 copy-done.4
  155.7 1.7 collective-permute-start.5
  157.4 0.7 copy-done.6
  158.2 0.3 collective-permute-start.10
  158.5 0.7 copy-done.13
  159.2 13.3 %collective-permute-done.4.x1 = bf16[512,384]{1,0:T(8,128)(2,1)S(1)} collective-permute-done((bf16[512,384]{1,0:T(8,128)(2,1)}, bf16[512,384]{1,0:T(8,128)(2,1)S(1)}, u32[]{:S(2)}, u32[]{:S(2)}) %collective-permute-start.4) | collective-permute-done | bytes 393248 | tf_op jit(solution)/shard_map/ppermute | solution.py:343
  172.5 0.7 copy-done.9
  173.2 1.7 collective-permute-start.1
  174.9 0.7 copy-done.11
  175.7 1.2 collective-permute-start.2
  176.9 1.9 collective-permute-done.10.refs_2_
  178.8 0.7 copy-done.21
  179.5 1.1 collective-permute-start.14
  180.6 0.7 copy-done.15
  181.3 0.9 collective-permute-start.6
  182.3 1.4 collective-permute-start.7
  183.6 12.1 %collective-permute-done.14.refs_6_ = bf16[384,384]{1,0:T(8,128)(2,1)S(1)} collective-permute-done((bf16[384,384]{1,0:T(8,128)(2,1)S(1)}, bf16[384,384]{1,0:T(8,128)(2,1)S(1)}, u32[]{:S(2)}, u32[]{:S(2)}) %collective-permute-start.14) | collective-permute-done | bytes 294944 | tf_op jit(solution)/shard_map/ppermute | solution.py:343
  195.7 0.7 copy-done.23
  196.5 3.4 %collective-permute-start.8 = (bf16[512,384]{1,0:T(8,128)(2,1)}, bf16[512,384]{1,0:T(8,128)(2,1)}, u32[]{:S(2)}, u32[]{:S(2)}) collective-permute-start(bf16[512,384]{1,0:T(8,128)(2,1)} %get-tuple-element.38), channel_id=1, source_target_pairs={{0,128},{64,192},{128,0},{192,64},{1,129},{65,193},{129,1},{193,65... | collective-permute-start | bytes 1179656 | tf_op jit(solution)/shard_map/ppermute | solution.py:343
  199.8 0.1 copy.16.ids_ref
  199.9 1.0 copy-done.1
  200.9 1.0 copy-done.3
  201.9 1.0 copy-done.5
  202.9 1.0 copy-done.7
  203.9 1.0 copy-done.14
  204.9 1.0 copy-done.16
  205.8 1.0 copy-done.18
  206.8 1.0 copy-done.20
  207.8 1.0 copy-done.22
  208.7 1.0 copy-done.24
  209.7 3.8 %shard_map.155 = bf16[768,512]{1,0:T(8,128)(2,1)} custom-call(bf16[384,384]{1,0:T(8,128)(2,1)} %get-tuple-element.41.refs_0_, bf16[384,384]{1,0:T(8,128)(2,1)S(1)} %copy-done.14, bf16[384,384]{1,0:T(8,128)(2,1)S(1)} %copy-done.22, bf16[384,384]{1,0:T(8,128)(2,1)S(1)} %copy-done.18, bf16[384,384]{1,0:T(8,128)(2,1)} %get-tuple-element.42.refs_4_, ...), custom_call_target="tpu_custom_call" | custom-call | flops 1258291200 | bytes 8388608 | tf_op jit(solution)/shard_map/pallas_call | solution.py:325
  213.5 4.4 %shard_map.153.acc = f32[2,512,768]{2,1,0:T(8,128)S(1)} custom-call(bf16[384,768]{1,0:T(8,128)(2,1)S(1)} %copy-done, bf16[384,768]{1,0:T(8,128)(2,1)} %collective-permute-done.g1, bf16[384,768]{1,0:T(8,128)(2,1)} %collective-permute-done.1.g3, bf16[384,768]{1,0:T(8,128)(2,1)} %get-tuple-element.34.u0, bf16[384,768]{1,0:T(8,128)(2,1)} %collective-permute-done.2.u1, ...), custom_call_target="tpu_custom_call" | custom-call | flops 1887436800 | bytes 8388608 | tf_op jit(solution)/shard_map/pallas_call | solution.py:325
  217.9 0.0 copy-start.31
  218.0 2.9 %shard_map.154 = (bf16[512,768]{1,0:T(8,128)(2,1)}, bf16[512,768]{1,0:T(8,128)(2,1)}) custom-call(f32[2,512,768]{2,1,0:T(8,128)S(1)} %shard_map.153.acc, bf16[384,768]{1,0:T(8,128)(2,1)S(1)} %collective-permute-done.6.gate_b, bf16[384,768]{1,0:T(8,128)(2,1)S(1)} %collective-permute-done.7.up_b, bf16[512,384]{1,0:T(8,128)(2,1)} %collective-permute-done.8.x2), custom_call_target="tpu_custom_call" | custom-call | flops 629145600 | bytes 8388608 | tf_op jit(solution)/shard_map/pallas_call | solution.py:325
  220.8 2.0 shard_map.152
  (57 shorter events, 0.1 us)
Async XLA Ops:
  4.0 12.3 %copy-start.26 = (s32[128,2]{0,1:T(2,128)S(1)}, s32[128,2]{0,1:T(2,128)}, u32[]{:S(2)}) copy-start(s32[128,2]{0,1:T(2,128)} %param.14) | copy-start | bytes 3076
  4.0 12.3 %copy-start.29 = (bf16[128,2048]{1,0:T(8,128)(2,1)S(1)}, bf16[128,2048]{1,0:T(8,128)(2,1)}, u32[]{:S(2)}) copy-start(bf16[128,2048]{1,0:T(8,128)(2,1)} %x_ref.2) | copy-start | bytes 1572868
  4.0 12.3 %copy-start.30 = (bf16[128,2]{0,1:T(2,128)(2,1)S(1)}, bf16[128,2]{0,1:T(2,128)(2,1)}, u32[]{:S(2)}) copy-start(bf16[128,2]{0,1:T(2,128)(2,1)} %param.13) | copy-start | bytes 1540
  4.0 50.7 %all-to-all-start.1 = ((bf16[64,24,512]{2,1,0:T(8,128)(2,1)}), bf16[64,24,512]{2,1,0:T(8,128)(2,1)S(1)}, u32[]{:S(2)}, u32[]{:S(2)}) async-start(bf16[64,24,512]{2,1,0:T(8,128)(2,1)} %bitcast.30), calls=%async_computation.1 | async-start | bytes 3145728 | tf_op jit(solution)/shard_map/all_to_all | solution.py:339
  18.6 43.5 %copy-start.25 = (bf16[192,192]{1,0:T(8,128)(2,1)S(1)}, bf16[192,192]{1,0:T(8,128)(2,1)}, u32[]{:S(2)}) copy-start(bf16[192,192]{1,0:T(8,128)(2,1)} %constant.14.clone.perm_ref) | copy-start | bytes 221188
  54.7 45.9 %all-to-all-start = ((bf16[64,24,512]{2,1,0:T(8,128)(2,1)}), bf16[64,24,512]{2,1,0:T(8,128)(2,1)S(1)}, u32[]{:S(2)}, u32[]{:S(2)}) async-start(bf16[64,24,512]{2,1,0:T(8,128)(2,1)} %bitcast.29), calls=%async_computation | async-start | bytes 3145728 | tf_op jit(solution)/shard_map/all_to_all | solution.py:339
  100.5 5.8 %copy-start.27 = (bf16[1,2048,768]{2,1,0:T(8,128)(2,1)S(1)}, bf16[1,2048,768]{2,1,0:T(8,128)(2,1)}, u32[]{:S(2)}) copy-start(bf16[1,2048,768]{2,1,0:T(8,128)(2,1)} %param.15) | copy-start | bytes 9437188
  100.5 5.8 %copy-start.28 = (bf16[1,2048,768]{2,1,0:T(8,128)(2,1)S(1)}, bf16[1,2048,768]{2,1,0:T(8,128)(2,1)}, u32[]{:S(2)}) copy-start(bf16[1,2048,768]{2,1,0:T(8,128)(2,1)} %param.16) | copy-start | bytes 9437188
  100.5 5.8 %copy-start.32 = (bf16[192,192]{1,0:T(8,128)(2,1)S(1)}, bf16[192,192]{1,0:T(8,128)(2,1)}, u32[]{:S(2)}) copy-start(bf16[192,192]{1,0:T(8,128)(2,1)} %constant.15.clone.pack_ref) | copy-start | bytes 221188
  100.5 5.9 %copy-start.33 = (bf16[64,48]{1,0:T(8,128)(2,1)S(1)}, bf16[64,48]{1,0:T(8,128)(2,1)}, u32[]{:S(2)}) copy-start(bf16[64,48]{1,0:T(8,128)(2,1)} %constant.17.clone.probs_ref) | copy-start | bytes 18436
  110.5 34.7 %copy-start = (bf16[384,768]{1,0:T(8,128)(2,1)S(1)}, bf16[384,768]{1,0:T(8,128)(2,1)}, u32[]{:S(2)}) copy-start(bf16[384,768]{1,0:T(8,128)(2,1)} %get-tuple-element.33.g0) | copy-start | bytes 1769476
  110.5 110.4 %all-to-all-start.2 = ((bf16[64,8,1664]{2,1,0:T(8,128)(2,1)}), bf16[64,8,1664]{2,1,0:T(8,128)(2,1)S(1)}, u32[]{:S(2)}, u32[]{:S(2)}) async-start(bf16[64,8,1664]{2,1,0:T(8,128)(2,1)} %bitcast.28), calls=%async_computation.2 | async-start | bytes 3407872 | tf_op jit(solution)/shard_map/all_to_all | solution.py:339
  118.0 10.2 %collective-permute-start.9 = (bf16[384,384]{1,0:T(8,128)(2,1)}, bf16[384,384]{1,0:T(8,128)(2,1)S(1)}, u32[]{:S(2)}, u32[]{:S(2)}) collective-permute-start(bf16[384,384]{1,0:T(8,128)(2,1)} %get-tuple-element.41.refs_0_), channel_id=1, source_target_pairs={{0,64},{64,128},{128,192},{192,0},{1,65},{65,129},{129,193},{193,1... | collective-permute-start | bytes 884744 | tf_op jit(solution)/shard_map/ppermute | solution.py:343
  119.6 17.8 %collective-permute-start.13 = (bf16[384,384]{1,0:T(8,128)(2,1)}, bf16[384,384]{1,0:T(8,128)(2,1)S(1)}, u32[]{:S(2)}, u32[]{:S(2)}) collective-permute-start(bf16[384,384]{1,0:T(8,128)(2,1)} %get-tuple-element.42.refs_4_), channel_id=1, source_target_pairs={{0,192},{64,0},{128,64},{192,128},{1,193},{65,1},{129,65},{193,129... | collective-permute-start | bytes 884744 | tf_op jit(solution)/shard_map/ppermute | solution.py:343
  120.1 33.8 %collective-permute-start.15 = (bf16[384,512]{1,0:T(8,128)(2,1)}, bf16[384,512]{1,0:T(8,128)(2,1)S(1)}, u32[]{:S(2)}, u32[]{:S(2)}) collective-permute-start(bf16[384,512]{1,0:T(8,128)(2,1)} %get-tuple-element.44), channel_id=1, source_target_pairs={{0,64},{64,128},{128,192},{192,0},{1,65},{65,129},{129,193},{193,1... | collective-permute-start | bytes 1179656 | tf_op jit(solution)/shard_map/ppermute | solution.py:343
  121.6 33.3 %collective-permute-start.16 = (bf16[384,512]{1,0:T(8,128)(2,1)}, bf16[384,512]{1,0:T(8,128)(2,1)S(1)}, u32[]{:S(2)}, u32[]{:S(2)}) collective-permute-start(bf16[384,512]{1,0:T(8,128)(2,1)} %get-tuple-element.45), channel_id=1, source_target_pairs={{0,128},{64,192},{128,0},{192,64},{1,129},{65,193},{129,1},{193,65... | collective-permute-start | bytes 1179656 | tf_op jit(solution)/shard_map/ppermute | solution.py:343
  124.0 20.5 %collective-permute-start.11 = (bf16[384,384]{1,0:T(8,128)(2,1)}, bf16[384,384]{1,0:T(8,128)(2,1)S(1)}, u32[]{:S(2)}, u32[]{:S(2)}) collective-permute-start(bf16[384,384]{1,0:T(8,128)(2,1)} %get-tuple-element.41.refs_0_), channel_id=1, source_target_pairs={{0,192},{64,0},{128,64},{192,128},{1,193},{65,1},{129,65},{193,129... | collective-permute-start | bytes 884744 | tf_op jit(solution)/shard_map/ppermute | solution.py:343
  128.2 23.2 %collective-permute-start.12 = (bf16[384,384]{1,0:T(8,128)(2,1)}, bf16[384,384]{1,0:T(8,128)(2,1)S(1)}, u32[]{:S(2)}, u32[]{:S(2)}) collective-permute-start(bf16[384,384]{1,0:T(8,128)(2,1)} %get-tuple-element.42.refs_4_), channel_id=1, source_target_pairs={{0,64},{64,128},{128,192},{192,0},{1,65},{65,129},{129,193},{193,1... | collective-permute-start | bytes 884744 | tf_op jit(solution)/shard_map/ppermute | solution.py:343
  137.4 20.0 %collective-permute-start.17 = (bf16[384,512]{1,0:T(8,128)(2,1)}, bf16[384,512]{1,0:T(8,128)(2,1)S(1)}, u32[]{:S(2)}, u32[]{:S(2)}) collective-permute-start(bf16[384,512]{1,0:T(8,128)(2,1)} %get-tuple-element.46), channel_id=1, source_target_pairs={{0,192},{64,0},{128,64},{192,128},{1,193},{65,1},{129,65},{193,129... | collective-permute-start | bytes 1179656 | tf_op jit(solution)/shard_map/ppermute | solution.py:343
  144.4 0.8 copy-start.17
  145.2 36.1 %collective-permute-start = (bf16[384,768]{1,0:T(8,128)(2,1)S(1)}, bf16[384,768]{1,0:T(8,128)(2,1)}, u32[]{:S(2)}, u32[]{:S(2)}) collective-permute-start(bf16[384,768]{1,0:T(8,128)(2,1)S(1)} %copy-done), channel_id=1, source_target_pairs={{0,64},{64,128},{128,192},{192,0},{1,65},{65,129},{129,193},{193,1... | collective-permute-start | bytes 1769480 | tf_op jit(solution)/shard_map/ppermute | solution.py:343
  151.4 0.8 copy-start.19
  152.2 30.1 %collective-permute-start.3 = (bf16[384,768]{1,0:T(8,128)(2,1)}, bf16[384,768]{1,0:T(8,128)(2,1)}, u32[]{:S(2)}, u32[]{:S(2)}) collective-permute-start(bf16[384,768]{1,0:T(8,128)(2,1)} %get-tuple-element.34.u0), channel_id=1, source_target_pairs={{0,192},{64,0},{128,64},{192,128},{1,193},{65,1},{129,65},{193,129... | collective-permute-start | bytes 1769480 | tf_op jit(solution)/shard_map/ppermute | solution.py:343
  153.9 0.7 copy-start.2
  154.6 17.8 %collective-permute-start.4 = (bf16[512,384]{1,0:T(8,128)(2,1)}, bf16[512,384]{1,0:T(8,128)(2,1)S(1)}, u32[]{:S(2)}, u32[]{:S(2)}) collective-permute-start(bf16[512,384]{1,0:T(8,128)(2,1)} %get-tuple-element.36), channel_id=1, source_target_pairs={{0,64},{64,128},{128,192},{192,0},{1,65},{65,129},{129,193},{193,1... | collective-permute-start | bytes 1179656 | tf_op jit(solution)/shard_map/ppermute | solution.py:343
  154.9 0.8 copy-start.4
  155.7 19.2 %collective-permute-start.5 = (bf16[512,384]{1,0:T(8,128)(2,1)}, bf16[512,384]{1,0:T(8,128)(2,1)S(1)}, u32[]{:S(2)}, u32[]{:S(2)}) collective-permute-start(bf16[512,384]{1,0:T(8,128)(2,1)} %get-tuple-element.37), channel_id=1, source_target_pairs={{0,192},{64,0},{128,64},{192,128},{1,193},{65,1},{129,65},{193,129... | collective-permute-start | bytes 1179656 | tf_op jit(solution)/shard_map/ppermute | solution.py:343
  157.4 0.7 copy-start.6
  158.2 20.6 %collective-permute-start.10 = (bf16[384,384]{1,0:T(8,128)(2,1)S(1)}, bf16[384,384]{1,0:T(8,128)(2,1)S(1)}, u32[]{:S(2)}, u32[]{:S(2)}) collective-permute-start(bf16[384,384]{1,0:T(8,128)(2,1)S(1)} %collective-permute-done.9.refs_1_), channel_id=1, source_target_pairs={{0,64},{64,128},{128,192},{192,0},{1,65},{65,129},{129,193},{193,1... | collective-permute-start | bytes 884744 | tf_op jit(solution)/shard_map/ppermute | solution.py:343
  158.5 0.7 copy-start.13
  172.5 0.7 copy-start.9
  173.2 40.3 %collective-permute-start.1 = (bf16[384,768]{1,0:T(8,128)(2,1)S(1)}, bf16[384,768]{1,0:T(8,128)(2,1)}, u32[]{:S(2)}, u32[]{:S(2)}) collective-permute-start(bf16[384,768]{1,0:T(8,128)(2,1)S(1)} %copy-done), channel_id=1, source_target_pairs={{0,192},{64,0},{128,64},{192,128},{1,193},{65,1},{129,65},{193,129... | collective-permute-start | bytes 1769480 | tf_op jit(solution)/shard_map/ppermute | solution.py:343
  174.9 0.7 copy-start.11
  175.7 37.8 %collective-permute-start.2 = (bf16[384,768]{1,0:T(8,128)(2,1)}, bf16[384,768]{1,0:T(8,128)(2,1)}, u32[]{:S(2)}, u32[]{:S(2)}) collective-permute-start(bf16[384,768]{1,0:T(8,128)(2,1)} %get-tuple-element.34.u0), channel_id=1, source_target_pairs={{0,64},{64,128},{128,192},{192,0},{1,65},{65,129},{129,193},{193,1... | collective-permute-start | bytes 1769480 | tf_op jit(solution)/shard_map/ppermute | solution.py:343
  178.8 0.7 copy-start.21
  179.5 16.2 %collective-permute-start.14 = (bf16[384,384]{1,0:T(8,128)(2,1)S(1)}, bf16[384,384]{1,0:T(8,128)(2,1)S(1)}, u32[]{:S(2)}, u32[]{:S(2)}) collective-permute-start(bf16[384,384]{1,0:T(8,128)(2,1)S(1)} %collective-permute-done.13.refs_7_), channel_id=1, source_target_pairs={{0,192},{64,0},{128,64},{192,128},{1,193},{65,1},{129,65},{193,129... | collective-permute-start | bytes 884744 | tf_op jit(solution)/shard_map/ppermute | solution.py:343
  180.6 0.7 copy-start.15
  181.3 36.6 %collective-permute-start.6 = (bf16[384,768]{1,0:T(8,128)(2,1)}, bf16[384,768]{1,0:T(8,128)(2,1)S(1)}, u32[]{:S(2)}, u32[]{:S(2)}) collective-permute-start(bf16[384,768]{1,0:T(8,128)(2,1)} %collective-permute-done.g1), channel_id=1, source_target_pairs={{0,64},{64,128},{128,192},{192,0},{1,65},{65,129},{129,193},{193,1... | collective-permute-start | bytes 1769480 | tf_op jit(solution)/shard_map/ppermute | solution.py:343
  182.3 35.7 %collective-permute-start.7 = (bf16[384,768]{1,0:T(8,128)(2,1)}, bf16[384,768]{1,0:T(8,128)(2,1)S(1)}, u32[]{:S(2)}, u32[]{:S(2)}) collective-permute-start(bf16[384,768]{1,0:T(8,128)(2,1)} %collective-permute-done.3.u3), channel_id=1, source_target_pairs={{0,192},{64,0},{128,64},{192,128},{1,193},{65,1},{129,65},{193,129... | collective-permute-start | bytes 1769480 | tf_op jit(solution)/shard_map/ppermute | solution.py:343
  195.7 0.7 copy-start.23
  196.5 21.5 %collective-permute-start.8 = (bf16[512,384]{1,0:T(8,128)(2,1)}, bf16[512,384]{1,0:T(8,128)(2,1)}, u32[]{:S(2)}, u32[]{:S(2)}) collective-permute-start(bf16[512,384]{1,0:T(8,128)(2,1)} %get-tuple-element.38), channel_id=1, source_target_pairs={{0,128},{64,192},{128,0},{192,64},{1,129},{65,193},{129,1},{193,65... | collective-permute-start | bytes 1179656 | tf_op jit(solution)/shard_map/ppermute | solution.py:343
  199.9 1.0 copy-start.1
  200.9 1.0 copy-start.3
  201.9 1.0 copy-start.5
  202.9 1.0 copy-start.7
  203.9 1.0 copy-start.14
  204.9 1.0 copy-start.16
  205.8 1.0 copy-start.18
  206.8 1.0 copy-start.20
  207.8 1.0 copy-start.22
  208.7 1.0 copy-start.24
  209.7 3.8 %copy-start.8 = (bf16[512,384]{1,0:T(8,128)(2,1)S(1)}, bf16[512,384]{1,0:T(8,128)(2,1)}, u32[]{:S(2)}) copy-start(bf16[512,384]{1,0:T(8,128)(2,1)} %get-tuple-element.35.x0) | copy-start | bytes 1179652
  209.7 3.8 %copy-start.10 = (bf16[512,384]{1,0:T(8,128)(2,1)S(1)}, bf16[512,384]{1,0:T(8,128)(2,1)}, u32[]{:S(2)}) copy-start(bf16[512,384]{1,0:T(8,128)(2,1)} %copy-done.9) | copy-start | bytes 1179652
  209.7 3.8 %copy-start.12 = (bf16[512,384]{1,0:T(8,128)(2,1)S(1)}, bf16[512,384]{1,0:T(8,128)(2,1)}, u32[]{:S(2)}) copy-start(bf16[512,384]{1,0:T(8,128)(2,1)} %copy-done.11) | copy-start | bytes 1179652
  217.9 2.9 %copy-start.31 = (bf16[192,192]{1,0:T(8,128)(2,1)S(1)}, bf16[192,192]{1,0:T(8,128)(2,1)}, u32[]{:S(2)}) copy-start(bf16[192,192]{1,0:T(8,128)(2,1)} %constant.16.clone.perm_ref) | copy-start | bytes 221188

commit v5 on v4

--- a/solution.py
+++ b/solution.py
@@ -135,6 +135,24 @@
         ref[...] = rows[which].astype(F32).T.astype(BF16)
 
 
+def scaled_kernel(dp_ref, perm_ref, got_ref, s0, s1, s2, s3, rows, sems):
+    @pl.loop(0, NGROUP)
+    def _(g):
+        source = pl.ds(pl.multiple_of(g * GROUP * SPAN, 64), GROUP * SPAN)
+        target = pl.ds(pl.multiple_of(g * GROWS, 16), GROWS)
+        part = mm(perm_ref[...], got_ref[source, :]).astype(BF16)
+        for s in range(NSEG):
+            rows[s, target, :] = part[s * GROWS : (s + 1) * GROWS]
+
+    copies = []
+    for k, ref in enumerate((s1, s3, s2, s0)):
+        which = lax.rem(dp_ref[0] + (1, 3, 2, 0)[k], DP)
+        copies.append(pltpu.make_async_copy(rows.at[which], ref, sems.at[k]))
+        copies[-1].start()
+    for copy in copies:
+        copy.wait()
+
+
 def forward_kernel(
     rows, gate_hbm, up_hbm, gate_ref, up_ref, hidden_low, hidden_high, gate_w, up_w, sems
 ):
@@ -159,8 +177,8 @@
 
 
 def backward_kernel(
-    dp_ref, perm_ref, got_ref, down_hbm, gate_hbm, up_hbm,
-    back_ref, q_ref, gate_out, up_out, s0, s1, s2, s3, rows, down_w, gate_ref, up_ref, sems, loads,
+    perm_ref, got_ref, down_hbm, gate_hbm, up_hbm,
+    back_ref, q_ref, gate_out, up_out, rows, down_w, gate_ref, up_ref, sems, loads,
 ):
     arriving = []
     for i in range(NFB):
@@ -175,9 +193,6 @@
             arriving[-1].start()
     unmix_rows(perm_ref, got_ref, rows)
     copies = []
-    for k, ref in enumerate((s0, s1, s2, s3)):
-        which = lax.rem(dp_ref[0] + k, DP)
-        copies.append(pltpu.make_async_copy(rows.at[which], ref, sems.at[k]))
     total = jnp.zeros((ROWS, 1), F32)
     for i in range(NFB):
         at = slice(i * FB, (i + 1) * FB)
@@ -192,14 +207,11 @@
         back_ref[0, :, at] = (back_hidden * up * sig * (1.0 + gate * (1.0 - sig))).astype(BF16)
         back_ref[1, :, at] = (back_hidden * activated).astype(BF16)
         total += jnp.sum(hidden * back_hidden, axis=1, keepdims=True)
-        if i == 0:
-            for copy in copies:
-                copy.start()
         for m, ref in enumerate((gate_out, up_out)):
             part = pl.ds(i * FB, FB)
             copies.append(
                 pltpu.make_async_copy(
-                    back_ref.at[m, :, part], ref.at[:, part], sems.at[DP + 2 * i + m]
+                    back_ref.at[m, :, part], ref.at[:, part], sems.at[2 * i + m]
                 )
             )
             copies[-1].start()
@@ -245,11 +257,28 @@
         copy.wait()
 
 
-def combine_kernel(ids_ref, ids_t_ref, prob_ref, perm_ref, got_ref, tok_ref, gprob_ref, rows):
+def load(sources, targets, sems):
+    copies = [
+        pltpu.make_async_copy(a, b, sems.at[i]) for i, (a, b) in enumerate(zip(sources, targets))
+    ]
+    for copy in copies:
+        copy.start()
+    return copies
+
+
+def combine_kernel(
+    ids_ref, ids_t_ref, prob_ref, perm_ref, got_hbm, tok_ref, gprob_ref, rows, got_ref, sems
+):
+    height = GROUP * BROWS
+    blocks = [pl.ds(g * height, height) for g in range(NGROUP)]
+    copies = load([got_hbm.at[b] for b in blocks], [got_ref.at[b] for b in blocks], sems)
+    at = [target * PER + slot for target, slot in places_in_rows(ids_ref)]
+    columns = iota((TOK, ROWS), 1)
+    pick = jnp.where((columns == at[0]) | (columns == at[1]), 1.0, 0.0).astype(BF16)
     perm = perm_ref[...]
-    height = GROUP * BROWS
     for g in range(NGROUP):
         top = g * height
+        copies[g].wait()
         stacked = jnp.concatenate(
             [
                 jnp.concatenate(
@@ -270,9 +299,6 @@
                 rows[g * GROWS : (g + 1) * GROWS, col : col + TILE] = part[
                     v * GROWS : (v + 1) * GROWS, u * TILE : (u + 1) * TILE
                 ]
-    at = [target * PER + slot for target, slot in places_in_rows(ids_ref)]
-    columns = iota((TOK, ROWS), 1)
-    pick = jnp.where((columns == at[0]) | (columns == at[1]), 1.0, 0.0).astype(BF16)
     tok_ref[...] = mm(pick, rows[...]).astype(BF16)
     home = got_ref[:, 3 * NU * TILE :].astype(F32)
     line = iota((N * BROWS, TOK), 0)
@@ -283,22 +309,61 @@
 
 
 def down_grad_kernel(*refs):
-    out_ref = refs[-1]
-    pieces = refs[2 * DP : 3 * DP]
+    low, high, pieces = refs[:DP], refs[DP : 2 * DP], refs[2 * DP : 3 * DP]
+    out_ref, lows, highs, cols, acc, sems = refs[3 * DP :]
     half = FF // 2
-    for m in range(2):
-        acc = sum(mm(refs[m * DP + k][...], pieces[k][...]) for k in range(DP))
-        out_ref[m * half : (m + 1) * half] = acc.astype(BF16)
-
-
-def grad_first_kernel(g0, g1, g3, u0, u1, u3, x0, x1, x3, acc):
-    acc[0] = mm(x0[...], g0[...]) + mm(x1[...], g1[...]) + mm(x3[...], g3[...])
-    acc[1] = mm(x0[...], u0[...]) + mm(x1[...], u1[...]) + mm(x3[...], u3[...])
-
-
-def grad_last_kernel(acc, gate_b, up_b, x2, gate_out, up_out):
-    gate_out[...] = (acc[0] + mm(x2[...], gate_b[...])).astype(BF16)
-    up_out[...] = (acc[1] + mm(x2[...], up_b[...])).astype(BF16)
+    order = (0, 1, 3, 2)
+    copies = load(
+        [r[k] for k in order for r in (pieces, low, high)],
+        [r.at[k] for k in order for r in (cols, lows, highs)],
+        sems,
+    )
+    for i, k in enumerate(order):
+        for copy in copies[3 * i : 3 * i + 3]:
+            copy.wait()
+        for m, part in enumerate((lows, highs)):
+            at = slice(m * half, (m + 1) * half)
+            term = mm(part[k], cols[k])
+            if i == 0:
+                acc[at] = term
+            elif i < DP - 1:
+                acc[at] = acc[at] + term
+            else:
+                out_ref[at] = (acc[at] + term).astype(BF16)
+
+
+def grad_first_kernel(*refs):
+    acc, gates, ups, cols, sems = refs[9:]
+    copies = load(
+        [refs[3 * m + k] for k in range(3) for m in (2, 0, 1)],
+        [r.at[k] for k in range(3) for r in (cols, gates, ups)],
+        sems,
+    )
+    for k in range(3):
+        for copy in copies[3 * k : 3 * k + 3]:
+            copy.wait()
+        for m, part in enumerate((gates, ups)):
+            term = mm(cols[k], part[k])
+            acc[m] = term if k == 0 else acc[m] + term
+
+
+def grad_last_kernel(acc, gate_b, up_b, x2, gate_out, up_out, col, parts, sent, sems, out_sems):
+    copies = load((x2, gate_b, up_b), (col, parts.at[0], parts.at[1]), sems)
+    copies[0].wait()
+    sends = []
+    half = SEG // 2
+    for m, out in enumerate((gate_out, up_out)):
+        copies[1 + m].wait()
+        for h in range(2):
+            at = slice(h * half, (h + 1) * half)
+            sent[m, at] = (acc[m, at] + mm(col[at], parts[m])).astype(BF16)
+            rows = pl.ds(h * half, half)
+            sends.append(
+                pltpu.make_async_copy(sent.at[m, rows], out.at[rows], out_sems.at[2 * m + h])
+            )
+            sends[-1].start()
+    for copy in sends:
+        copy.wait()
 
 
 def shape(dims, kind=BF16):
@@ -391,22 +456,26 @@
     )(in_vmem(rows), in_hbm(gate_weight[0]), in_hbm(up_weight[0]))
     h_low, h_high = around(hidden_low, hidden_high)
 
-    back_near, q, back_gate, back_up, *s_pieces = call(
+    back_near, q, back_gate, back_up = call(
         backward_kernel,
         [near((2, ROWS, FF)), near((ROWS, TILE), F32)]
-        + [shape((ROWS, FF))] * 2
-        + [shape((ROWS, SEG))] * DP,
+        + [shape((ROWS, FF))] * 2,
         scratch=[
             pltpu.VMEM((NSEG, ROWS, SEG), BF16),
             pltpu.VMEM((FF, D), BF16),
             pltpu.VMEM((ROWS, FF), BF16),
             pltpu.VMEM((ROWS, FF), BF16),
-            pltpu.SemaphoreType.DMA((DP + 2 * NFB,)),
+            pltpu.SemaphoreType.DMA((2 * NFB,)),
             pltpu.SemaphoreType.DMA((3 * NFB,)),
         ],
-        scalars=1, far=(3, 4, 5), by_hand=(2, 3, 4, 5, 6, 7), flops=2000 << 20,
-    )(dp, unmix, got_c, in_hbm(down_weight[0]), in_hbm(gate), in_hbm(up))
+        far=(2, 3, 4), by_hand=(2, 3), flops=2000 << 20,
+    )(unmix, got_c, in_hbm(down_weight[0]), in_hbm(gate), in_hbm(up))
     b_gate, b_up = around(back_gate, back_up)
+    s_pieces = call(
+        scaled_kernel, [shape((ROWS, SEG))] * DP,
+        scratch=[pltpu.VMEM((NSEG, ROWS, SEG), BF16), pltpu.SemaphoreType.DMA((DP,))],
+        scalars=1, by_hand=(0, 1, 2, 3), flops=300 << 20,
+    )(dp, unmix, got_c)
     s_pieces = spread(s_pieces)
 
     (send_b,) = call(
@@ -420,19 +489,47 @@
     )(pack, probs_perm, in_vmem(back_near), in_vmem(q), in_vmem(gate_weight[0]), in_vmem(up_weight[0]))
     got_b = exchange(send_b.reshape(N, BROWS, BCOLS)).reshape(N * BROWS, BCOLS)
 
-    (acc,) = call(grad_first_kernel, [near((2, SEG, FF), F32)], flops=1800 << 20)(
-        *(b[k] for b in (b_gate, b_up, x_pieces) for k in (0, 1, 3))
-    )
-    (grad_down,) = call(down_grad_kernel, [shape((FF, SEG))], flops=1200 << 20)(
-        *h_low, *h_high, *s_pieces
-    )
-    grad_gate, grad_up = call(grad_last_kernel, [shape((SEG, FF))] * 2, flops=600 << 20)(
-        in_vmem(acc), b_gate[2], b_up[2], x_pieces[2]
-    )
+    (acc,) = call(
+        grad_first_kernel, [near((2, SEG, FF), F32)],
+        scratch=[
+            pltpu.VMEM((3, ROWS, FF), BF16),
+            pltpu.VMEM((3, ROWS, FF), BF16),
+            pltpu.VMEM((3, SEG, ROWS), BF16),
+            pltpu.SemaphoreType.DMA((9,)),
+        ],
+        far=range(9), flops=1800 << 20,
+    )(*(b[k] for b in (b_gate, b_up, x_pieces) for k in (0, 1, 3)))
+    (grad_down,) = call(
+        down_grad_kernel, [shape((FF, SEG))],
+        scratch=[
+            pltpu.VMEM((DP, FF // 2, ROWS), BF16),
+            pltpu.VMEM((DP, FF // 2, ROWS), BF16),
+            pltpu.VMEM((DP, ROWS, SEG), BF16),
+            pltpu.VMEM((FF, SEG), F32),
+            pltpu.SemaphoreType.DMA((3 * DP,)),
+        ],
+        far=range(3 * DP), flops=1200 << 20,
+    )(*h_low, *h_high, *s_pieces)
+    grad_gate, grad_up = call(
+        grad_last_kernel, [shape((SEG, FF))] * 2,
+        scratch=[
+            pltpu.VMEM((SEG, ROWS), BF16),
+            pltpu.VMEM((2, ROWS, FF), BF16),
+            pltpu.VMEM((2, SEG, FF), BF16),
+            pltpu.SemaphoreType.DMA((3,)),
+            pltpu.SemaphoreType.DMA((4,)),
+        ],
+        far=(1, 2, 3), by_hand=(0, 1), flops=600 << 20,
+    )(in_vmem(acc), b_gate[2], b_up[2], x_pieces[2])
     grad_tokens, grad_probs = call(
         combine_kernel, [shape((TOK, D)), shape((2, TOK))],
-        scratch=[pltpu.VMEM((ROWS, D), BF16)], flops=1000 << 20,
-    )(expert_ids, ids_t, probs_t, unpack, got_b)
+        scratch=[
+            pltpu.VMEM((ROWS, D), BF16),
+            pltpu.VMEM((N * BROWS, BCOLS), BF16),
+            pltpu.SemaphoreType.DMA((NGROUP,)),
+        ],
+        far=(4,), flops=1000 << 20,
+    )(in_hbm(expert_ids), in_hbm(ids_t), in_hbm(probs_t), in_hbm(unpack), got_b)
     return grad_tokens, grad_probs.T, grad_gate[None], grad_up[None], grad_down[None]
 
 

time: 224 us -> 231 us (1.031)
  waiting for transfers between devices: 116 us -> 108 us
  Pallas kernels: 37.3 us -> 44.5 us
  starting transfers between devices: 50.8 us -> 56.3 us
  local copies, waits for them, and re-layouts: 18.1 us -> 20.6 us
    ppermute x18, waiting for transfers between devices: 49.9 us -> 41.8 us  [shift(): return lax.ppermute(values, 'dp', [(i, (i + k) % DP) for i in range(DP)])]
    pallas_call x10 -> x11, Pallas kernels: 37.3 us -> 44.5 us  [run(): pl.pallas_call(kernel, in_specs=[pl.BlockSpec(memory_space=v) for v in sp...]
    ppermute x18, starting transfers between devices: 23.7 us -> 29.2 us  [shift(): return lax.ppermute(values, 'dp', [(i, (i + k) % DP) for i in range(DP)])]
    unnamed x69 -> x73, local copies, waits for them, and re-layouts: 18.1 us -> 20.6 us
  transfers between devices with their start and end apart: 21 -> 21, of which waited for: 9 -> 8; matrix products, arithmetic and copies ran while one was open for 0% -> 0% of each run, Pallas kernels for 10% -> 11%
where the time goes in v5:
time: 231 us; the launch traced here: 230 us
  waiting for transfers between devices  108 us (47%)
  starting transfers between devices  56.3 us (24%)
  Pallas kernels  44.5 us (19%)
  local copies, waits for them, and re-layouts  20.6 us (9%)
    all_to_all x3, waiting for transfers between devices, exchange(): lax.all_to_all(values, 'expert', split_axis=0, concat_axis=0, tiled=True)  65.8 us
    pallas_call x11, Pallas kernels, run(): pl.pallas_call(kernel, in_specs=[pl.BlockSpec(memory_space=v) for v in sp...  44.5 us
    ppermute x18, waiting for transfers between devices, shift(): return lax.ppermute(values, 'dp', [(i, (i + k) % DP) for i in range(DP)])  41.8 us
    ppermute x18, starting transfers between devices, shift(): return lax.ppermute(values, 'dp', [(i, (i + k) % DP) for i in range(DP)])  29.2 us
    all_to_all x3, starting transfers between devices, exchange(): lax.all_to_all(values, 'expert', split_axis=0, concat_axis=0, tiled=True)  27 us
    unnamed x73, local copies, waits for them, and re-layouts  20.6 us
  transfers between devices with their start and end apart: 21, of which 8 were waited for; matrix products, arithmetic and copies ran while one was open for 0% of the time, Pallas kernels for 11%

profile of v5, /device:TPU:10, one launch (start us, length us, event | category | flops | bytes accessed | tf_op | source)
XLA Modules:
  0.0 230.0 jit_solution(14214112511905456213)
XLA Ops:
  0.6 3.3 %shard_map.147 = bf16[1536,512]{1,0:T(8,128)(2,1)} custom-call(s32[2,128]{1,0:T(2,128)} %bitcast.20, bf16[128,2048]{1,0:T(8,128)(2,1)} %x_ref.3), custom_call_target="tpu_custom_call" | custom-call | flops 838860800 | bytes 8388608 | tf_op jit(solution)/shard_map/pallas_call | solution.py:390
  4.0 12.2 %all-to-all-start.1 = ((bf16[64,24,512]{2,1,0:T(8,128)(2,1)}), bf16[64,24,512]{2,1,0:T(8,128)(2,1)S(1)}, u32[]{:S(2)}, u32[]{:S(2)}) async-start(bf16[64,24,512]{2,1,0:T(8,128)(2,1)} %bitcast.31), calls=%async_computation.1 | async-start | bytes 3145728 | tf_op jit(solution)/shard_map/all_to_all | solution.py:404
  16.2 2.3 %shard_map.146 = bf16[1536,512]{1,0:T(8,128)(2,1)} custom-call(s32[2,128]{1,0:T(2,128)S(1)} %bitcast.22, bf16[2,128]{1,0:T(2,128)(2,1)S(1)} %bitcast.28, bf16[128,2048]{1,0:T(8,128)(2,1)S(1)} %copy-done.32), custom_call_target="tpu_custom_call" | custom-call | flops 838860800 | bytes 8388608 | tf_op jit(solution)/shard_map/pallas_call | solution.py:390
  18.6 36.1 %all-to-all-done.1 = bf16[64,24,512]{2,1,0:T(8,128)(2,1)S(1)} async-done(((bf16[64,24,512]{2,1,0:T(8,128)(2,1)}), bf16[64,24,512]{2,1,0:T(8,128)(2,1)S(1)}, u32[]{:S(2)}, u32[]{:S(2)}) %all-to-all-start.1) | async-done | bytes 1572896 | tf_op jit(solution)/shard_map/all_to_all | solution.py:404
  54.7 7.4 %all-to-all-start = ((bf16[64,24,512]{2,1,0:T(8,128)(2,1)}), bf16[64,24,512]{2,1,0:T(8,128)(2,1)S(1)}, u32[]{:S(2)}, u32[]{:S(2)}) async-start(bf16[64,24,512]{2,1,0:T(8,128)(2,1)} %bitcast.30), calls=%async_computation | async-start | bytes 3145728 | tf_op jit(solution)/shard_map/all_to_all | solution.py:404
  62.1 2.1 shard_map.148
  64.2 6.6 %shard_map.149 = (bf16[384,768]{1,0:T(8,128)(2,1)}, bf16[384,768]{1,0:T(8,128)(2,1)}, bf16[384,384]{1,0:T(8,128)(2,1)}, bf16[384,384]{1,0:T(8,128)(2,1)}) custom-call(bf16[4,384,512]{2,1,0:T(8,128)(2,1)S(1)} %get-tuple-element.26.rows, bf16[2048,768]{1,0:T(8,128)(2,1)} %bitcast.23, bf16[2048,768]{1,0:T(8,128)(2,1)} %bitcast.25), custom_call_target="tpu_custom_call" | custom-call | flops 3145728000 | bytes 8388608 | tf_op jit(solution)/shard_map/pallas_call | solution.py:390
  70.9 29.7 %all-to-all-done = bf16[64,24,512]{2,1,0:T(8,128)(2,1)S(1)} async-done(((bf16[64,24,512]{2,1,0:T(8,128)(2,1)}), bf16[64,24,512]{2,1,0:T(8,128)(2,1)S(1)}, u32[]{:S(2)}, u32[]{:S(2)}) %all-to-all-start) | async-done | bytes 1572896 | tf_op jit(solution)/shard_map/all_to_all | solution.py:404
  100.6 5.8 %shard_map.150 = (bf16[2,384,768]{2,1,0:T(8,128)(2,1)S(1)}, f32[384,128]{1,0:T(8,128)S(1)}, bf16[384,768]{1,0:T(8,128)(2,1)}, bf16[384,768]{1,0:T(8,128)(2,1)}) custom-call(bf16[192,192]{1,0:T(8,128)(2,1)S(1)} %copy-done.9, bf16[1536,512]{1,0:T(8,128)(2,1)S(1)} %bitcast.16, bf16[768,2048]{1,0:T(8,128)(2,1)} %bitcast.33, ...), custom_call_target="tpu_custom_call" | custom-call | flops 2097152000 | bytes 8388608 | tf_op jit(solution)/shard_map/pallas_call | solution.py:390
  106.4 4.0 %shard_map.151 = bf16[512,1664]{1,0:T(8,128)(2,1)} custom-call(bf16[192,192]{1,0:T(8,128)(2,1)S(1)} %copy-done.34, bf16[64,48]{1,0:T(8,128)(2,1)S(1)} %copy-done.35, bf16[2,384,768]{2,1,0:T(8,128)(2,1)S(1)} %get-tuple-element.29.back_ref, f32[384,128]{1,0:T(8,128)S(1)} %get-tuple-element.30.q_ref, bf16[2048,768]{1,0:T(8,128)(2,1)S(1)} %bitcast.24, ...), custom_call_target="tpu_custom_call" | custom-call | flops 3145728000 | bytes 8388608 | tf_op jit(solution)/shard_map/pallas_call | solution.py:390
  110.4 7.4 %all-to-all-start.2 = ((bf16[64,8,1664]{2,1,0:T(8,128)(2,1)}), bf16[64,8,1664]{2,1,0:T(8,128)(2,1)S(1)}, u32[]{:S(2)}, u32[]{:S(2)}) async-start(bf16[64,8,1664]{2,1,0:T(8,128)(2,1)} %bitcast.29), calls=%async_computation.2 | async-start | bytes 3407872 | tf_op jit(solution)/shard_map/all_to_all | solution.py:404
  117.9 1.6 collective-permute-start.9
  119.4 0.5 collective-permute-start.13
  120.0 2.8 %shard_map.155 = (bf16[384,512]{1,0:T(8,128)(2,1)}, bf16[384,512]{1,0:T(8,128)(2,1)}, bf16[384,512]{1,0:T(8,128)(2,1)}, bf16[384,512]{1,0:T(8,128)(2,1)}) custom-call(s32[1]{0:T(128)} %bitcast.5.dp_ref, bf16[192,192]{1,0:T(8,128)(2,1)S(1)} %copy-done.9, bf16[1536,512]{1,0:T(8,128)(2,1)S(1)} %bitcast.17), custom_call_target="tpu_custom_call" | custom-call | flops 314572800 | bytes 8388608 | tf_op jit(solution)/shard_map/pallas_call | solution.py:390
  122.8 1.6 collective-permute-start.15
  124.4 2.3 %collective-permute-start.16 = (bf16[384,512]{1,0:T(8,128)(2,1)}, bf16[384,512]{1,0:T(8,128)(2,1)S(1)}, u32[]{:S(2)}, u32[]{:S(2)}) collective-permute-start(bf16[384,512]{1,0:T(8,128)(2,1)} %get-tuple-element.45), channel_id=1, source_target_pairs={{0,128},{64,192},{128,0},{192,64},{1,129},{65,193},{129,1},{193,65... | collective-permute-start | bytes 1179656 | tf_op jit(solution)/shard_map/ppermute | solution.py:408
  126.7 0.9 collective-permute-start.11
  127.6 0.4 collective-permute-done.9.refs_1_
  128.0 1.5 collective-permute-start.12
  129.5 5.8 %collective-permute-start.17 = (bf16[384,512]{1,0:T(8,128)(2,1)}, bf16[384,512]{1,0:T(8,128)(2,1)S(1)}, u32[]{:S(2)}, u32[]{:S(2)}) collective-permute-start(bf16[384,512]{1,0:T(8,128)(2,1)} %get-tuple-element.46), channel_id=1, source_target_pairs={{0,192},{64,0},{128,64},{192,128},{1,193},{65,1},{129,65},{193,129... | collective-permute-start | bytes 1179656 | tf_op jit(solution)/shard_map/ppermute | solution.py:408
  135.3 8.5 %collective-permute-done.11.refs_3_ = bf16[384,384]{1,0:T(8,128)(2,1)S(1)} collective-permute-done((bf16[384,384]{1,0:T(8,128)(2,1)}, bf16[384,384]{1,0:T(8,128)(2,1)S(1)}, u32[]{:S(2)}, u32[]{:S(2)}) %collective-permute-start.11) | collective-permute-done | bytes 294944 | tf_op jit(solution)/shard_map/ppermute | solution.py:408
  143.9 0.7 copy-done.21
  144.6 1.6 collective-permute-start
  146.2 5.1 %collective-permute-done.12.refs_5_ = bf16[384,384]{1,0:T(8,128)(2,1)S(1)} collective-permute-done((bf16[384,384]{1,0:T(8,128)(2,1)}, bf16[384,384]{1,0:T(8,128)(2,1)S(1)}, u32[]{:S(2)}, u32[]{:S(2)}) %collective-permute-start.12) | collective-permute-done | bytes 294944 | tf_op jit(solution)/shard_map/ppermute | solution.py:408
  151.2 0.7 copy-done.23
  152.0 1.6 collective-permute-start.3
  153.6 0.8 copy-done.3
  154.3 0.4 collective-permute-start.4
  154.8 0.8 copy-done.5
  155.5 1.6 collective-permute-start.5
  157.1 0.8 copy-done.7
  157.9 0.4 collective-permute-start.10
  158.3 0.7 copy-done.17
  159.0 13.3 %collective-permute-done.4.refs_7_ = bf16[512,384]{1,0:T(8,128)(2,1)S(1)} collective-permute-done((bf16[512,384]{1,0:T(8,128)(2,1)}, bf16[512,384]{1,0:T(8,128)(2,1)S(1)}, u32[]{:S(2)}, u32[]{:S(2)}) %collective-permute-start.4) | collective-permute-done | bytes 393248 | tf_op jit(solution)/shard_map/ppermute | solution.py:408
  172.3 0.7 copy-done.11
  173.1 1.6 collective-permute-start.1
  174.6 0.8 copy-done.13
  175.4 1.1 collective-permute-start.2
  176.5 2.1 collective-permute-done.10.refs_2_
  178.6 0.7 copy-done.25
  179.4 1.0 collective-permute-start.14
  180.4 0.7 copy-done.19
  181.1 1.0 collective-permute-start.6
  182.1 1.4 collective-permute-start.7
  183.5 12.3 %collective-permute-done.14.refs_6_ = bf16[384,384]{1,0:T(8,128)(2,1)S(1)} collective-permute-done((bf16[384,384]{1,0:T(8,128)(2,1)S(1)}, bf16[384,384]{1,0:T(8,128)(2,1)S(1)}, u32[]{:S(2)}, u32[]{:S(2)}) %collective-permute-start.14) | collective-permute-done | bytes 294944 | tf_op jit(solution)/shard_map/ppermute | solution.py:408
  195.8 0.7 copy-done.27
  196.5 3.3 %collective-permute-start.8 = (bf16[512,384]{1,0:T(8,128)(2,1)}, bf16[512,384]{1,0:T(8,128)(2,1)}, u32[]{:S(2)}, u32[]{:S(2)}) collective-permute-start(bf16[512,384]{1,0:T(8,128)(2,1)} %get-tuple-element.38), channel_id=1, source_target_pairs={{0,128},{64,192},{128,0},{192,64},{1,129},{65,193},{129,1},{193,65... | collective-permute-start | bytes 1179656 | tf_op jit(solution)/shard_map/ppermute | solution.py:408
  199.9 0.7 copy.16.ids_ref
  200.6 1.0 copy-done.2
  201.6 1.0 copy-done.4
  202.6 1.0 copy-done.6
  203.6 1.0 copy-done.8
  204.6 1.0 copy-done.15
  205.6 1.0 copy-done.16
  206.5 1.0 copy-done.18
  207.5 1.0 copy-done.20
  208.4 1.0 copy-done.22
  209.4 1.0 copy-done.24
  210.4 1.0 copy-done.26
  211.3 1.0 copy-done.28
  212.3 4.2 %shard_map.156 = bf16[768,512]{1,0:T(8,128)(2,1)} custom-call(bf16[384,384]{1,0:T(8,128)(2,1)S(1)} %copy-done.15, bf16[384,384]{1,0:T(8,128)(2,1)S(1)} %copy-done.18, bf16[384,384]{1,0:T(8,128)(2,1)S(1)} %copy-done.26, bf16[384,384]{1,0:T(8,128)(2,1)S(1)} %copy-done.22, bf16[384,384]{1,0:T(8,128)(2,1)S(1)} %copy-done.16, bf16[384,384]{1,0:T(8,128)(2,1)S(1)} %copy-done.24, ...), custom_call_target="tpu_custom_call" | custom-call | flops 1258291200 | bytes 8388608 | tf_op jit(solution)/shard_map/pallas_call | solution.py:390
  216.5 3.8 %shard_map.153.acc = f32[2,512,768]{2,1,0:T(8,128)S(1)} custom-call(bf16[384,768]{1,0:T(8,128)(2,1)S(1)} %copy-done, bf16[384,768]{1,0:T(8,128)(2,1)S(1)} %collective-permute-done.refs_1_, bf16[384,768]{1,0:T(8,128)(2,1)} %collective-permute-done.1.refs_2_, bf16[384,768]{1,0:T(8,128)(2,1)S(1)} %copy-done.1, bf16[384,768]{1,0:T(8,128)(2,1)} %collective-permute-done.2.refs_4_, ...), custom_call_target="tpu_custom_call" | custom-call | flops 1887436800 | bytes 8388608 | tf_op jit(solution)/shard_map/pallas_call | solution.py:390
  220.4 3.0 %shard_map.154 = (bf16[512,768]{1,0:T(8,128)(2,1)}, bf16[512,768]{1,0:T(8,128)(2,1)}) custom-call(f32[2,512,768]{2,1,0:T(8,128)S(1)} %shard_map.153.acc, bf16[384,768]{1,0:T(8,128)(2,1)S(1)} %collective-permute-done.6.gate_b, bf16[384,768]{1,0:T(8,128)(2,1)S(1)} %collective-permute-done.7.up_b, bf16[512,384]{1,0:T(8,128)(2,1)} %collective-permute-done.8.x2), custom_call_target="tpu_custom_call" | custom-call | flops 629145600 | bytes 8388608 | tf_op jit(solution)/shard_map/pallas_call | solution.py:390
  223.4 6.4 %shard_map.152 = (bf16[128,2048]{1,0:T(8,128)(2,1)}, bf16[2,128]{1,0:T(2,128)(2,1)}) custom-call(s32[128,2]{1,0:T(8,128)} %copy.16.ids_ref, s32[2,128]{1,0:T(2,128)} %bitcast.21, bf16[2,128]{1,0:T(2,128)(2,1)} %bitcast.27, bf16[192,192]{1,0:T(8,128)(2,1)} %constant.16.clone.perm_ref, bf16[512,1664]{1,0:T(8,128)(2,1)S(1)} %bitcast.19), custom_call_target="tpu_custom_call" | custom-call | flops 1048576000 | bytes 8388608 | tf_op jit(solution)/shard_map/pallas_call | solution.py:390
  (62 shorter events, 0.1 us)
Async XLA Ops:
  4.0 12.3 %copy-start.29 = (s32[128,2]{0,1:T(2,128)S(1)}, s32[128,2]{0,1:T(2,128)}, u32[]{:S(2)}) copy-start(s32[128,2]{0,1:T(2,128)} %param.14) | copy-start | bytes 3076
  4.0 12.3 %copy-start.32 = (bf16[128,2048]{1,0:T(8,128)(2,1)S(1)}, bf16[128,2048]{1,0:T(8,128)(2,1)}, u32[]{:S(2)}) copy-start(bf16[128,2048]{1,0:T(8,128)(2,1)} %x_ref.2) | copy-start | bytes 1572868
  4.0 12.3 %copy-start.33 = (bf16[128,2]{0,1:T(2,128)(2,1)S(1)}, bf16[128,2]{0,1:T(2,128)(2,1)}, u32[]{:S(2)}) copy-start(bf16[128,2]{0,1:T(2,128)(2,1)} %param.13) | copy-start | bytes 1540
  4.0 50.7 %all-to-all-start.1 = ((bf16[64,24,512]{2,1,0:T(8,128)(2,1)}), bf16[64,24,512]{2,1,0:T(8,128)(2,1)S(1)}, u32[]{:S(2)}, u32[]{:S(2)}) async-start(bf16[64,24,512]{2,1,0:T(8,128)(2,1)} %bitcast.31), calls=%async_computation.1 | async-start | bytes 3145728 | tf_op jit(solution)/shard_map/all_to_all | solution.py:404
  18.6 43.5 %copy-start.9 = (bf16[192,192]{1,0:T(8,128)(2,1)S(1)}, bf16[192,192]{1,0:T(8,128)(2,1)}, u32[]{:S(2)}) copy-start(bf16[192,192]{1,0:T(8,128)(2,1)} %constant.14.clone.perm_ref) | copy-start | bytes 221188
  54.7 45.9 %all-to-all-start = ((bf16[64,24,512]{2,1,0:T(8,128)(2,1)}), bf16[64,24,512]{2,1,0:T(8,128)(2,1)S(1)}, u32[]{:S(2)}, u32[]{:S(2)}) async-start(bf16[64,24,512]{2,1,0:T(8,128)(2,1)} %bitcast.30), calls=%async_computation | async-start | bytes 3145728 | tf_op jit(solution)/shard_map/all_to_all | solution.py:404
  100.5 5.8 %copy-start.30 = (bf16[1,2048,768]{2,1,0:T(8,128)(2,1)S(1)}, bf16[1,2048,768]{2,1,0:T(8,128)(2,1)}, u32[]{:S(2)}) copy-start(bf16[1,2048,768]{2,1,0:T(8,128)(2,1)} %param.15) | copy-start | bytes 9437188
  100.5 5.8 %copy-start.31 = (bf16[1,2048,768]{2,1,0:T(8,128)(2,1)S(1)}, bf16[1,2048,768]{2,1,0:T(8,128)(2,1)}, u32[]{:S(2)}) copy-start(bf16[1,2048,768]{2,1,0:T(8,128)(2,1)} %param.16) | copy-start | bytes 9437188
  100.5 5.8 %copy-start.34 = (bf16[192,192]{1,0:T(8,128)(2,1)S(1)}, bf16[192,192]{1,0:T(8,128)(2,1)}, u32[]{:S(2)}) copy-start(bf16[192,192]{1,0:T(8,128)(2,1)} %constant.15.clone.pack_ref) | copy-start | bytes 221188
  100.6 5.8 %copy-start.35 = (bf16[64,48]{1,0:T(8,128)(2,1)S(1)}, bf16[64,48]{1,0:T(8,128)(2,1)}, u32[]{:S(2)}) copy-start(bf16[64,48]{1,0:T(8,128)(2,1)} %constant.17.clone.probs_ref) | copy-start | bytes 18436
  110.4 112.9 %all-to-all-start.2 = ((bf16[64,8,1664]{2,1,0:T(8,128)(2,1)}), bf16[64,8,1664]{2,1,0:T(8,128)(2,1)S(1)}, u32[]{:S(2)}, u32[]{:S(2)}) async-start(bf16[64,8,1664]{2,1,0:T(8,128)(2,1)} %bitcast.29), calls=%async_computation.2 | async-start | bytes 3407872 | tf_op jit(solution)/shard_map/all_to_all | solution.py:404
  117.9 10.2 %collective-permute-start.9 = (bf16[384,384]{1,0:T(8,128)(2,1)}, bf16[384,384]{1,0:T(8,128)(2,1)S(1)}, u32[]{:S(2)}, u32[]{:S(2)}) collective-permute-start(bf16[384,384]{1,0:T(8,128)(2,1)} %get-tuple-element.41.refs_0_), channel_id=1, source_target_pairs={{0,64},{64,128},{128,192},{192,0},{1,65},{65,129},{129,193},{193,1... | collective-permute-start | bytes 884744 | tf_op jit(solution)/shard_map/ppermute | solution.py:408
  119.4 10.1 %collective-permute-start.13 = (bf16[384,384]{1,0:T(8,128)(2,1)}, bf16[384,384]{1,0:T(8,128)(2,1)S(1)}, u32[]{:S(2)}, u32[]{:S(2)}) collective-permute-start(bf16[384,384]{1,0:T(8,128)(2,1)} %get-tuple-element.42.refs_4_), channel_id=1, source_target_pairs={{0,192},{64,0},{128,64},{192,128},{1,193},{65,1},{129,65},{193,129... | collective-permute-start | bytes 884744 | tf_op jit(solution)/shard_map/ppermute | solution.py:408
  122.8 30.8 %collective-permute-start.15 = (bf16[384,512]{1,0:T(8,128)(2,1)}, bf16[384,512]{1,0:T(8,128)(2,1)S(1)}, u32[]{:S(2)}, u32[]{:S(2)}) collective-permute-start(bf16[384,512]{1,0:T(8,128)(2,1)} %get-tuple-element.44), channel_id=1, source_target_pairs={{0,64},{64,128},{128,192},{192,0},{1,65},{65,129},{129,193},{193,1... | collective-permute-start | bytes 1179656 | tf_op jit(solution)/shard_map/ppermute | solution.py:408
  124.4 30.4 %collective-permute-start.16 = (bf16[384,512]{1,0:T(8,128)(2,1)}, bf16[384,512]{1,0:T(8,128)(2,1)S(1)}, u32[]{:S(2)}, u32[]{:S(2)}) collective-permute-start(bf16[384,512]{1,0:T(8,128)(2,1)} %get-tuple-element.45), channel_id=1, source_target_pairs={{0,128},{64,192},{128,0},{192,64},{1,129},{65,193},{129,1},{193,65... | collective-permute-start | bytes 1179656 | tf_op jit(solution)/shard_map/ppermute | solution.py:408
  126.7 17.2 %collective-permute-start.11 = (bf16[384,384]{1,0:T(8,128)(2,1)}, bf16[384,384]{1,0:T(8,128)(2,1)S(1)}, u32[]{:S(2)}, u32[]{:S(2)}) collective-permute-start(bf16[384,384]{1,0:T(8,128)(2,1)} %get-tuple-element.41.refs_0_), channel_id=1, source_target_pairs={{0,192},{64,0},{128,64},{192,128},{1,193},{65,1},{129,65},{193,129... | collective-permute-start | bytes 884744 | tf_op jit(solution)/shard_map/ppermute | solution.py:408
  128.0 23.2 %collective-permute-start.12 = (bf16[384,384]{1,0:T(8,128)(2,1)}, bf16[384,384]{1,0:T(8,128)(2,1)S(1)}, u32[]{:S(2)}, u32[]{:S(2)}) collective-permute-start(bf16[384,384]{1,0:T(8,128)(2,1)} %get-tuple-element.42.refs_4_), channel_id=1, source_target_pairs={{0,64},{64,128},{128,192},{192,0},{1,65},{65,129},{129,193},{193,1... | collective-permute-start | bytes 884744 | tf_op jit(solution)/shard_map/ppermute | solution.py:408
  129.5 27.6 %collective-permute-start.17 = (bf16[384,512]{1,0:T(8,128)(2,1)}, bf16[384,512]{1,0:T(8,128)(2,1)S(1)}, u32[]{:S(2)}, u32[]{:S(2)}) collective-permute-start(bf16[384,512]{1,0:T(8,128)(2,1)} %get-tuple-element.46), channel_id=1, source_target_pairs={{0,192},{64,0},{128,64},{192,128},{1,193},{65,1},{129,65},{193,129... | collective-permute-start | bytes 1179656 | tf_op jit(solution)/shard_map/ppermute | solution.py:408
  143.9 0.7 copy-start.21
  144.6 36.5 %collective-permute-start = (bf16[384,768]{1,0:T(8,128)(2,1)}, bf16[384,768]{1,0:T(8,128)(2,1)S(1)}, u32[]{:S(2)}, u32[]{:S(2)}) collective-permute-start(bf16[384,768]{1,0:T(8,128)(2,1)} %get-tuple-element.33.refs_0_), channel_id=1, source_target_pairs={{0,64},{64,128},{128,192},{192,0},{1,65},{65,129},{129,193},{193,1... | collective-permute-start | bytes 1769480 | tf_op jit(solution)/shard_map/ppermute | solution.py:408
  151.2 0.7 copy-start.23
  152.0 30.1 %collective-permute-start.3 = (bf16[384,768]{1,0:T(8,128)(2,1)}, bf16[384,768]{1,0:T(8,128)(2,1)}, u32[]{:S(2)}, u32[]{:S(2)}) collective-permute-start(bf16[384,768]{1,0:T(8,128)(2,1)} %get-tuple-element.34.refs_3_), channel_id=1, source_target_pairs={{0,192},{64,0},{128,64},{192,128},{1,193},{65,1},{129,65},{193,129... | collective-permute-start | bytes 1769480 | tf_op jit(solution)/shard_map/ppermute | solution.py:408
  153.6 0.8 copy-start.3
  154.3 18.0 %collective-permute-start.4 = (bf16[512,384]{1,0:T(8,128)(2,1)}, bf16[512,384]{1,0:T(8,128)(2,1)S(1)}, u32[]{:S(2)}, u32[]{:S(2)}) collective-permute-start(bf16[512,384]{1,0:T(8,128)(2,1)} %get-tuple-element.36), channel_id=1, source_target_pairs={{0,64},{64,128},{128,192},{192,0},{1,65},{65,129},{129,193},{193,1... | collective-permute-start | bytes 1179656 | tf_op jit(solution)/shard_map/ppermute | solution.py:408
  154.8 0.8 copy-start.5
  155.5 19.1 %collective-permute-start.5 = (bf16[512,384]{1,0:T(8,128)(2,1)}, bf16[512,384]{1,0:T(8,128)(2,1)S(1)}, u32[]{:S(2)}, u32[]{:S(2)}) collective-permute-start(bf16[512,384]{1,0:T(8,128)(2,1)} %get-tuple-element.37), channel_id=1, source_target_pairs={{0,192},{64,0},{128,64},{192,128},{1,193},{65,1},{129,65},{193,129... | collective-permute-start | bytes 1179656 | tf_op jit(solution)/shard_map/ppermute | solution.py:408
  157.1 0.8 copy-start.7
  157.9 20.7 %collective-permute-start.10 = (bf16[384,384]{1,0:T(8,128)(2,1)S(1)}, bf16[384,384]{1,0:T(8,128)(2,1)S(1)}, u32[]{:S(2)}, u32[]{:S(2)}) collective-permute-start(bf16[384,384]{1,0:T(8,128)(2,1)S(1)} %collective-permute-done.9.refs_1_), channel_id=1, source_target_pairs={{0,64},{64,128},{128,192},{192,0},{1,65},{65,129},{129,193},{193,1... | collective-permute-start | bytes 884744 | tf_op jit(solution)/shard_map/ppermute | solution.py:408
  158.3 0.7 copy-start.17
  172.3 0.7 copy-start.11
  173.1 43.4 %collective-permute-start.1 = (bf16[384,768]{1,0:T(8,128)(2,1)}, bf16[384,768]{1,0:T(8,128)(2,1)}, u32[]{:S(2)}, u32[]{:S(2)}) collective-permute-start(bf16[384,768]{1,0:T(8,128)(2,1)} %get-tuple-element.33.refs_0_), channel_id=1, source_target_pairs={{0,192},{64,0},{128,64},{192,128},{1,193},{65,1},{129,65},{193,129... | collective-permute-start | bytes 1769480 | tf_op jit(solution)/shard_map/ppermute | solution.py:408
  174.6 0.8 copy-start.13
  175.4 41.1 %collective-permute-start.2 = (bf16[384,768]{1,0:T(8,128)(2,1)}, bf16[384,768]{1,0:T(8,128)(2,1)}, u32[]{:S(2)}, u32[]{:S(2)}) collective-permute-start(bf16[384,768]{1,0:T(8,128)(2,1)} %get-tuple-element.34.refs_3_), channel_id=1, source_target_pairs={{0,64},{64,128},{128,192},{192,0},{1,65},{65,129},{129,193},{193,1... | collective-permute-start | bytes 1769480 | tf_op jit(solution)/shard_map/ppermute | solution.py:408
  178.6 0.7 copy-start.25
  179.4 16.4 %collective-permute-start.14 = (bf16[384,384]{1,0:T(8,128)(2,1)S(1)}, bf16[384,384]{1,0:T(8,128)(2,1)S(1)}, u32[]{:S(2)}, u32[]{:S(2)}) collective-permute-start(bf16[384,384]{1,0:T(8,128)(2,1)S(1)} %collective-permute-done.13.refs_7_), channel_id=1, source_target_pairs={{0,192},{64,0},{128,64},{192,128},{1,193},{65,1},{129,65},{193,129... | collective-permute-start | bytes 884744 | tf_op jit(solution)/shard_map/ppermute | solution.py:408
  180.4 0.7 copy-start.19
  181.1 39.3 %collective-permute-start.6 = (bf16[384,768]{1,0:T(8,128)(2,1)S(1)}, bf16[384,768]{1,0:T(8,128)(2,1)S(1)}, u32[]{:S(2)}, u32[]{:S(2)}) collective-permute-start(bf16[384,768]{1,0:T(8,128)(2,1)S(1)} %collective-permute-done.refs_1_), channel_id=1, source_target_pairs={{0,64},{64,128},{128,192},{192,0},{1,65},{65,129},{129,193},{193,1... | collective-permute-start | bytes 1769480 | tf_op jit(solution)/shard_map/ppermute | solution.py:408
  182.1 38.3 %collective-permute-start.7 = (bf16[384,768]{1,0:T(8,128)(2,1)}, bf16[384,768]{1,0:T(8,128)(2,1)S(1)}, u32[]{:S(2)}, u32[]{:S(2)}) collective-permute-start(bf16[384,768]{1,0:T(8,128)(2,1)} %collective-permute-done.3.refs_5_), channel_id=1, source_target_pairs={{0,192},{64,0},{128,64},{192,128},{1,193},{65,1},{129,65},{193,129... | collective-permute-start | bytes 1769480 | tf_op jit(solution)/shard_map/ppermute | solution.py:408
  195.8 0.7 copy-start.27
  196.5 23.9 %collective-permute-start.8 = (bf16[512,384]{1,0:T(8,128)(2,1)}, bf16[512,384]{1,0:T(8,128)(2,1)}, u32[]{:S(2)}, u32[]{:S(2)}) collective-permute-start(bf16[512,384]{1,0:T(8,128)(2,1)} %get-tuple-element.38), channel_id=1, source_target_pairs={{0,128},{64,192},{128,0},{192,64},{1,129},{65,193},{129,1},{193,65... | collective-permute-start | bytes 1179656 | tf_op jit(solution)/shard_map/ppermute | solution.py:408
  200.6 1.0 copy-start.2
  201.6 1.0 copy-start.4
  202.6 1.0 copy-start.6
  203.6 1.0 copy-start.8
  204.6 1.0 copy-start.15
  205.6 1.0 copy-start.16
  206.5 1.0 copy-start.18
  207.5 1.0 copy-start.20
  208.4 1.0 copy-start.22
  209.4 1.0 copy-start.24
  210.4 1.0 copy-start.26
  211.3 1.0 copy-start.28
  212.3 4.2 %copy-start = (bf16[384,768]{1,0:T(8,128)(2,1)S(1)}, bf16[384,768]{1,0:T(8,128)(2,1)}, u32[]{:S(2)}) copy-start(bf16[384,768]{1,0:T(8,128)(2,1)} %get-tuple-element.33.refs_0_) | copy-start | bytes 1769476
  212.3 4.2 %copy-start.1 = (bf16[384,768]{1,0:T(8,128)(2,1)S(1)}, bf16[384,768]{1,0:T(8,128)(2,1)}, u32[]{:S(2)}) copy-start(bf16[384,768]{1,0:T(8,128)(2,1)} %get-tuple-element.34.refs_3_) | copy-start | bytes 1769476
  212.3 4.2 %copy-start.10 = (bf16[512,384]{1,0:T(8,128)(2,1)S(1)}, bf16[512,384]{1,0:T(8,128)(2,1)}, u32[]{:S(2)}) copy-start(bf16[512,384]{1,0:T(8,128)(2,1)} %get-tuple-element.35.refs_6_) | copy-start | bytes 1179652
  212.3 4.2 %copy-start.12 = (bf16[512,384]{1,0:T(8,128)(2,1)S(1)}, bf16[512,384]{1,0:T(8,128)(2,1)}, u32[]{:S(2)}) copy-start(bf16[512,384]{1,0:T(8,128)(2,1)} %copy-done.11) | copy-start | bytes 1179652
  212.3 4.2 %copy-start.14 = (bf16[512,384]{1,0:T(8,128)(2,1)S(1)}, bf16[512,384]{1,0:T(8,128)(2,1)}, u32[]{:S(2)}) copy-start(bf16[512,384]{1,0:T(8,128)(2,1)} %copy-done.13) | copy-start | bytes 1179652

commit v6 on v5

--- a/solution.py
+++ b/solution.py
@@ -44,10 +44,10 @@
             for v in range(4):
                 c, r = divmod(v * PER + j, BROWS)
                 pack[(c * GROUP + d) * BROWS + r, v * GROWS + row] = 1
-    return unmix, pack, np.ascontiguousarray(pack.T), probs
-
-
-UNMIX, PACK, UNPACK, PROBS = permutations()
+    return unmix, pack, probs
+
+
+UNMIX, PACK, PROBS = permutations()
 
 
 def mm(a, b):
@@ -77,19 +77,6 @@
     out = []
     for k in range(2):
         rank = jnp.sum(count * hot[k], axis=0, keepdims=True).astype(jnp.int32)
-        target, first = split_slot(ids[k])
-        out.append((target, first + rank))
-    return out
-
-
-def places_in_rows(ids_ref):
-    ids = [ids_ref[:, k : k + 1] for k in range(2)]
-    hot = [(iota((TOK, 2 * N), 1) == v).astype(F32) for v in ids]
-    before = (iota((TOK, TOK), 1) < iota((TOK, TOK), 0)).astype(F32).astype(BF16)
-    count = mm(before, (hot[0] + hot[1]).astype(BF16))
-    out = []
-    for k in range(2):
-        rank = jnp.sum(count * hot[k], axis=1, keepdims=True).astype(jnp.int32)
         target, first = split_slot(ids[k])
         out.append((target, first + rank))
     return out
@@ -266,19 +253,31 @@
     return copies
 
 
-def combine_kernel(
-    ids_ref, ids_t_ref, prob_ref, perm_ref, got_hbm, tok_ref, gprob_ref, rows, got_ref, sems
-):
+def unpack_matrix():
+    size = 4 * GROWS
+
+    def sixth(v):
+        return lax.shift_right_logical(v * 43691, 18)
+
+    a = iota((size, 1), 0)
+    owner = sixth(a)
+    piece = lax.shift_right_logical(owner, 3) * PER + a - owner * PER
+    b = iota((1, size), 1)
+    line = lax.shift_right_logical(b, 3)
+    slot = lax.shift_right_logical(line, 3) * BROWS + (b & 7)
+    hit = (piece == slot) & ((owner & 7) == (line & 7))
+    return jnp.where(hit, 1.0, 0.0).astype(BF16)
+
+
+def combine_kernel(ids_t_ref, prob_ref, got_ref, tok_ref, gprob_ref, rows):
     height = GROUP * BROWS
-    blocks = [pl.ds(g * height, height) for g in range(NGROUP)]
-    copies = load([got_hbm.at[b] for b in blocks], [got_ref.at[b] for b in blocks], sems)
-    at = [target * PER + slot for target, slot in places_in_rows(ids_ref)]
-    columns = iota((TOK, ROWS), 1)
-    pick = jnp.where((columns == at[0]) | (columns == at[1]), 1.0, 0.0).astype(BF16)
-    perm = perm_ref[...]
+    places = places_in_lanes(ids_t_ref)
+    at = [target * PER + slot for target, slot in places]
+    lines = iota((ROWS, TOK), 0)
+    pick = jnp.where((lines == at[0]) | (lines == at[1]), 1.0, 0.0).T.astype(BF16)
+    perm = unpack_matrix()
     for g in range(NGROUP):
         top = g * height
-        copies[g].wait()
         stacked = jnp.concatenate(
             [
                 jnp.concatenate(
@@ -302,7 +301,7 @@
     tok_ref[...] = mm(pick, rows[...]).astype(BF16)
     home = got_ref[:, 3 * NU * TILE :].astype(F32)
     line = iota((N * BROWS, TOK), 0)
-    for k, (target, slot) in enumerate(places_in_lanes(ids_t_ref)):
+    for k, (target, slot) in enumerate(places):
         hit = jnp.where(line == target * BROWS + slot, home, 0.0)
         value = jnp.sum(hit, axis=0, keepdims=True)
         gprob_ref[k : k + 1, :] = (value / prob_ref[k : k + 1, :].astype(F32)).astype(BF16)
@@ -333,7 +332,7 @@
 
 
 def grad_first_kernel(*refs):
-    acc, gates, ups, cols, sems = refs[9:]
+    out, gates, ups, cols, acc, sems = refs[9:]
     copies = load(
         [refs[3 * m + k] for k in range(3) for m in (2, 0, 1)],
         [r.at[k] for k in range(3) for r in (cols, gates, ups)],
@@ -344,7 +343,12 @@
             copy.wait()
         for m, part in enumerate((gates, ups)):
             term = mm(cols[k], part[k])
-            acc[m] = term if k == 0 else acc[m] + term
+            if k == 0:
+                acc[m] = term
+            elif k == 1:
+                acc[m] = acc[m] + term
+            else:
+                out[m] = (acc[m] + term).astype(BF16)
 
 
 def grad_last_kernel(acc, gate_b, up_b, x2, gate_out, up_out, col, parts, sent, sems, out_sems):
@@ -356,7 +360,7 @@
         copies[1 + m].wait()
         for h in range(2):
             at = slice(h * half, (h + 1) * half)
-            sent[m, at] = (acc[m, at] + mm(col[at], parts[m])).astype(BF16)
+            sent[m, at] = (acc[m, at].astype(F32) + mm(col[at], parts[m])).astype(BF16)
             rows = pl.ds(h * half, half)
             sends.append(
                 pltpu.make_async_copy(sent.at[m, rows], out.at[rows], out_sems.at[2 * m + h])
@@ -436,7 +440,7 @@
     )
     got_c = exchange(send_c.reshape(N, SPAN, SEG)).reshape(N * SPAN, SEG)
 
-    unmix, pack, unpack, probs_perm = [jnp.asarray(v, BF16) for v in (UNMIX, PACK, UNPACK, PROBS)]
+    unmix, pack, probs_perm = [jnp.asarray(v, BF16) for v in (UNMIX, PACK, PROBS)]
 
     rows, *x_pieces = call(
         unmix_kernel,
@@ -490,11 +494,12 @@
     got_b = exchange(send_b.reshape(N, BROWS, BCOLS)).reshape(N * BROWS, BCOLS)
 
     (acc,) = call(
-        grad_first_kernel, [near((2, SEG, FF), F32)],
+        grad_first_kernel, [near((2, SEG, FF))],
         scratch=[
             pltpu.VMEM((3, ROWS, FF), BF16),
             pltpu.VMEM((3, ROWS, FF), BF16),
             pltpu.VMEM((3, SEG, ROWS), BF16),
+            pltpu.VMEM((2, SEG, FF), F32),
             pltpu.SemaphoreType.DMA((9,)),
         ],
         far=range(9), flops=1800 << 20,
@@ -523,13 +528,8 @@
     )(in_vmem(acc), b_gate[2], b_up[2], x_pieces[2])
     grad_tokens, grad_probs = call(
         combine_kernel, [shape((TOK, D)), shape((2, TOK))],
-        scratch=[
-            pltpu.VMEM((ROWS, D), BF16),
-            pltpu.VMEM((N * BROWS, BCOLS), BF16),
-            pltpu.SemaphoreType.DMA((NGROUP,)),
-        ],
-        far=(4,), flops=1000 << 20,
-    )(in_hbm(expert_ids), in_hbm(ids_t), in_hbm(probs_t), in_hbm(unpack), got_b)
+        scratch=[pltpu.VMEM((ROWS, D), BF16)], flops=1000 << 20,
+    )(ids_t, probs_t, got_b)
     return grad_tokens, grad_probs.T, grad_gate[None], grad_up[None], grad_down[None]
 
 

time: 231 us -> 220 us (0.952)
  the two profiles are of different devices: /device:TPU:10 before, /device:TPU:1 now
where the time goes in v6:
time: 220 us; the launch traced here: 218 us
  waiting for transfers between devices  130 us (59%)
  starting transfers between devices  46.3 us (21%)
  Pallas kernels  39.7 us (18%)
    all_to_all x3, waiting for transfers between devices, exchange(): lax.all_to_all(values, 'expert', split_axis=0, concat_axis=0, tiled=True)  68.4 us
    ppermute x18, waiting for transfers between devices, shift(): return lax.ppermute(values, 'dp', [(i, (i + k) % DP) for i in range(DP)])  61.9 us
    pallas_call x11, Pallas kernels, run(): pl.pallas_call(kernel, in_specs=[pl.BlockSpec(memory_space=v) for v in sp...  39.7 us
    all_to_all x3, starting transfers between devices, exchange(): lax.all_to_all(values, 'expert', split_axis=0, concat_axis=0, tiled=True)  25.6 us
    ppermute x18, starting transfers between devices, shift(): return lax.ppermute(values, 'dp', [(i, (i + k) % DP) for i in range(DP)])  20.7 us
  transfers between devices with their start and end apart: 21, of which 9 were waited for; matrix products, arithmetic and copies ran while one was open for 0% of the time, Pallas kernels for 11%

profile of v6, /device:TPU:1, one launch (start us, length us, event | category | flops | bytes accessed | tf_op | source)
XLA Modules:
  0.0 218.3 jit_solution(14147842146548788435)
XLA Ops:
  0.6 3.4 %shard_map.138 = bf16[1536,512]{1,0:T(8,128)(2,1)} custom-call(s32[2,128]{1,0:T(2,128)} %bitcast.24, bf16[128,2048]{1,0:T(8,128)(2,1)} %x_ref.3), custom_call_target="tpu_custom_call" | custom-call | flops 838860800 | bytes 8388608 | tf_op jit(solution)/shard_map/pallas_call | solution.py:394
  4.0 13.3 %all-to-all-start.1 = ((bf16[64,24,512]{2,1,0:T(8,128)(2,1)}), bf16[64,24,512]{2,1,0:T(8,128)(2,1)S(1)}, u32[]{:S(2)}, u32[]{:S(2)}) async-start(bf16[64,24,512]{2,1,0:T(8,128)(2,1)} %bitcast.31), calls=%async_computation.1 | async-start | bytes 3145728 | tf_op jit(solution)/shard_map/all_to_all | solution.py:408
  17.3 0.0 copy-done.8
  17.3 0.0 copy-done.10
  17.3 0.0 copy-done.11
  17.3 2.3 %shard_map.137 = bf16[1536,512]{1,0:T(8,128)(2,1)} custom-call(s32[2,128]{1,0:T(2,128)S(1)} %bitcast.25, bf16[2,128]{1,0:T(2,128)(2,1)S(1)} %bitcast.27, bf16[128,2048]{1,0:T(8,128)(2,1)S(1)} %copy-done.8), custom_call_target="tpu_custom_call" | custom-call | flops 838860800 | bytes 8388608 | tf_op jit(solution)/shard_map/pallas_call | solution.py:394
  19.6 37.4 %all-to-all-done.1 = bf16[64,24,512]{2,1,0:T(8,128)(2,1)S(1)} async-done(((bf16[64,24,512]{2,1,0:T(8,128)(2,1)}), bf16[64,24,512]{2,1,0:T(8,128)(2,1)S(1)}, u32[]{:S(2)}, u32[]{:S(2)}) %all-to-all-start.1) | async-done | bytes 1572896 | tf_op jit(solution)/shard_map/all_to_all | solution.py:408
  57.0 6.2 %all-to-all-start = ((bf16[64,24,512]{2,1,0:T(8,128)(2,1)}), bf16[64,24,512]{2,1,0:T(8,128)(2,1)S(1)}, u32[]{:S(2)}, u32[]{:S(2)}) async-start(bf16[64,24,512]{2,1,0:T(8,128)(2,1)} %bitcast.30), calls=%async_computation | async-start | bytes 3145728 | tf_op jit(solution)/shard_map/all_to_all | solution.py:408
  63.3 2.2 shard_map.139
  65.4 6.6 %shard_map.140 = (bf16[384,768]{1,0:T(8,128)(2,1)}, bf16[384,768]{1,0:T(8,128)(2,1)}, bf16[384,384]{1,0:T(8,128)(2,1)}, bf16[384,384]{1,0:T(8,128)(2,1)}) custom-call(bf16[4,384,512]{2,1,0:T(8,128)(2,1)S(1)} %get-tuple-element.26.rows, bf16[2048,768]{1,0:T(8,128)(2,1)} %bitcast.20, bf16[2048,768]{1,0:T(8,128)(2,1)} %bitcast.22), custom_call_target="tpu_custom_call" | custom-call | flops 3145728000 | bytes 8388608 | tf_op jit(solution)/shard_map/pallas_call | solution.py:394
  72.1 30.9 %all-to-all-done = bf16[64,24,512]{2,1,0:T(8,128)(2,1)S(1)} async-done(((bf16[64,24,512]{2,1,0:T(8,128)(2,1)}), bf16[64,24,512]{2,1,0:T(8,128)(2,1)S(1)}, u32[]{:S(2)}, u32[]{:S(2)}) %all-to-all-start) | async-done | bytes 1572896 | tf_op jit(solution)/shard_map/all_to_all | solution.py:408
  103.0 5.8 %shard_map.141 = (bf16[2,384,768]{2,1,0:T(8,128)(2,1)S(1)}, f32[384,128]{1,0:T(8,128)S(1)}, bf16[384,768]{1,0:T(8,128)(2,1)}, bf16[384,768]{1,0:T(8,128)(2,1)}) custom-call(bf16[192,192]{1,0:T(8,128)(2,1)S(1)} %copy-done.1, bf16[1536,512]{1,0:T(8,128)(2,1)S(1)} %bitcast.16, bf16[768,2048]{1,0:T(8,128)(2,1)} %bitcast.33, ...), custom_call_target="tpu_custom_call" | custom-call | flops 2097152000 | bytes 8388608 | tf_op jit(solution)/shard_map/pallas_call | solution.py:394
  108.8 0.0 copy-done.4
  108.8 0.0 copy-done.5
  108.8 0.0 copy-done.12
  108.9 0.0 copy-done.13
  108.9 4.1 %shard_map.142 = bf16[512,1664]{1,0:T(8,128)(2,1)} custom-call(bf16[192,192]{1,0:T(8,128)(2,1)S(1)} %copy-done.12, bf16[64,48]{1,0:T(8,128)(2,1)S(1)} %copy-done.13, bf16[2,384,768]{2,1,0:T(8,128)(2,1)S(1)} %get-tuple-element.29.back_ref, f32[384,128]{1,0:T(8,128)S(1)} %get-tuple-element.30.q_ref, bf16[2048,768]{1,0:T(8,128)(2,1)S(1)} %bitcast.21, ...), custom_call_target="tpu_custom_call" | custom-call | flops 3145728000 | bytes 8388608 | tf_op jit(solution)/shard_map/pallas_call | solution.py:394
  112.9 6.1 %all-to-all-start.2 = ((bf16[64,8,1664]{2,1,0:T(8,128)(2,1)}), bf16[64,8,1664]{2,1,0:T(8,128)(2,1)S(1)}, u32[]{:S(2)}, u32[]{:S(2)}) async-start(bf16[64,8,1664]{2,1,0:T(8,128)(2,1)} %bitcast.29), calls=%async_computation.2 | async-start | bytes 3407872 | tf_op jit(solution)/shard_map/all_to_all | solution.py:408
  119.1 0.0 copy-start.6
  119.1 1.3 collective-permute-start.9
  120.4 1.5 collective-permute-start.13
  121.8 2.8 %shard_map.146 = (bf16[384,512]{1,0:T(8,128)(2,1)}, bf16[384,512]{1,0:T(8,128)(2,1)}, bf16[384,512]{1,0:T(8,128)(2,1)}, bf16[384,512]{1,0:T(8,128)(2,1)}) custom-call(s32[1]{0:T(128)} %bitcast.5.dp_ref, bf16[192,192]{1,0:T(8,128)(2,1)S(1)} %copy-done.1, bf16[1536,512]{1,0:T(8,128)(2,1)S(1)} %bitcast.17), custom_call_target="tpu_custom_call" | custom-call | flops 314572800 | bytes 8388608 | tf_op jit(solution)/shard_map/pallas_call | solution.py:394
  124.7 0.1 collective-permute-start.15
  124.8 2.4 %collective-permute-start.16 = (bf16[384,512]{1,0:T(8,128)(2,1)}, bf16[384,512]{1,0:T(8,128)(2,1)S(1)}, u32[]{:S(2)}, u32[]{:S(2)}) collective-permute-start(bf16[384,512]{1,0:T(8,128)(2,1)} %get-tuple-element.45), channel_id=1, source_target_pairs={{0,128},{64,192},{128,0},{192,64},{1,129},{65,193},{129,1},{193,65... | collective-permute-start | bytes 1179656 | tf_op jit(solution)/shard_map/ppermute | solution.py:412
  127.2 1.2 collective-permute-start.11
  128.4 0.3 collective-permute-done.9.refs_1_
  128.7 0.0 collective-permute-start.12
  128.7 0.0 collective-permute-done.13.refs_7_
  128.7 2.7 %collective-permute-start.17 = (bf16[384,512]{1,0:T(8,128)(2,1)}, bf16[384,512]{1,0:T(8,128)(2,1)S(1)}, u32[]{:S(2)}, u32[]{:S(2)}) collective-permute-start(bf16[384,512]{1,0:T(8,128)(2,1)} %get-tuple-element.46), channel_id=1, source_target_pairs={{0,192},{64,0},{128,64},{192,128},{1,193},{65,1},{129,65},{193,129... | collective-permute-start | bytes 1179656 | tf_op jit(solution)/shard_map/ppermute | solution.py:412
  131.4 12.1 %collective-permute-done.11.refs_3_ = bf16[384,384]{1,0:T(8,128)(2,1)S(1)} collective-permute-done((bf16[384,384]{1,0:T(8,128)(2,1)S(1)}, bf16[384,384]{1,0:T(8,128)(2,1)S(1)}, u32[]{:S(2)}, u32[]{:S(2)}) %collective-permute-start.11) | collective-permute-done | bytes 294944 | tf_op jit(solution)/shard_map/ppermute | solution.py:412
  143.5 1.4 collective-permute-start
  144.9 7.2 %collective-permute-done.12.refs_5_ = bf16[384,384]{1,0:T(8,128)(2,1)S(1)} collective-permute-done((bf16[384,384]{1,0:T(8,128)(2,1)S(1)}, bf16[384,384]{1,0:T(8,128)(2,1)S(1)}, u32[]{:S(2)}, u32[]{:S(2)}) %collective-permute-start.12) | collective-permute-done | bytes 294944 | tf_op jit(solution)/shard_map/ppermute | solution.py:412
  152.0 1.1 collective-permute-start.3
  153.2 0.0 collective-permute-done.15.refs_9_
  153.2 0.3 collective-permute-start.4
  153.5 0.0 collective-permute-done.16.refs_10_
  153.5 2.4 %collective-permute-start.5 = (bf16[512,384]{1,0:T(8,128)(2,1)}, bf16[512,384]{1,0:T(8,128)(2,1)S(1)}, u32[]{:S(2)}, u32[]{:S(2)}) collective-permute-start(bf16[512,384]{1,0:T(8,128)(2,1)} %get-tuple-element.37), channel_id=1, source_target_pairs={{0,192},{64,0},{128,64},{192,128},{1,193},{65,1},{129,65},{193,129... | collective-permute-start | bytes 1179656 | tf_op jit(solution)/shard_map/ppermute | solution.py:412
  155.9 0.0 collective-permute-done.17.refs_11_
  155.9 0.0 collective-permute-start.10
  155.9 17.2 %collective-permute-done.4.refs_7_ = bf16[512,384]{1,0:T(8,128)(2,1)S(1)} collective-permute-done((bf16[512,384]{1,0:T(8,128)(2,1)}, bf16[512,384]{1,0:T(8,128)(2,1)S(1)}, u32[]{:S(2)}, u32[]{:S(2)}) %collective-permute-start.4) | collective-permute-done | bytes 393248 | tf_op jit(solution)/shard_map/ppermute | solution.py:412
  173.1 1.1 collective-permute-start.1
  174.3 0.0 collective-permute-done.5.refs_8_
  174.3 0.3 collective-permute-start.2
  174.6 4.8 %collective-permute-done.10.refs_2_ = bf16[384,384]{1,0:T(8,128)(2,1)S(1)} collective-permute-done((bf16[384,384]{1,0:T(8,128)(2,1)S(1)}, bf16[384,384]{1,0:T(8,128)(2,1)S(1)}, u32[]{:S(2)}, u32[]{:S(2)}) %collective-permute-start.10) | collective-permute-done | bytes 294944 | tf_op jit(solution)/shard_map/ppermute | solution.py:412
  179.4 1.1 collective-permute-start.14
  180.6 0.0 collective-permute-done.refs_1_
  180.6 0.3 collective-permute-start.6
  180.9 0.0 collective-permute-done.3.refs_5_
  180.9 2.4 %collective-permute-start.7 = (bf16[384,768]{1,0:T(8,128)(2,1)S(1)}, bf16[384,768]{1,0:T(8,128)(2,1)S(1)}, u32[]{:S(2)}, u32[]{:S(2)}) collective-permute-start(bf16[384,768]{1,0:T(8,128)(2,1)S(1)} %collective-permute-done.3.refs_5_), channel_id=1, source_target_pairs={{0,192},{64,0},{128,64},{192,128},{1,193},{65,1},{129,65},{193,129... | collective-permute-start | bytes 1769480 | tf_op jit(solution)/shard_map/ppermute | solution.py:412
  183.3 9.6 %collective-permute-done.14.refs_6_ = bf16[384,384]{1,0:T(8,128)(2,1)S(1)} collective-permute-done((bf16[384,384]{1,0:T(8,128)(2,1)S(1)}, bf16[384,384]{1,0:T(8,128)(2,1)S(1)}, u32[]{:S(2)}, u32[]{:S(2)}) %collective-permute-start.14) | collective-permute-done | bytes 294944 | tf_op jit(solution)/shard_map/ppermute | solution.py:412
  192.8 1.1 collective-permute-start.8
  193.9 1.0 copy-done
  194.9 4.1 %shard_map.147 = bf16[768,512]{1,0:T(8,128)(2,1)} custom-call(bf16[384,384]{1,0:T(8,128)(2,1)S(1)} %copy-done.2, bf16[384,384]{1,0:T(8,128)(2,1)S(1)} %collective-permute-done.9.refs_1_, bf16[384,384]{1,0:T(8,128)(2,1)S(1)} %collective-permute-done.10.refs_2_, bf16[384,384]{1,0:T(8,128)(2,1)S(1)} %collective-permute-done.11.refs_3_, ...), custom_call_target="tpu_custom_call" | custom-call | flops 1258291200 | bytes 8388608 | tf_op jit(solution)/shard_map/pallas_call | solution.py:394
  199.0 0.0 collective-permute-done.1.refs_2_
  199.1 0.0 collective-permute-done.2.refs_4_
  199.1 0.0 copy-done.7
  199.1 0.0 copy-done.9
  199.1 4.2 %shard_map.144.acc = bf16[2,512,768]{2,1,0:T(8,128)(2,1)S(1)} custom-call(bf16[384,768]{1,0:T(8,128)(2,1)S(1)} %copy-done.6, bf16[384,768]{1,0:T(8,128)(2,1)S(1)} %collective-permute-done.refs_1_, bf16[384,768]{1,0:T(8,128)(2,1)S(1)} %collective-permute-done.1.refs_2_, bf16[384,768]{1,0:T(8,128)(2,1)S(1)} %copy-done.7, ...), custom_call_target="tpu_custom_call" | custom-call | flops 1887436800 | bytes 8388608 | tf_op jit(solution)/shard_map/pallas_call | solution.py:394
  203.3 10.7 %collective-permute-done.8.x2 = bf16[512,384]{1,0:T(8,128)(2,1)S(1)} collective-permute-done((bf16[512,384]{1,0:T(8,128)(2,1)S(1)}, bf16[512,384]{1,0:T(8,128)(2,1)S(1)}, u32[]{:S(2)}, u32[]{:S(2)}) %collective-permute-start.8) | collective-permute-done | bytes 393248 | tf_op jit(solution)/shard_map/ppermute | solution.py:412
  214.0 0.0 collective-permute-done.6.gate_b
  214.0 0.0 collective-permute-done.7.up_b
  214.0 2.4 %shard_map.145 = (bf16[512,768]{1,0:T(8,128)(2,1)}, bf16[512,768]{1,0:T(8,128)(2,1)}) custom-call(bf16[2,512,768]{2,1,0:T(8,128)(2,1)S(1)} %shard_map.144.acc, bf16[384,768]{1,0:T(8,128)(2,1)S(1)} %collective-permute-done.6.gate_b, bf16[384,768]{1,0:T(8,128)(2,1)S(1)} %collective-permute-done.7.up_b, bf16[512,384]{1,0:T(8,128)(2,1)S(1)} %collective-permute-done.8.x2), custom_call_target="tpu_custom_call" | custom-call | flops 629145600 | bytes 8388608 | tf_op jit(solution)/shard_map/pallas_call | solution.py:394
  216.4 0.0 all-to-all-done.2
  216.4 1.9 shard_map.143
  (19 shorter events, 0.0 us)
Async XLA Ops:
  4.0 13.3 %copy-start.8 = (bf16[128,2048]{1,0:T(8,128)(2,1)S(1)}, bf16[128,2048]{1,0:T(8,128)(2,1)}, u32[]{:S(2)}) copy-start(bf16[128,2048]{1,0:T(8,128)(2,1)} %x_ref.2) | copy-start | bytes 1572868
  4.0 13.3 %copy-start.10 = (s32[128,2]{0,1:T(2,128)S(1)}, s32[128,2]{0,1:T(2,128)}, u32[]{:S(2)}) copy-start(s32[128,2]{0,1:T(2,128)} %param.13) | copy-start | bytes 3076
  4.0 13.3 %copy-start.11 = (bf16[128,2]{0,1:T(2,128)(2,1)S(1)}, bf16[128,2]{0,1:T(2,128)(2,1)}, u32[]{:S(2)}) copy-start(bf16[128,2]{0,1:T(2,128)(2,1)} %param.12) | copy-start | bytes 1540
  4.0 53.0 %all-to-all-start.1 = ((bf16[64,24,512]{2,1,0:T(8,128)(2,1)}), bf16[64,24,512]{2,1,0:T(8,128)(2,1)S(1)}, u32[]{:S(2)}, u32[]{:S(2)}) async-start(bf16[64,24,512]{2,1,0:T(8,128)(2,1)} %bitcast.31), calls=%async_computation.1 | async-start | bytes 3145728 | tf_op jit(solution)/shard_map/all_to_all | solution.py:408
  57.0 6.2 %copy-start.1 = (bf16[192,192]{1,0:T(8,128)(2,1)S(1)}, bf16[192,192]{1,0:T(8,128)(2,1)}, u32[]{:S(2)}) copy-start(bf16[192,192]{1,0:T(8,128)(2,1)} %constant.12.clone.perm_ref) | copy-start | bytes 221188
  57.0 46.0 %all-to-all-start = ((bf16[64,24,512]{2,1,0:T(8,128)(2,1)}), bf16[64,24,512]{2,1,0:T(8,128)(2,1)S(1)}, u32[]{:S(2)}, u32[]{:S(2)}) async-start(bf16[64,24,512]{2,1,0:T(8,128)(2,1)} %bitcast.30), calls=%async_computation | async-start | bytes 3145728 | tf_op jit(solution)/shard_map/all_to_all | solution.py:408
  103.0 5.8 %copy-start.4 = (bf16[1,2048,768]{2,1,0:T(8,128)(2,1)S(1)}, bf16[1,2048,768]{2,1,0:T(8,128)(2,1)}, u32[]{:S(2)}) copy-start(bf16[1,2048,768]{2,1,0:T(8,128)(2,1)} %param.14) | copy-start | bytes 9437188
  103.0 5.8 %copy-start.5 = (bf16[1,2048,768]{2,1,0:T(8,128)(2,1)S(1)}, bf16[1,2048,768]{2,1,0:T(8,128)(2,1)}, u32[]{:S(2)}) copy-start(bf16[1,2048,768]{2,1,0:T(8,128)(2,1)} %param.15) | copy-start | bytes 9437188
  103.0 5.8 %copy-start.12 = (bf16[192,192]{1,0:T(8,128)(2,1)S(1)}, bf16[192,192]{1,0:T(8,128)(2,1)}, u32[]{:S(2)}) copy-start(bf16[192,192]{1,0:T(8,128)(2,1)} %constant.13.clone.pack_ref) | copy-start | bytes 221188
  103.0 5.8 %copy-start.13 = (bf16[64,48]{1,0:T(8,128)(2,1)S(1)}, bf16[64,48]{1,0:T(8,128)(2,1)}, u32[]{:S(2)}) copy-start(bf16[64,48]{1,0:T(8,128)(2,1)} %constant.14.clone.probs_ref) | copy-start | bytes 18436
  112.9 103.5 %all-to-all-start.2 = ((bf16[64,8,1664]{2,1,0:T(8,128)(2,1)}), bf16[64,8,1664]{2,1,0:T(8,128)(2,1)S(1)}, u32[]{:S(2)}, u32[]{:S(2)}) async-start(bf16[64,8,1664]{2,1,0:T(8,128)(2,1)} %bitcast.29), calls=%async_computation.2 | async-start | bytes 3407872 | tf_op jit(solution)/shard_map/all_to_all | solution.py:408
  119.0 8.2 %copy-start.2 = (bf16[384,384]{1,0:T(8,128)(2,1)S(1)}, bf16[384,384]{1,0:T(8,128)(2,1)}, u32[]{:S(2)}) copy-start(bf16[384,384]{1,0:T(8,128)(2,1)} %get-tuple-element.41.refs_0_) | copy-start | bytes 884740
  119.1 9.6 %copy-start.3 = (bf16[384,384]{1,0:T(8,128)(2,1)S(1)}, bf16[384,384]{1,0:T(8,128)(2,1)}, u32[]{:S(2)}) copy-start(bf16[384,384]{1,0:T(8,128)(2,1)} %get-tuple-element.42.refs_4_) | copy-start | bytes 884740
  119.1 24.4 %copy-start.6 = (bf16[384,768]{1,0:T(8,128)(2,1)S(1)}, bf16[384,768]{1,0:T(8,128)(2,1)}, u32[]{:S(2)}) copy-start(bf16[384,768]{1,0:T(8,128)(2,1)} %get-tuple-element.33.refs_0_) | copy-start | bytes 1769476
  119.1 73.8 %copy-start.14 = (bf16[512,384]{1,0:T(8,128)(2,1)S(1)}, bf16[512,384]{1,0:T(8,128)(2,1)}, u32[]{:S(2)}) copy-start(bf16[512,384]{1,0:T(8,128)(2,1)} %get-tuple-element.38) | copy-start | bytes 1179652
  119.1 9.6 %collective-permute-start.9 = (bf16[384,384]{1,0:T(8,128)(2,1)}, bf16[384,384]{1,0:T(8,128)(2,1)S(1)}, u32[]{:S(2)}, u32[]{:S(2)}) collective-permute-start(bf16[384,384]{1,0:T(8,128)(2,1)} %get-tuple-element.41.refs_0_), channel_id=1, source_target_pairs={{0,64},{64,128},{128,192},{192,0},{1,65},{65,129},{129,193},{193,1... | collective-permute-start | bytes 884744 | tf_op jit(solution)/shard_map/ppermute | solution.py:412
  120.4 8.3 %collective-permute-start.13 = (bf16[384,384]{1,0:T(8,128)(2,1)}, bf16[384,384]{1,0:T(8,128)(2,1)S(1)}, u32[]{:S(2)}, u32[]{:S(2)}) collective-permute-start(bf16[384,384]{1,0:T(8,128)(2,1)} %get-tuple-element.42.refs_4_), channel_id=1, source_target_pairs={{0,192},{64,0},{128,64},{192,128},{1,193},{65,1},{129,65},{193,129... | collective-permute-start | bytes 884744 | tf_op jit(solution)/shard_map/ppermute | solution.py:412
  124.7 28.5 %collective-permute-start.15 = (bf16[384,512]{1,0:T(8,128)(2,1)}, bf16[384,512]{1,0:T(8,128)(2,1)S(1)}, u32[]{:S(2)}, u32[]{:S(2)}) collective-permute-start(bf16[384,512]{1,0:T(8,128)(2,1)} %get-tuple-element.44), channel_id=1, source_target_pairs={{0,64},{64,128},{128,192},{192,0},{1,65},{65,129},{129,193},{193,1... | collective-permute-start | bytes 1179656 | tf_op jit(solution)/shard_map/ppermute | solution.py:412
  124.8 28.7 %collective-permute-start.16 = (bf16[384,512]{1,0:T(8,128)(2,1)}, bf16[384,512]{1,0:T(8,128)(2,1)S(1)}, u32[]{:S(2)}, u32[]{:S(2)}) collective-permute-start(bf16[384,512]{1,0:T(8,128)(2,1)} %get-tuple-element.45), channel_id=1, source_target_pairs={{0,128},{64,192},{128,0},{192,64},{1,129},{65,193},{129,1},{193,65... | collective-permute-start | bytes 1179656 | tf_op jit(solution)/shard_map/ppermute | solution.py:412
  127.2 16.2 %collective-permute-start.11 = (bf16[384,384]{1,0:T(8,128)(2,1)S(1)}, bf16[384,384]{1,0:T(8,128)(2,1)S(1)}, u32[]{:S(2)}, u32[]{:S(2)}) collective-permute-start(bf16[384,384]{1,0:T(8,128)(2,1)S(1)} %copy-done.2), channel_id=1, source_target_pairs={{0,192},{64,0},{128,64},{192,128},{1,193},{65,1},{129,65},{193,129... | collective-permute-start | bytes 884744 | tf_op jit(solution)/shard_map/ppermute | solution.py:412
  128.7 23.3 %collective-permute-start.12 = (bf16[384,384]{1,0:T(8,128)(2,1)S(1)}, bf16[384,384]{1,0:T(8,128)(2,1)S(1)}, u32[]{:S(2)}, u32[]{:S(2)}) collective-permute-start(bf16[384,384]{1,0:T(8,128)(2,1)S(1)} %copy-done.3), channel_id=1, source_target_pairs={{0,64},{64,128},{128,192},{192,0},{1,65},{65,129},{129,193},{193,1... | collective-permute-start | bytes 884744 | tf_op jit(solution)/shard_map/ppermute | solution.py:412
  128.7 27.2 %collective-permute-start.17 = (bf16[384,512]{1,0:T(8,128)(2,1)}, bf16[384,512]{1,0:T(8,128)(2,1)S(1)}, u32[]{:S(2)}, u32[]{:S(2)}) collective-permute-start(bf16[384,512]{1,0:T(8,128)(2,1)} %get-tuple-element.46), channel_id=1, source_target_pairs={{0,192},{64,0},{128,64},{192,128},{1,193},{65,1},{129,65},{193,129... | collective-permute-start | bytes 1179656 | tf_op jit(solution)/shard_map/ppermute | solution.py:412
  143.5 37.1 %collective-permute-start = (bf16[384,768]{1,0:T(8,128)(2,1)S(1)}, bf16[384,768]{1,0:T(8,128)(2,1)S(1)}, u32[]{:S(2)}, u32[]{:S(2)}) collective-permute-start(bf16[384,768]{1,0:T(8,128)(2,1)S(1)} %copy-done.6), channel_id=1, source_target_pairs={{0,64},{64,128},{128,192},{192,0},{1,65},{65,129},{129,193},{193,1... | collective-permute-start | bytes 1769480 | tf_op jit(solution)/shard_map/ppermute | solution.py:412
  152.0 28.9 %collective-permute-start.3 = (bf16[384,768]{1,0:T(8,128)(2,1)}, bf16[384,768]{1,0:T(8,128)(2,1)S(1)}, u32[]{:S(2)}, u32[]{:S(2)}) collective-permute-start(bf16[384,768]{1,0:T(8,128)(2,1)} %get-tuple-element.34.refs_3_), channel_id=1, source_target_pairs={{0,192},{64,0},{128,64},{192,128},{1,193},{65,1},{129,65},{193,129... | collective-permute-start | bytes 1769480 | tf_op jit(solution)/shard_map/ppermute | solution.py:412
  153.2 19.9 %collective-permute-start.4 = (bf16[512,384]{1,0:T(8,128)(2,1)}, bf16[512,384]{1,0:T(8,128)(2,1)S(1)}, u32[]{:S(2)}, u32[]{:S(2)}) collective-permute-start(bf16[512,384]{1,0:T(8,128)(2,1)} %get-tuple-element.36), channel_id=1, source_target_pairs={{0,64},{64,128},{128,192},{192,0},{1,65},{65,129},{129,193},{193,1... | collective-permute-start | bytes 1179656 | tf_op jit(solution)/shard_map/ppermute | solution.py:412
  153.5 20.7 %collective-permute-start.5 = (bf16[512,384]{1,0:T(8,128)(2,1)}, bf16[512,384]{1,0:T(8,128)(2,1)S(1)}, u32[]{:S(2)}, u32[]{:S(2)}) collective-permute-start(bf16[512,384]{1,0:T(8,128)(2,1)} %get-tuple-element.37), channel_id=1, source_target_pairs={{0,192},{64,0},{128,64},{192,128},{1,193},{65,1},{129,65},{193,129... | collective-permute-start | bytes 1179656 | tf_op jit(solution)/shard_map/ppermute | solution.py:412
  155.9 23.5 %collective-permute-start.10 = (bf16[384,384]{1,0:T(8,128)(2,1)S(1)}, bf16[384,384]{1,0:T(8,128)(2,1)S(1)}, u32[]{:S(2)}, u32[]{:S(2)}) collective-permute-start(bf16[384,384]{1,0:T(8,128)(2,1)S(1)} %collective-permute-done.9.refs_1_), channel_id=1, source_target_pairs={{0,64},{64,128},{128,192},{192,0},{1,65},{65,129},{129,193},{193,1... | collective-permute-start | bytes 884744 | tf_op jit(solution)/shard_map/ppermute | solution.py:412
  173.1 25.9 %collective-permute-start.1 = (bf16[384,768]{1,0:T(8,128)(2,1)S(1)}, bf16[384,768]{1,0:T(8,128)(2,1)S(1)}, u32[]{:S(2)}, u32[]{:S(2)}) collective-permute-start(bf16[384,768]{1,0:T(8,128)(2,1)S(1)} %copy-done.6), channel_id=1, source_target_pairs={{0,192},{64,0},{128,64},{192,128},{1,193},{65,1},{129,65},{193,129... | collective-permute-start | bytes 1769480 | tf_op jit(solution)/shard_map/ppermute | solution.py:412
  174.3 24.8 %collective-permute-start.2 = (bf16[384,768]{1,0:T(8,128)(2,1)}, bf16[384,768]{1,0:T(8,128)(2,1)S(1)}, u32[]{:S(2)}, u32[]{:S(2)}) collective-permute-start(bf16[384,768]{1,0:T(8,128)(2,1)} %get-tuple-element.34.refs_3_), channel_id=1, source_target_pairs={{0,64},{64,128},{128,192},{192,0},{1,65},{65,129},{129,193},{193,1... | collective-permute-start | bytes 1769480 | tf_op jit(solution)/shard_map/ppermute | solution.py:412
  179.4 13.4 %collective-permute-start.14 = (bf16[384,384]{1,0:T(8,128)(2,1)S(1)}, bf16[384,384]{1,0:T(8,128)(2,1)S(1)}, u32[]{:S(2)}, u32[]{:S(2)}) collective-permute-start(bf16[384,384]{1,0:T(8,128)(2,1)S(1)} %collective-permute-done.13.refs_7_), channel_id=1, source_target_pairs={{0,192},{64,0},{128,64},{192,128},{1,193},{65,1},{129,65},{193,129... | collective-permute-start | bytes 884744 | tf_op jit(solution)/shard_map/ppermute | solution.py:412
  180.6 33.4 %collective-permute-start.6 = (bf16[384,768]{1,0:T(8,128)(2,1)S(1)}, bf16[384,768]{1,0:T(8,128)(2,1)S(1)}, u32[]{:S(2)}, u32[]{:S(2)}) collective-permute-start(bf16[384,768]{1,0:T(8,128)(2,1)S(1)} %collective-permute-done.refs_1_), channel_id=1, source_target_pairs={{0,64},{64,128},{128,192},{192,0},{1,65},{65,129},{129,193},{193,1... | collective-permute-start | bytes 1769480 | tf_op jit(solution)/shard_map/ppermute | solution.py:412
  180.9 33.1 %collective-permute-start.7 = (bf16[384,768]{1,0:T(8,128)(2,1)S(1)}, bf16[384,768]{1,0:T(8,128)(2,1)S(1)}, u32[]{:S(2)}, u32[]{:S(2)}) collective-permute-start(bf16[384,768]{1,0:T(8,128)(2,1)S(1)} %collective-permute-done.3.refs_5_), channel_id=1, source_target_pairs={{0,192},{64,0},{128,64},{192,128},{1,193},{65,1},{129,65},{193,129... | collective-permute-start | bytes 1769480 | tf_op jit(solution)/shard_map/ppermute | solution.py:412
  192.8 21.2 %collective-permute-start.8 = (bf16[512,384]{1,0:T(8,128)(2,1)S(1)}, bf16[512,384]{1,0:T(8,128)(2,1)S(1)}, u32[]{:S(2)}, u32[]{:S(2)}) collective-permute-start(bf16[512,384]{1,0:T(8,128)(2,1)S(1)} %copy-done.14), channel_id=1, source_target_pairs={{0,128},{64,192},{128,0},{192,64},{1,129},{65,193},{129,1},{193,65... | collective-permute-start | bytes 1179656 | tf_op jit(solution)/shard_map/ppermute | solution.py:412
  193.9 1.0 copy-start
  194.9 4.2 %copy-start.7 = (bf16[384,768]{1,0:T(8,128)(2,1)S(1)}, bf16[384,768]{1,0:T(8,128)(2,1)}, u32[]{:S(2)}) copy-start(bf16[384,768]{1,0:T(8,128)(2,1)} %get-tuple-element.34.refs_3_) | copy-start | bytes 1769476
  194.9 4.2 %copy-start.9 = (bf16[512,384]{1,0:T(8,128)(2,1)S(1)}, bf16[512,384]{1,0:T(8,128)(2,1)}, u32[]{:S(2)}) copy-start(bf16[512,384]{1,0:T(8,128)(2,1)} %get-tuple-element.35.refs_6_) | copy-start | bytes 1179652
